TPU v7x, 512 devices: a whole 4x4x16 slice. The times are simulated.
512 devices in a mesh: shard: 128 (over y, z, core), tensor: 4 (over x).
Axes of the slice: x: 4, y: 4, z: 16, core: 2. Of those that a mesh axis runs over, the one named last changes fastest.
Arguments:
- expert_grads: bfloat16 [2, 128, 2, 512, 1024], P(None, 'shard', None, None, 'tensor')
- embed_grads: bfloat16 [2, 128, 4096, 512], P(None, 'shard', None, 'tensor')
- small_grads: bfloat16 [2, 128, 512, 36], P(None, 'shard', None, 'tensor')
- expert_master: float32 [2, 512, 1024], P(None, 'shard', 'tensor'), may hold values from -0.2 to 0.2
- expert_first: float32 [2, 512, 1024], P(None, 'shard', 'tensor'), may hold values from -6 to 6
- expert_second: float32 [2, 512, 1024], P(None, 'shard', 'tensor'), may hold values from 0.02 to 0.2
- embed_master: float32 [4096, 512], P('shard', 'tensor'), may hold values from -0.2 to 0.2
- embed_first: float32 [4096, 512], P('shard', 'tensor'), may hold values from -6 to 6
- embed_second: float32 [4096, 512], P('shard', 'tensor'), may hold values from 0.02 to 0.2
- small_master: float32 [512, 36], P('shard', 'tensor'), may hold values from -0.2 to 0.2
- small_first: float32 [512, 36], P('shard', 'tensor'), may hold values from -6 to 6
- small_second: float32 [512, 36], P('shard', 'tensor'), may hold values from 0.02 to 0.2
- class_steps: int32 [4096], P('shard'), may hold values from 1 to 2000
- clip_rms: float32 [], replicated, may hold values from 1 to 1.5
Outputs:
- expert_weights: bfloat16 [2, 512, 1024], P(None, None, 'tensor')
- embed_weights: bfloat16 [4096, 512], P(None, 'tensor')
- small_weights: bfloat16 [512, 36], P(None, 'tensor')
- expert_master_new: float32 [2, 512, 1024], P(None, 'shard', 'tensor')
- expert_first_new: float32 [2, 512, 1024], P(None, 'shard', 'tensor')
- expert_second_new: float32 [2, 512, 1024], P(None, 'shard', 'tensor')
- embed_master_new: float32 [4096, 512], P('shard', 'tensor')
- embed_first_new: float32 [4096, 512], P('shard', 'tensor')
- embed_second_new: float32 [4096, 512], P('shard', 'tensor')
- embed_step: float32 [4096, 512], P('shard', 'tensor')
- small_master_new: float32 [512, 36], P('shard', 'tensor')
- small_first_new: float32 [512, 36], P('shard', 'tensor')
- small_second_new: float32 [512, 36], P('shard', 'tensor')
- clip_scale: float32 [], replicated
All inputs are finite; a program needn't handle non-finite values.
Results may differ from a plain program's by a relative error of at most 0.001.
Values may be sent and summed in bfloat16 or wider, within the bound.
No kernel may reach another device: no remote copies, remote signals or barrier semaphores. Data moves between devices by JAX's collectives and lax.ppermute only.
A program may use at most 64 MiB of HBM per device.

v0:
```python
import jax
import jax.numpy as jnp
from jax import lax
from jax.sharding import PartitionSpec as P

STEP = 1000
P_TOT = 3164160


BETA_ONE = 0.9
BETA_TWO = 0.999
LEARN_RATE = 0.001
DECAY_RATE = 0.1
EPSILON = 1e-08


def local_total(gradients):
    summed = gradients[0, 0].astype(jnp.float32)
    summed = summed + gradients[1, 0].astype(jnp.float32)
    return summed


def finish(first_new, second_new, master, corr_one, corr_two):
    update_step = (
        first_new / corr_one / (jnp.sqrt(second_new / corr_two) + EPSILON) + DECAY_RATE * master
    )
    master_new = master - LEARN_RATE * update_step
    return (master_new, update_step)


def body(
    expert_grads,
    embed_grads,
    small_grads,
    expert_master,
    expert_first,
    expert_second,
    embed_master,
    embed_first,
    embed_second,
    small_master,
    small_first,
    small_second,
    class_steps,
    clip_rms,
):
    expert_local = local_total(expert_grads)
    embed_local = local_total(embed_grads)
    small_local = local_total(small_grads)
    expert_sum = lax.psum_scatter(expert_local, "shard", scatter_dimension=1, tiled=True)
    embed_sum = lax.psum_scatter(embed_local, "shard", scatter_dimension=0, tiled=True)
    small_sum = lax.psum_scatter(small_local, "shard", scatter_dimension=0, tiled=True)
    summed_all = (expert_sum, embed_sum, small_sum)
    squares = (
        jnp.sum(expert_sum * expert_sum)
        + jnp.sum(embed_sum * embed_sum)
        + jnp.sum(small_sum * small_sum)
    )
    total_squares = lax.psum(squares, ("shard", "tensor"))
    clip_factor = clip_rms * jnp.sqrt(P_TOT / total_squares)

    def moments(group_index, first_moment, second_moment):
        scaled = clip_factor * summed_all[group_index]
        return (
            BETA_ONE * first_moment + (1.0 - BETA_ONE) * scaled,
            BETA_TWO * second_moment + (1.0 - BETA_TWO) * scaled * scaled,
        )

    fixed_one = 1.0 - BETA_ONE**STEP
    fixed_two = 1.0 - BETA_TWO**STEP
    row_float = class_steps.astype(jnp.float32)[:, None]
    row_one = 1.0 - BETA_ONE**row_float
    row_two = 1.0 - BETA_TWO**row_float
    expert_first_new, expert_second_new = moments(0, expert_first, expert_second)
    embed_first_new, embed_second_new = moments(1, embed_first, embed_second)
    small_first_new, small_second_new = moments(2, small_first, small_second)
    expert_master_new, expert_update = finish(
        expert_first_new, expert_second_new, expert_master, fixed_one, fixed_two
    )
    embed_master_new, embed_update = finish(
        embed_first_new, embed_second_new, embed_master, row_one, row_two
    )
    small_master_new, small_update = finish(
        small_first_new, small_second_new, small_master, fixed_one, fixed_two
    )
    expert_cast = expert_master_new.astype(jnp.bfloat16)
    embed_cast = embed_master_new.astype(jnp.bfloat16)
    small_cast = small_master_new.astype(jnp.bfloat16)
    expert_weights = lax.all_gather(expert_cast, "shard", axis=1, tiled=True)
    embed_weights = lax.all_gather(embed_cast, "shard", axis=0, tiled=True)
    small_weights = lax.all_gather(small_cast, "shard", axis=0, tiled=True)
    return (
        expert_weights,
        embed_weights,
        small_weights,
        expert_master_new,
        expert_first_new,
        expert_second_new,
        embed_master_new,
        embed_first_new,
        embed_second_new,
        embed_update,
        small_master_new,
        small_first_new,
        small_second_new,
        clip_factor,
    )


def solution(mesh):
    in_specs = (
        P(None, "shard", None, None, "tensor"),
        P(None, "shard", None, "tensor"),
        P(None, "shard", None, "tensor"),
        P(None, "shard", "tensor"),
        P(None, "shard", "tensor"),
        P(None, "shard", "tensor"),
        P("shard", "tensor"),
        P("shard", "tensor"),
        P("shard", "tensor"),
        P("shard", "tensor"),
        P("shard", "tensor"),
        P("shard", "tensor"),
        P("shard"),
        P(),
    )
    out_specs = (
        P(None, None, "tensor"),
        P(None, "tensor"),
        P(None, "tensor"),
        P(None, "shard", "tensor"),
        P(None, "shard", "tensor"),
        P(None, "shard", "tensor"),
        P("shard", "tensor"),
        P("shard", "tensor"),
        P("shard", "tensor"),
        P("shard", "tensor"),
        P("shard", "tensor"),
        P("shard", "tensor"),
        P("shard", "tensor"),
        P(),
    )
    return jax.shard_map(body, mesh=mesh, in_specs=in_specs, out_specs=out_specs, check_vma=False)
```

profile of v0, /device:TPU:1, one launch (start us, length us, event | category | flops | bytes accessed | tf_op | source)
XLA Modules:
  0.0 900.7 jit_solution(16309437702115690155)
XLA Ops:
  7.2 0.0 all-reduce.4.cloned.1.call-start
  7.2 2.4 add_bitcast_fusion.1
  9.7 0.0 all-reduce.4.cloned.1.call-update
  9.7 0.0 reduce-scatter.3.cloned.1.call-start
  9.7 1.5 add_bitcast_fusion
  11.3 0.0 copy-start.4
  11.3 0.0 copy-start.5
  11.3 0.0 copy-start.6
  11.3 0.0 copy-start.7
  11.3 0.0 copy-start.8
  11.4 0.0 copy-start.9
  11.4 0.0 reduce-scatter.3.cloned.1.call-update
  11.4 0.0 all-gather.3.cloned.1.call-start
  11.5 0.5 copy-done.1
  12.1 0.1 copy.38
  12.2 1.3 dynamic-slice
  14.1 498.3 %all-reduce.1 = f32[512,9]{1,0:T(8,128)S(1)} all-reduce(f32[512,9]{1,0:T(8,128)S(1)} %copy.38), channel_id=4, replica_groups=mesh['shard'=128,'tensor'=4] {'shard'}, use_global_device_ids=true, to_apply=%region_4.0.clone | all-reduce | flops 4608 | bytes 36864
  512.4 0.6 multiply_reduce_fusion.2
  513.0 0.0 all-reduce.4.cloned.1.call-done
  513.1 1.3 multiply_reduce_fusion.1
  514.4 91.1 %reduce-scatter.3.cloned.1.call-done = f32[32,128]{1,0:T(8,128)} async-done(((f32[4096,128]{1,0:T(8,128)}), f32[32,128]{1,0:T(8,128)}) %reduce-scatter.3.cloned.1.call-update) | async-done | bytes 16400 | tf_op jit(solution)/shard_map/reduce_scatter | solution.py:51
  605.5 1.3 multiply_reduce_fusion
  609.4 112.9 %psum.7 = f32[]{:T(128)} all-reduce(f32[]{:T(128)S(6)} %add.84), channel_id=1, replica_groups=mesh['shard'=128,'tensor'=4] {'shard','tensor'}, use_global_device_ids=true, to_apply=%region_6.0 | all-reduce | flops 1 | bytes 8 | tf_op jit(solution)/shard_map/psum | solution.py:59
  723.0 1.4 fusion.4
  724.5 0.0 all-gather.3.cloned.1.call-update
  724.5 1.4 fusion.6
  725.9 81.5 %all_gather.9 = bf16[2,512,256]{2,0,1:T(2,128)(2,1)S(1)} all-gather(bf16[2,4,256]{2,0,1:T(2,128)(2,1)S(1)} %copy.39), channel_id=1, replica_groups=mesh['shard'=128,'tensor'=4] {'shard'}, dimensions={1}, use_global_device_ids=true | all-gather | bytes 528384 | tf_op jit(solution)/shard_map/all_gather | solution.py:89
  807.4 0.9 copy.40
  808.2 0.6 convert_bitcast_fusion
  808.8 81.2 %all-gather = bf16[128,4,9]{2,1,0:T(4,128)(2,1)S(1)} all-gather(bf16[1,4,9]{2,1,0:T(4,128)(2,1)S(1)} %get-tuple-element.56), channel_id=1, replica_groups=mesh['shard'=128,'tensor'=4] {'shard'}, dimensions={0}, use_global_device_ids=true | all-gather | bytes 9288 | tf_op jit(solution)/shard_map/all_gather | solution.py:91
  890.1 0.7 copy.41
  890.8 2.3 copy.51
  (22 shorter events, 0.1 us)
Async XLA Ops:
  7.2 2.6 copy-start
  7.2 505.9 %all-reduce.4.cloned.1.call-start = ((), (), s32[]{:S(2)}) async-start(), calls=%async_computation.3 | async-start | bytes 2097152
  9.7 595.8 %reduce-scatter.3.cloned.1.call-start = ((), (), s32[]{:S(2)}) async-start(), calls=%async_computation.1 | async-start | bytes 2113536 | tf_op jit(solution)/shard_map/reduce_scatter | solution.py:51
  11.3 0.7 copy-start.1
  11.3 501.7 %copy-start.11 = (s32[32]{0:T(128)S(1)}, s32[32]{0:T(128)}, u32[]{:S(2)}) copy-start(s32[32]{0:T(128)} %param.26) | copy-start | bytes 388
  11.3 711.7 %copy-start.2 = (f32[32,128]{1,0:T(8,128)S(1)}, f32[32,128]{1,0:T(8,128)}, u32[]{:S(2)}) copy-start(f32[32,128]{1,0:T(8,128)} %param.20) | copy-start | bytes 49156
  11.3 711.7 %copy-start.3 = (f32[32,128]{1,0:T(8,128)S(1)}, f32[32,128]{1,0:T(8,128)}, u32[]{:S(2)}) copy-start(f32[32,128]{1,0:T(8,128)} %param.22) | copy-start | bytes 49156
  11.3 711.7 %copy-start.4 = (f32[32,128]{1,0:T(8,128)S(1)}, f32[32,128]{1,0:T(8,128)}, u32[]{:S(2)}) copy-start(f32[32,128]{1,0:T(8,128)} %param.21) | copy-start | bytes 49156
  11.3 713.2 %copy-start.5 = (f32[2,4,256]{2,1,0:T(4,128)S(1)}, f32[2,4,256]{2,1,0:T(4,128)}, u32[]{:S(2)}) copy-start(f32[2,4,256]{2,1,0:T(4,128)} %param.17) | copy-start | bytes 24580
  11.3 713.2 %copy-start.6 = (f32[2,4,256]{2,1,0:T(4,128)S(1)}, f32[2,4,256]{2,1,0:T(4,128)}, u32[]{:S(2)}) copy-start(f32[2,4,256]{2,1,0:T(4,128)} %param.19) | copy-start | bytes 24580
  11.3 713.2 %copy-start.7 = (f32[2,4,256]{2,1,0:T(4,128)S(1)}, f32[2,4,256]{2,1,0:T(4,128)}, u32[]{:S(2)}) copy-start(f32[2,4,256]{2,1,0:T(4,128)} %param.18) | copy-start | bytes 24580
  11.3 796.9 %copy-start.8 = (f32[4,9]{1,0:T(4,128)S(1)}, f32[4,9]{1,0:T(4,128)}, u32[]{:S(2)}) copy-start(f32[4,9]{1,0:T(4,128)} %param.23) | copy-start | bytes 436
  11.4 796.9 %copy-start.9 = (f32[4,9]{1,0:T(4,128)S(1)}, f32[4,9]{1,0:T(4,128)}, u32[]{:S(2)}) copy-start(f32[4,9]{1,0:T(4,128)} %param.25) | copy-start | bytes 436
  11.4 796.9 %copy-start.10 = (f32[4,9]{1,0:T(4,128)S(1)}, f32[4,9]{1,0:T(4,128)}, u32[]{:S(2)}) copy-start(f32[4,9]{1,0:T(4,128)} %param.24) | copy-start | bytes 436
  11.4 879.4 %all-gather.3.cloned.1.call-start = ((), (), s32[]{:S(2)}) async-start(), calls=%async_computation.2 | async-start | bytes 1056768 | tf_op jit(solution)/shard_map/all_gather | solution.py:90
Sparse Core Ops, SparseCore 0:
  12.1 340.1 all-reduce.3
  357.5 247.9 reduce-scatter.2
  724.6 125.6 all-gather.2
where the time goes:
time: 901 us
  blocking collectives  774 us (86%)
  waiting for transfers between devices  91.2 us (10%)
  between operations  19 us (2%)
  other arithmetic  10.6 us (1%)
    unnamed x1, blocking collectives  498 us
    psum x1, blocking collectives, body(): total_squares = lax.psum(squares, ('shard', 'tensor'))  113 us
    reduce_scatter x1, waiting for transfers between devices, body(): lax.psum_scatter(embed_local, 'shard', scatter_dimension=0, tiled=True)  91.1 us
    all_gather x1, blocking collectives, body(): expert_weights = lax.all_gather(expert_cast, 'shard', axis=1, tiled=True)  81.5 us
    all_gather x1, blocking collectives, body(): small_weights = lax.all_gather(small_cast, 'shard', axis=0, tiled=True)  81.2 us
  transfers between devices with their start and end apart: 3, of which 1 were waited for; matrix products, arithmetic and copies ran while one was open for 1% of the time, Pallas kernels for 0%

commit v1 on v0

v1 whole, which is shorter than its diff:
```python
import jax
import jax.numpy as jnp
from jax import lax
from jax.sharding import Mesh, PartitionSpec as P

STEP = 1000
P_TOT = 3164160

BETA_ONE = 0.9
BETA_TWO = 0.999
LEARN_RATE = 0.001
DECAY_RATE = 0.1
EPSILON = 1e-08

Y, Z, C, T = 4, 16, 2, 4


def local_total(gradients):
    return gradients[0, 0].astype(jnp.float32) + gradients[1, 0].astype(jnp.float32)


def finish(first_new, second_new, master, corr_one, corr_two):
    update_step = (
        first_new / corr_one / (jnp.sqrt(second_new / corr_two) + EPSILON) + DECAY_RATE * master
    )
    master_new = master - LEARN_RATE * update_step
    return (master_new, update_step)


def pack_expert(x):
    return x.reshape(2, 4, 2, 128).transpose(0, 2, 1, 3).reshape(16, 128)


def unpack_expert(x):
    return x.reshape(2, 2, 4, 128).transpose(0, 2, 1, 3).reshape(2, 4, 256)


def exchange(x, axes):
    return lax.all_to_all(x, axes, 0, 0, tiled=True)


def spread(x, n, axes):
    return exchange(jnp.broadcast_to(x[None], (n,) + x.shape), axes)


def body(
    expert_grads,
    embed_grads,
    small_grads,
    expert_master,
    expert_first,
    expert_second,
    embed_master,
    embed_first,
    embed_second,
    small_master,
    small_first,
    small_second,
    class_steps,
    clip_rms,
):
    e = local_total(expert_grads).reshape(2, Y, Z, C, 4, 2, 128)
    e = e.transpose(3, 1, 2, 0, 5, 4, 6).reshape(C, Y, Z, 16, 128)
    m = local_total(embed_grads).reshape(Y, Z, C, 32, 128).transpose(2, 0, 1, 3, 4)
    s = local_total(small_grads).reshape(Y, Z, C, 4, 9).transpose(2, 0, 1, 3, 4)
    s = jnp.pad(s, ((0, 0),) * 3 + ((0, 4), (0, 119)))
    buf = jnp.concatenate([m, e, s], axis=3)
    got = exchange(buf, ("c",))
    part = got[0] + got[1]
    big = part[:, :, :48].astype(jnp.bfloat16)
    small_part = part[:, :, 48:52]
    high = lax.reduce_precision(small_part, 8, 7)
    low = (small_part - high).astype(jnp.bfloat16)
    got = exchange(jnp.concatenate([big, high.astype(jnp.bfloat16), low], axis=2), ("y",))
    got = got.astype(jnp.float32)
    part = got[0] + got[1] + got[2] + got[3]
    part = jnp.concatenate([part[:, :48], part[:, 48:52] + part[:, 52:56], jnp.zeros((Z, 4, 128), jnp.float32)], axis=1)
    got = exchange(part, ("z",))
    total = jnp.sum(got, axis=0)
    squares = jnp.sum(total * total)
    line = jnp.broadcast_to(squares, (Y * C * T, 128))
    line = exchange(line, ("y", "c", "t"))
    line = jnp.broadcast_to(jnp.sum(line, axis=0)[None], (Z, 128))
    total_squares = jnp.sum(exchange(line, ("z",))[:, 0])
    clip_factor = clip_rms * jnp.sqrt(P_TOT / total_squares)

    embed_sum = total[:32]
    expert_sum = unpack_expert(total[32:48])
    small_sum = total[48:52, :9]
    summed_all = (expert_sum, embed_sum, small_sum)

    def moments(group_index, first_moment, second_moment):
        scaled = clip_factor * summed_all[group_index]
        return (
            BETA_ONE * first_moment + (1.0 - BETA_ONE) * scaled,
            BETA_TWO * second_moment + (1.0 - BETA_TWO) * scaled * scaled,
        )

    fixed_one = 1.0 - BETA_ONE**STEP
    fixed_two = 1.0 - BETA_TWO**STEP
    row_float = class_steps.astype(jnp.float32)[:, None]
    row_one = 1.0 - BETA_ONE**row_float
    row_two = 1.0 - BETA_TWO**row_float
    expert_first_new, expert_second_new = moments(0, expert_first, expert_second)
    embed_first_new, embed_second_new = moments(1, embed_first, embed_second)
    small_first_new, small_second_new = moments(2, small_first, small_second)
    expert_master_new, expert_update = finish(
        expert_first_new, expert_second_new, expert_master, fixed_one, fixed_two
    )
    embed_master_new, embed_update = finish(
        embed_first_new, embed_second_new, embed_master, row_one, row_two
    )
    small_master_new, small_update = finish(
        small_first_new, small_second_new, small_master, fixed_one, fixed_two
    )
    own = jnp.concatenate(
        [
            embed_master_new.astype(jnp.bfloat16),
            pack_expert(expert_master_new.astype(jnp.bfloat16)),
            jnp.pad(small_master_new.astype(jnp.bfloat16), ((0, 4), (0, 119))),
        ],
        axis=0,
    )
    full = spread(own, Z, ("z",))
    full = spread(full, Y, ("y",))
    full = spread(full, C, ("c",))
    full = full.transpose(1, 2, 0, 3, 4)
    embed_weights = full[:, :, :, :32].reshape(4096, 128)
    expert_weights = full[:, :, :, 32:48].reshape(Y, Z, C, 2, 2, 4, 128)
    expert_weights = expert_weights.transpose(3, 0, 1, 2, 5, 4, 6).reshape(2, 512, 256)
    small_weights = full[:, :, :, 48:52, :9].reshape(512, 9)
    return (
        expert_weights,
        embed_weights,
        small_weights,
        expert_master_new,
        expert_first_new,
        expert_second_new,
        embed_master_new,
        embed_first_new,
        embed_second_new,
        embed_update,
        small_master_new,
        small_first_new,
        small_second_new,
        clip_factor,
    )


def solution(mesh):
    fine = Mesh(mesh.devices.reshape(Y, Z, C, T), ("y", "z", "c", "t"))
    sh = ("y", "z", "c")
    in_specs = (
        P(None, sh, None, None, "t"),
        P(None, sh, None, "t"),
        P(None, sh, None, "t"),
        P(None, sh, "t"),
        P(None, sh, "t"),
        P(None, sh, "t"),
        P(sh, "t"),
        P(sh, "t"),
        P(sh, "t"),
        P(sh, "t"),
        P(sh, "t"),
        P(sh, "t"),
        P(sh),
        P(),
    )
    out_specs = (
        P(None, None, "t"),
        P(None, "t"),
        P(None, "t"),
        P(None, sh, "t"),
        P(None, sh, "t"),
        P(None, sh, "t"),
        P(sh, "t"),
        P(sh, "t"),
        P(sh, "t"),
        P(sh, "t"),
        P(sh, "t"),
        P(sh, "t"),
        P(sh, "t"),
        P(),
    )
    return jax.shard_map(body, mesh=fine, in_specs=in_specs, out_specs=out_specs, check_vma=False)
```

time: 901 us -> 154 us (0.17)
  blocking collectives: 774 us -> 99.9 us
  waiting for transfers between devices: 91.2 us -> 23.9 us
  between operations: 19 us -> 3.51 us
  starting transfers between devices: 0.12 us -> 10.2 us
    unnamed x1 -> x0, blocking collectives: 498 us -> none
    all_gather x2 -> x0, blocking collectives: 163 us -> none  [the longest x1 81.5 us: body(): expert_weights = lax.all_gather(expert_cast, 'shard', axis=1, tiled=True)]
    psum x1 -> x0, blocking collectives: 113 us -> none  [body(): total_squares = lax.psum(squares, ('shard', 'tensor'))]
    all_to_all x0 -> x6, blocking collectives: none -> 99.9 us  [exchange(): return lax.all_to_all(x, axes, 0, 0, tiled=True)]
    reduce_scatter x1 -> x0, waiting for transfers between devices: 91.1 us -> none  [body(): lax.psum_scatter(embed_local, 'shard', scatter_dimension=0, tiled=True)]
    all_to_all x0 -> x2, waiting for transfers between devices: none -> 23.9 us  [exchange(): return lax.all_to_all(x, axes, 0, 0, tiled=True)]
    all_to_all x0 -> x2, starting transfers between devices: none -> 10.2 us  [exchange(): return lax.all_to_all(x, axes, 0, 0, tiled=True)]
  transfers between devices with their start and end apart: 3 -> 2, of which waited for: 1 -> 2; matrix products, arithmetic and copies ran while one was open for 1% -> 0% of each run, Pallas kernels for 0% -> 0%
where the time goes in v1:
time: 154 us
  blocking collectives  99.9 us (65%)
  waiting for transfers between devices  23.9 us (16%)
  starting transfers between devices  10.2 us (7%)
  local copies, waits for them, and re-layouts  9.22 us (6%)
  other arithmetic  6.73 us (4%)
  between operations  3.51 us (2%)
    all_to_all x6, blocking collectives, exchange(): return lax.all_to_all(x, axes, 0, 0, tiled=True)  99.9 us
    all_to_all x2, waiting for transfers between devices, exchange(): return lax.all_to_all(x, axes, 0, 0, tiled=True)  23.9 us
    all_to_all x2, starting transfers between devices, exchange(): return lax.all_to_all(x, axes, 0, 0, tiled=True)  10.2 us
  transfers between devices with their start and end apart: 2, of which 2 were waited for; matrix products, arithmetic and copies ran while one was open for 0% of the time, Pallas kernels for 0%

profile of v1, /device:TPU:1, one launch (start us, length us, event | category | flops | bytes accessed | tf_op | source)
XLA Modules:
  0.0 153.5 jit_solution(10557802093728414882)
XLA Ops:
  0.6 1.3 convert_add_fusion.1
  2.0 0.5 add.96
  2.5 0.3 copy.82
  2.8 1.3 copy-done
  4.1 0.2 convert_add_fusion
  4.3 0.5 copy-done.1
  5.0 0.3 select_maximum_fusion
  5.4 0.3 copy.84
  5.6 13.2 %all_to_all.45 = f32[2,4,16,56,128]{4,3,2,1,0:T(8,128)S(1)} all-to-all(f32[2,4,16,56,128]{4,3,2,1,0:T(8,128)S(1)} %copy.84), channel_id=1, replica_groups=mesh['y'=4,'z'=16,'c'=2,'t'=4] {'c'}, dimensions={0} | all-to-all | bytes 7340032 | tf_op jit(solution)/shard_map/all_to_all | solution.py:39
  19.2 1.1 pad_maximum_fusion
  20.2 3.5 %all-to-all-start.1 = ((bf16[4,16,56,128]{3,2,1,0:T(8,128)(2,1)}), bf16[4,16,56,128]{3,2,1,0:T(8,128)(2,1)S(1)}, u32[]{:S(2)}, u32[]{:S(2)}) async-start(bf16[4,16,56,128]{3,2,1,0:T(8,128)(2,1)} %pad_maximum_fusion), calls=%async_computation.1 | async-start | bytes 1835008 | tf_op jit(solution)/shard_map/all_to_all | solution.py:39
  23.8 13.3 %all-to-all-done.1 = bf16[4,16,56,128]{3,2,1,0:T(8,128)(2,1)S(1)} async-done(((bf16[4,16,56,128]{3,2,1,0:T(8,128)(2,1)}), bf16[4,16,56,128]{3,2,1,0:T(8,128)(2,1)S(1)}, u32[]{:S(2)}, u32[]{:S(2)}) %all-to-all-start.1) | async-done | bytes 917536 | tf_op jit(solution)/shard_map/all_to_all | solution.py:39
  37.7 29.3 %all_to_all.46 = f32[16,56,128]{2,1,0:T(8,128)S(1)} all-to-all(f32[16,56,128]{2,1,0:T(8,128)S(1)} %maximum_maximum_fusion), channel_id=1, replica_groups=mesh['y'=4,'z'=16,'c'=2,'t'=4] {'z'}, dimensions={0} | all-to-all | bytes 917504 | tf_op jit(solution)/shard_map/all_to_all | solution.py:39
  67.0 0.6 multiply_reduce_fusion
  67.6 0.7 broadcast_in_dim.13
  68.3 18.7 %all_to_all.47 = f32[32,1,128]{2,1,0:T(1,128)S(1)} all-to-all(f32[32,1,128]{2,1,0:T(1,128)S(1)} %broadcast_in_dim.13), channel_id=1, replica_groups=mesh['y'=4,'z'=16,'c'=2,'t'=4] {'y','c','t'}, dimensions={0} | all-to-all | bytes 32768 | tf_op jit(solution)/shard_map/all_to_all | solution.py:39
  87.0 0.6 broadcast_in_dim.14
  87.6 6.7 %all-to-all-start.4 = ((f32[16,1,128]{2,1,0:T(1,128)}), f32[16,1,128]{2,1,0:T(1,128)S(1)}, u32[]{:S(2)}, u32[]{:S(2)}) async-start(f32[16,1,128]{2,1,0:T(1,128)} %broadcast_in_dim.14), calls=%async_computation.4 | async-start | bytes 16384 | tf_op jit(solution)/shard_map/all_to_all | solution.py:39
  95.0 10.6 %all-to-all-done.4 = f32[16,1,128]{2,1,0:T(1,128)S(1)} async-done(((f32[16,1,128]{2,1,0:T(1,128)}), f32[16,1,128]{2,1,0:T(1,128)S(1)}, u32[]{:S(2)}, u32[]{:S(2)}) %all-to-all-start.4) | async-done | bytes 8224 | tf_op jit(solution)/shard_map/all_to_all | solution.py:39
  105.6 0.6 slice_reduce_fusion
  107.0 0.6 fusion.12
  107.6 0.6 fusion.10
  108.2 0.7 fusion.8
  109.0 15.2 %all_to_all.48 = bf16[16,56,128]{2,1,0:T(8,128)(2,1)S(1)} all-to-all(bf16[16,56,128]{2,1,0:T(8,128)(2,1)S(1)} %broadcast_in_dim.15), channel_id=1, replica_groups=mesh['y'=4,'z'=16,'c'=2,'t'=4] {'z'}, dimensions={0} | all-to-all | bytes 458752 | tf_op jit(solution)/shard_map/all_to_all | solution.py:39
  124.4 11.5 %all_to_all.49 = bf16[4,16,56,128]{3,1,2,0:T(8,128)(2,1)S(1)} all-to-all(bf16[4,16,56,128]{3,1,2,0:T(8,128)(2,1)S(1)} %broadcast_in_dim.16), channel_id=1, replica_groups=mesh['y'=4,'z'=16,'c'=2,'t'=4] {'y'}, dimensions={0} | all-to-all | bytes 1835008 | tf_op jit(solution)/shard_map/all_to_all | solution.py:39
  135.8 0.2 broadcast_in_dim.17
  136.1 12.0 %all_to_all.50 = bf16[2,4,16,56,128]{4,2,3,1,0:T(8,128)(2,1)S(1)} all-to-all(bf16[2,4,16,56,128]{4,2,3,1,0:T(8,128)(2,1)S(1)} %broadcast_in_dim.17), channel_id=1, replica_groups=mesh['y'=4,'z'=16,'c'=2,'t'=4] {'c'}, dimensions={0} | all-to-all | bytes 3670016 | tf_op jit(solution)/shard_map/all_to_all | solution.py:39
  148.1 0.3 copy.97
  148.7 1.2 copy.92
  149.9 0.5 copy.91
  150.5 1.1 reshape.98
  151.7 0.7 copy.94
  (46 shorter events, 1.5 us)
Async XLA Ops:
  2.5 1.6 %copy-start = (bf16[2,1,4096,128]{3,2,1,0:T(8,128)(2,1)S(1)}, bf16[2,1,4096,128]{3,2,1,0:T(8,128)(2,1)}, u32[]{:S(2)}) copy-start(bf16[2,1,4096,128]{3,2,1,0:T(8,128)(2,1)} %param.15) | copy-start | bytes 6291460
  4.1 0.7 copy-start.1
  20.2 16.9 %all-to-all-start.1 = ((bf16[4,16,56,128]{3,2,1,0:T(8,128)(2,1)}), bf16[4,16,56,128]{3,2,1,0:T(8,128)(2,1)S(1)}, u32[]{:S(2)}, u32[]{:S(2)}) async-start(bf16[4,16,56,128]{3,2,1,0:T(8,128)(2,1)} %pad_maximum_fusion), calls=%async_computation.1 | async-start | bytes 1835008 | tf_op jit(solution)/shard_map/all_to_all | solution.py:39
  37.4 57.0 %copy-start.11 = (s32[32]{0:T(128)S(1)}, s32[32]{0:T(128)}, u32[]{:S(2)}) copy-start(s32[32]{0:T(128)} %param.26) | copy-start | bytes 388
  37.4 69.5 %copy-start.8 = (f32[4,9]{1,0:T(4,128)S(1)}, f32[4,9]{1,0:T(4,128)}, u32[]{:S(2)}) copy-start(f32[4,9]{1,0:T(4,128)} %param.23) | copy-start | bytes 436
  37.4 69.5 %copy-start.9 = (f32[4,9]{1,0:T(4,128)S(1)}, f32[4,9]{1,0:T(4,128)}, u32[]{:S(2)}) copy-start(f32[4,9]{1,0:T(4,128)} %param.25) | copy-start | bytes 436
  37.4 69.5 %copy-start.10 = (f32[4,9]{1,0:T(4,128)S(1)}, f32[4,9]{1,0:T(4,128)}, u32[]{:S(2)}) copy-start(f32[4,9]{1,0:T(4,128)} %param.24) | copy-start | bytes 436
  37.4 70.1 %copy-start.5 = (f32[2,4,256]{2,1,0:T(4,128)S(1)}, f32[2,4,256]{2,1,0:T(4,128)}, u32[]{:S(2)}) copy-start(f32[2,4,256]{2,1,0:T(4,128)} %param.17) | copy-start | bytes 24580
  37.4 70.1 %copy-start.6 = (f32[2,4,256]{2,1,0:T(4,128)S(1)}, f32[2,4,256]{2,1,0:T(4,128)}, u32[]{:S(2)}) copy-start(f32[2,4,256]{2,1,0:T(4,128)} %param.19) | copy-start | bytes 24580
  37.5 70.1 %copy-start.7 = (f32[2,4,256]{2,1,0:T(4,128)S(1)}, f32[2,4,256]{2,1,0:T(4,128)}, u32[]{:S(2)}) copy-start(f32[2,4,256]{2,1,0:T(4,128)} %param.18) | copy-start | bytes 24580
  37.5 70.8 %copy-start.2 = (f32[32,128]{1,0:T(8,128)S(1)}, f32[32,128]{1,0:T(8,128)}, u32[]{:S(2)}) copy-start(f32[32,128]{1,0:T(8,128)} %param.20) | copy-start | bytes 49156
  37.5 70.7 %copy-start.3 = (f32[32,128]{1,0:T(8,128)S(1)}, f32[32,128]{1,0:T(8,128)}, u32[]{:S(2)}) copy-start(f32[32,128]{1,0:T(8,128)} %param.22) | copy-start | bytes 49156
  37.5 70.7 %copy-start.4 = (f32[32,128]{1,0:T(8,128)S(1)}, f32[32,128]{1,0:T(8,128)}, u32[]{:S(2)}) copy-start(f32[32,128]{1,0:T(8,128)} %param.21) | copy-start | bytes 49156
  87.6 18.0 %all-to-all-start.4 = ((f32[16,1,128]{2,1,0:T(1,128)}), f32[16,1,128]{2,1,0:T(1,128)S(1)}, u32[]{:S(2)}, u32[]{:S(2)}) async-start(f32[16,1,128]{2,1,0:T(1,128)} %broadcast_in_dim.14), calls=%async_computation.4 | async-start | bytes 16384 | tf_op jit(solution)/shard_map/all_to_all | solution.py:39

commit v2 on v1

--- a/solution.py
+++ b/solution.py
@@ -12,7 +12,9 @@
 DECAY_RATE = 0.1
 EPSILON = 1e-08
 
-Y, Z, C, T = 4, 16, 2, 4
+Y, ZH, ZL, C, T = 4, 8, 2, 2, 4
+Z = ZH * ZL
+NEAR = ("y", "w")
 
 
 def local_total(gradients):
@@ -59,10 +61,12 @@
     class_steps,
     clip_rms,
 ):
-    e = local_total(expert_grads).reshape(2, Y, Z, C, 4, 2, 128)
-    e = e.transpose(3, 1, 2, 0, 5, 4, 6).reshape(C, Y, Z, 16, 128)
-    m = local_total(embed_grads).reshape(Y, Z, C, 32, 128).transpose(2, 0, 1, 3, 4)
-    s = local_total(small_grads).reshape(Y, Z, C, 4, 9).transpose(2, 0, 1, 3, 4)
+    e = local_total(expert_grads).reshape(2, Y, ZH, ZL, C, 4, 2, 128)
+    e = e.transpose(4, 1, 3, 2, 0, 6, 5, 7).reshape(C, Y * ZL, ZH, 16, 128)
+    m = local_total(embed_grads).reshape(Y, ZH, ZL, C, 32, 128)
+    m = m.transpose(3, 0, 2, 1, 4, 5).reshape(C, Y * ZL, ZH, 32, 128)
+    s = local_total(small_grads).reshape(Y, ZH, ZL, C, 4, 9)
+    s = s.transpose(3, 0, 2, 1, 4, 5).reshape(C, Y * ZL, ZH, 4, 9)
     s = jnp.pad(s, ((0, 0),) * 3 + ((0, 4), (0, 119)))
     buf = jnp.concatenate([m, e, s], axis=3)
     got = exchange(buf, ("c",))
@@ -71,16 +75,17 @@
     small_part = part[:, :, 48:52]
     high = lax.reduce_precision(small_part, 8, 7)
     low = (small_part - high).astype(jnp.bfloat16)
-    got = exchange(jnp.concatenate([big, high.astype(jnp.bfloat16), low], axis=2), ("y",))
-    got = got.astype(jnp.float32)
-    part = got[0] + got[1] + got[2] + got[3]
-    part = jnp.concatenate([part[:, :48], part[:, 48:52] + part[:, 52:56], jnp.zeros((Z, 4, 128), jnp.float32)], axis=1)
-    got = exchange(part, ("z",))
-    total = jnp.sum(got, axis=0)
+    got = exchange(jnp.concatenate([big, high.astype(jnp.bfloat16), low], axis=2), NEAR)
+    part = jnp.sum(got.astype(jnp.float32), axis=0)
+    part = jnp.concatenate(
+        [part[:, :48], part[:, 48:52] + part[:, 52:56], jnp.zeros((ZH, 4, 128), jnp.float32)],
+        axis=1,
+    )
+    total = jnp.sum(exchange(part.reshape(ZH, 56, 128), ("z",)), axis=0)
     squares = jnp.sum(total * total)
-    line = jnp.broadcast_to(squares, (Y * C * T, 128))
-    line = exchange(line, ("y", "c", "t"))
-    line = jnp.broadcast_to(jnp.sum(line, axis=0)[None], (Z, 128))
+    line = jnp.broadcast_to(squares, (Y * ZL * C * T, 128))
+    line = exchange(line, NEAR + ("c", "t"))
+    line = jnp.broadcast_to(jnp.sum(line, axis=0)[None], (ZH, 128))
     total_squares = jnp.sum(exchange(line, ("z",))[:, 0])
     clip_factor = clip_rms * jnp.sqrt(P_TOT / total_squares)
 
@@ -121,14 +126,14 @@
         ],
         axis=0,
     )
-    full = spread(own, Z, ("z",))
-    full = spread(full, Y, ("y",))
-    full = spread(full, C, ("c",))
-    full = full.transpose(1, 2, 0, 3, 4)
-    embed_weights = full[:, :, :, :32].reshape(4096, 128)
-    expert_weights = full[:, :, :, 32:48].reshape(Y, Z, C, 2, 2, 4, 128)
-    expert_weights = expert_weights.transpose(3, 0, 1, 2, 5, 4, 6).reshape(2, 512, 256)
-    small_weights = full[:, :, :, 48:52, :9].reshape(512, 9)
+    full = spread(own, ZH, ("z",))
+    full = spread(full, Y * ZL, NEAR)
+    full = spread(full, C, ("c",)).reshape(C, Y, ZL, ZH, 56, 128)
+    full = full.transpose(1, 3, 2, 0, 4, 5)
+    embed_weights = full[..., :32, :].reshape(4096, 128)
+    expert_weights = full[..., 32:48, :].reshape(Y, ZH, ZL, C, 2, 2, 4, 128)
+    expert_weights = expert_weights.transpose(4, 0, 1, 2, 3, 6, 5, 7).reshape(2, 512, 256)
+    small_weights = full[..., 48:52, :9].reshape(512, 9)
     return (
         expert_weights,
         embed_weights,
@@ -148,8 +153,8 @@
 
 
 def solution(mesh):
-    fine = Mesh(mesh.devices.reshape(Y, Z, C, T), ("y", "z", "c", "t"))
-    sh = ("y", "z", "c")
+    fine = Mesh(mesh.devices.reshape(Y, ZH, ZL, C, T), ("y", "z", "w", "c", "t"))
+    sh = ("y", "z", "w", "c")
     in_specs = (
         P(None, sh, None, None, "t"),
         P(None, sh, None, "t"),

time: 154 us -> 150 us (0.974)
  blocking collectives: 99.9 us -> 95.3 us
  starting transfers between devices: 10.2 us -> 7.01 us
    all_to_all x6, blocking collectives: 99.9 us -> 95.3 us  [exchange(): return lax.all_to_all(x, axes, 0, 0, tiled=True)]
    all_to_all x2, starting transfers between devices: 10.2 us -> 7.01 us  [exchange(): return lax.all_to_all(x, axes, 0, 0, tiled=True)]
where the time goes in v2:
time: 150 us; the launch traced here: 149 us
  blocking collectives  95.3 us (64%)
  waiting for transfers between devices  24.4 us (16%)
  local copies, waits for them, and re-layouts  10.7 us (7%)
  other arithmetic  7.95 us (5%)
  starting transfers between devices  7.01 us (5%)
  between operations  3.49 us (2%)
    all_to_all x6, blocking collectives, exchange(): return lax.all_to_all(x, axes, 0, 0, tiled=True)  95.3 us
    all_to_all x2, waiting for transfers between devices, exchange(): return lax.all_to_all(x, axes, 0, 0, tiled=True)  24.4 us
    all_to_all x2, starting transfers between devices, exchange(): return lax.all_to_all(x, axes, 0, 0, tiled=True)  7.01 us
  transfers between devices with their start and end apart: 2, of which 2 were waited for; matrix products, arithmetic and copies ran while one was open for 0% of the time, Pallas kernels for 0%

profile of v2, /device:TPU:1, one launch (start us, length us, event | category | flops | bytes accessed | tf_op | source)
XLA Modules:
  0.0 148.9 jit_solution(6818910970001476651)
XLA Ops:
  0.6 0.8 fusion.13
  1.8 1.7 %convert_add_fusion = f32[1,1,4096,128]{3,2,1,0:T(8,128)S(1)} fusion(bf16[2,1,4096,128]{3,2,1,0:T(8,128)(2,1)} %param.15), kind=kLoop, calls=%fused_computation.2 | loop fusion | flops 1572864 | bytes 4194304 | tf_op jit(solution)/shard_map/add | solution.py:21
  3.6 0.2 copy.86
  3.8 1.0 copy-done
  4.8 1.1 convert_add_fusion.1
  5.9 1.7 %add.82 = f32[2,4,8,2,2,4,2,128]{7,6,5,4,3,2,1,0:T(2,128)S(1)} reshape(f32[1,1,2,512,256]{4,3,2,1,0:T(8,128)} %convert_add_fusion.1) | data formatting | bytes 2097152 | tf_op jit(solution)/shard_map/add | solution.py:21
  7.6 0.6 copy.87
  8.4 0.4 select_maximum_fusion
  8.8 13.2 %all_to_all.45 = f32[2,8,8,56,128]{4,3,2,1,0:T(8,128)S(1)} all-to-all(f32[2,8,8,56,128]{4,3,2,1,0:T(8,128)S(1)} %select_maximum_fusion), channel_id=1, replica_groups=mesh['y'=4,'z'=8,'w'=2,'c'=2,'t'=4] {'c'}, dimensions={0} | all-to-all | bytes 7340032 | tf_op jit(solution)/shard_map/all_to_all | solution.py:41
  22.0 0.2 fusion
  22.4 1.1 pad_maximum_fusion
  23.5 3.7 %all-to-all-start.1 = ((bf16[8,8,56,128]{3,2,1,0:T(8,128)(2,1)}), bf16[8,8,56,128]{3,2,1,0:T(8,128)(2,1)S(1)}, u32[]{:S(2)}, u32[]{:S(2)}) async-start(bf16[8,8,56,128]{3,2,1,0:T(8,128)(2,1)} %pad_maximum_fusion), calls=%async_computation.1 | async-start | bytes 1835008 | tf_op jit(solution)/shard_map/all_to_all | solution.py:41
  27.3 13.9 %all-to-all-done.1 = bf16[8,8,56,128]{3,2,1,0:T(8,128)(2,1)S(1)} async-done(((bf16[8,8,56,128]{3,2,1,0:T(8,128)(2,1)}), bf16[8,8,56,128]{3,2,1,0:T(8,128)(2,1)S(1)}, u32[]{:S(2)}, u32[]{:S(2)}) %all-to-all-start.1) | async-done | bytes 917536 | tf_op jit(solution)/shard_map/all_to_all | solution.py:41
  41.5 26.8 %all_to_all.46 = f32[8,56,128]{2,1,0:T(8,128)S(1)} all-to-all(f32[8,56,128]{2,1,0:T(8,128)S(1)} %maximum_maximum_fusion), channel_id=1, replica_groups=mesh['y'=4,'z'=8,'w'=2,'c'=2,'t'=4] {'z'}, dimensions={0} | all-to-all | bytes 458752 | tf_op jit(solution)/shard_map/all_to_all | solution.py:41
  68.4 0.6 multiply_reduce_fusion
  69.0 0.7 broadcast_in_dim.13
  69.6 17.5 %all_to_all.47 = f32[64,1,128]{2,1,0:T(1,128)S(1)} all-to-all(f32[64,1,128]{2,1,0:T(1,128)S(1)} %broadcast_in_dim.13), channel_id=1, replica_groups=mesh['y'=4,'z'=8,'w'=2,'c'=2,'t'=4] {'y','w','c','t'}, dimensions={0} | all-to-all | bytes 65536 | tf_op jit(solution)/shard_map/all_to_all | solution.py:41
  87.1 0.6 broadcast_in_dim.14
  87.7 3.3 %all-to-all-start.4 = ((f32[8,1,128]{2,1,0:T(1,128)}), f32[8,1,128]{2,1,0:T(1,128)S(1)}, u32[]{:S(2)}, u32[]{:S(2)}) async-start(f32[8,1,128]{2,1,0:T(1,128)} %broadcast_in_dim.14), calls=%async_computation.4 | async-start | bytes 8192 | tf_op jit(solution)/shard_map/all_to_all | solution.py:41
  91.7 10.5 %all-to-all-done.4 = f32[8,1,128]{2,1,0:T(1,128)S(1)} async-done(((f32[8,1,128]{2,1,0:T(1,128)}), f32[8,1,128]{2,1,0:T(1,128)S(1)}, u32[]{:S(2)}, u32[]{:S(2)}) %all-to-all-start.4) | async-done | bytes 4128 | tf_op jit(solution)/shard_map/all_to_all | solution.py:41
  102.2 0.6 slice_reduce_fusion
  103.6 0.6 fusion.11
  104.2 0.6 fusion.9
  104.9 0.7 fusion.7
  105.6 15.0 %all_to_all.48 = bf16[8,56,128]{2,1,0:T(8,128)(2,1)S(1)} all-to-all(bf16[8,56,128]{2,1,0:T(8,128)(2,1)S(1)} %broadcast_in_dim.15), channel_id=1, replica_groups=mesh['y'=4,'z'=8,'w'=2,'c'=2,'t'=4] {'z'}, dimensions={0} | all-to-all | bytes 229376 | tf_op jit(solution)/shard_map/all_to_all | solution.py:41
  120.7 13.4 %all_to_all.49 = bf16[8,8,56,128]{3,2,1,0:T(8,128)(2,1)S(1)} all-to-all(bf16[8,8,56,128]{3,2,1,0:T(8,128)(2,1)S(1)} %broadcast_in_dim.16), channel_id=1, replica_groups=mesh['y'=4,'z'=8,'w'=2,'c'=2,'t'=4] {'y','w'}, dimensions={0} | all-to-all | bytes 1835008 | tf_op jit(solution)/shard_map/all_to_all | solution.py:41
  134.1 0.4 broadcast_in_dim.17
  134.5 9.4 %all_to_all.50 = bf16[2,8,8,56,128]{4,3,2,1,0:T(8,128)(2,1)S(1)} all-to-all(bf16[2,8,8,56,128]{4,3,2,1,0:T(8,128)(2,1)S(1)} %broadcast_in_dim.17), channel_id=1, replica_groups=mesh['y'=4,'z'=8,'w'=2,'c'=2,'t'=4] {'c'}, dimensions={0} | all-to-all | bytes 3670016 | tf_op jit(solution)/shard_map/all_to_all | solution.py:41
  144.1 1.1 copy.100
  145.4 0.4 copy.99
  145.8 1.1 reshape.107
  147.0 0.7 copy.102
  (46 shorter events, 1.6 us)
Async XLA Ops:
  3.6 1.2 copy-start
  23.5 67.6 %copy-start.10 = (s32[32]{0:T(128)S(1)}, s32[32]{0:T(128)}, u32[]{:S(2)}) copy-start(s32[32]{0:T(128)} %param.26) | copy-start | bytes 388
  23.5 80.1 %copy-start.7 = (f32[4,9]{1,0:T(4,128)S(1)}, f32[4,9]{1,0:T(4,128)}, u32[]{:S(2)}) copy-start(f32[4,9]{1,0:T(4,128)} %param.23) | copy-start | bytes 436
  23.5 80.1 %copy-start.8 = (f32[4,9]{1,0:T(4,128)S(1)}, f32[4,9]{1,0:T(4,128)}, u32[]{:S(2)}) copy-start(f32[4,9]{1,0:T(4,128)} %param.25) | copy-start | bytes 436
  23.5 80.1 %copy-start.9 = (f32[4,9]{1,0:T(4,128)S(1)}, f32[4,9]{1,0:T(4,128)}, u32[]{:S(2)}) copy-start(f32[4,9]{1,0:T(4,128)} %param.24) | copy-start | bytes 436
  23.5 80.7 %copy-start.4 = (f32[2,4,256]{2,1,0:T(4,128)S(1)}, f32[2,4,256]{2,1,0:T(4,128)}, u32[]{:S(2)}) copy-start(f32[2,4,256]{2,1,0:T(4,128)} %param.17) | copy-start | bytes 24580
  23.5 80.7 %copy-start.5 = (f32[2,4,256]{2,1,0:T(4,128)S(1)}, f32[2,4,256]{2,1,0:T(4,128)}, u32[]{:S(2)}) copy-start(f32[2,4,256]{2,1,0:T(4,128)} %param.19) | copy-start | bytes 24580
  23.5 80.7 %copy-start.6 = (f32[2,4,256]{2,1,0:T(4,128)S(1)}, f32[2,4,256]{2,1,0:T(4,128)}, u32[]{:S(2)}) copy-start(f32[2,4,256]{2,1,0:T(4,128)} %param.18) | copy-start | bytes 24580
  23.5 81.3 %copy-start.1 = (f32[32,128]{1,0:T(8,128)S(1)}, f32[32,128]{1,0:T(8,128)}, u32[]{:S(2)}) copy-start(f32[32,128]{1,0:T(8,128)} %param.20) | copy-start | bytes 49156
  23.5 81.3 %copy-start.2 = (f32[32,128]{1,0:T(8,128)S(1)}, f32[32,128]{1,0:T(8,128)}, u32[]{:S(2)}) copy-start(f32[32,128]{1,0:T(8,128)} %param.22) | copy-start | bytes 49156
  23.5 81.3 %copy-start.3 = (f32[32,128]{1,0:T(8,128)S(1)}, f32[32,128]{1,0:T(8,128)}, u32[]{:S(2)}) copy-start(f32[32,128]{1,0:T(8,128)} %param.21) | copy-start | bytes 49156
  23.5 17.7 %all-to-all-start.1 = ((bf16[8,8,56,128]{3,2,1,0:T(8,128)(2,1)}), bf16[8,8,56,128]{3,2,1,0:T(8,128)(2,1)S(1)}, u32[]{:S(2)}, u32[]{:S(2)}) async-start(bf16[8,8,56,128]{3,2,1,0:T(8,128)(2,1)} %pad_maximum_fusion), calls=%async_computation.1 | async-start | bytes 1835008 | tf_op jit(solution)/shard_map/all_to_all | solution.py:41
  87.7 14.5 %all-to-all-start.4 = ((f32[8,1,128]{2,1,0:T(1,128)}), f32[8,1,128]{2,1,0:T(1,128)S(1)}, u32[]{:S(2)}, u32[]{:S(2)}) async-start(f32[8,1,128]{2,1,0:T(1,128)} %broadcast_in_dim.14), calls=%async_computation.4 | async-start | bytes 8192 | tf_op jit(solution)/shard_map/all_to_all | solution.py:41

commit v3 on v1

v3 whole, which is shorter than its diff:
```python
import functools

import jax
import jax.numpy as jnp
from jax import lax
from jax.experimental import pallas as pl
from jax.experimental.pallas import tpu as pltpu
from jax.sharding import Mesh, PartitionSpec as P

STEP = 1000
P_TOT = 3164160

BETA_ONE = 0.9
BETA_TWO = 0.999
LEARN_RATE = 0.001
DECAY_RATE = 0.1
EPSILON = 1e-08

Y, ZH, W, C, T = 4, 8, 2, 2, 4
A = Y * W
NEAR = ("y", "w")
EMB, EXP, ROWS = 32, 16, 56
SMA = EMB + EXP
SWAP = ((0, 1), (1, 0))
F32, BF16 = jnp.float32, jnp.bfloat16


def whole(shape):
    return pl.BlockSpec(shape, lambda *_: (0,) * len(shape))


def low_rows(shape):
    return lax.broadcasted_iota(jnp.int32, shape, len(shape) - 2) < 4


def flip(x):
    return pltpu.roll(x, 4, x.ndim - 2)


def pack_kernel(expert_ref, embed_ref, small_ref, keep_ref, send_ref):
    first_core = lax.axis_index("c") == 0

    def put(index, rows, zero, one):
        keep_ref[index + rows] = jnp.where(first_core, zero, one)
        send_ref[index + rows] = jnp.where(first_core, one, zero)

    small = small_ref[:, 0, :].astype(F32) + small_ref[:, 1, :].astype(F32)
    small = jnp.concatenate([small, jnp.zeros((128 - 9, 128), F32)], axis=0).T
    for z in range(ZH):
        for w in range(W):
            index = (0, w, z)
            base = (z * W + w) * C * EMB
            pair = [
                embed_ref[0, 0, pl.ds(base + c * EMB, EMB), :].astype(F32)
                + embed_ref[1, 0, pl.ds(base + c * EMB, EMB), :].astype(F32)
                for c in range(C)
            ]
            put(index, (slice(0, EMB),), *pair)
            row = (z * W + w) * 8
            for m in range(2):
                tile = expert_ref[0, 0, m, pl.ds(row, 8), :].astype(F32) + expert_ref[
                    1, 0, m, pl.ds(row, 8), :
                ].astype(F32)
                left, right = tile[:, :128], tile[:, 128:]
                upper = low_rows((8, 128))
                put(
                    index,
                    (slice(EMB + 8 * m, EMB + 8 * m + 8),),
                    jnp.where(upper, left, flip(right)),
                    jnp.where(upper, flip(left), right),
                )
            tile = small[row : row + 8]
            put(index, (slice(SMA, ROWS),), tile, flip(tile))


def pack(expert_grads, embed_grads, small_grads):
    out = jax.ShapeDtypeStruct((Y, W, ZH, ROWS, 128), F32)
    spec = pl.BlockSpec((1, W, ZH, ROWS, 128), lambda y: (y, 0, 0, 0, 0))
    return pl.pallas_call(
        pack_kernel,
        grid=(Y,),
        in_specs=[
            pl.BlockSpec((2, 1, 2, 128, 256), lambda y: (0, 0, 0, y, 0)),
            pl.BlockSpec((2, 1, 1024, 128), lambda y: (0, 0, y, 0)),
            pl.BlockSpec((9, 2, 128), lambda y: (0, 0, y)),
        ],
        out_specs=[spec, spec],
        out_shape=[out, out],
        name="pack",
    )(expert_grads, embed_grads, small_grads[:, 0].transpose(2, 0, 1))


def pair_kernel(keep_ref, got_ref, out_ref):
    out_ref[:, :, :SMA] = (keep_ref[:, :, :SMA] + got_ref[:, :, :SMA]).astype(BF16)
    small = keep_ref[:, :, SMA:] + got_ref[:, :, SMA:]
    high = small.astype(BF16).astype(F32)
    low = small - high
    shape = (W * ZH, 8, 128)
    both = jnp.where(low_rows(shape), high.reshape(shape), flip(low.reshape(shape)))
    out_ref[:, :, SMA:] = both.astype(BF16).reshape(W, ZH, 8, 128)


def add_pair(keep, got):
    spec = pl.BlockSpec((W, ZH, ROWS, 128), lambda y: (y, 0, 0, 0))
    return pl.pallas_call(
        pair_kernel,
        grid=(Y,),
        in_specs=[spec, spec],
        out_specs=spec,
        out_shape=jax.ShapeDtypeStruct((A, ZH, ROWS, 128), BF16),
        name="add_pair",
    )(keep.reshape(A, ZH, ROWS, 128), got.reshape(A, ZH, ROWS, 128))


def near_kernel(got_ref, out_ref):
    total = got_ref[0].astype(F32)
    for a in range(1, A):
        total = total + got_ref[a].astype(F32)
    out_ref[:, :SMA] = total[:, :SMA]
    small = total[:, SMA:]
    out_ref[:, SMA:] = small + flip(small)


def add_near(got):
    return pl.pallas_call(
        near_kernel,
        grid=(4,),
        in_specs=[pl.BlockSpec((A, ZH // 4, ROWS, 128), lambda i: (0, i, 0, 0))],
        out_specs=pl.BlockSpec((ZH // 4, ROWS, 128), lambda i: (i, 0, 0)),
        out_shape=jax.ShapeDtypeStruct((ZH, ROWS, 128), F32),
        name="add_near",
    )(got)


def far_kernel(got_ref, total_ref, line_ref):
    total = got_ref[0]
    for a in range(1, ZH):
        total = total + got_ref[a]
    total_ref[...] = total
    main = total[: SMA + 4]
    line_ref[...] = jnp.full(line_ref.shape, jnp.sum(main * main), F32)


def add_far(got):
    return pl.pallas_call(
        far_kernel,
        out_shape=[
            jax.ShapeDtypeStruct((ROWS, 128), F32),
            jax.ShapeDtypeStruct((A * C * T, 128), F32),
        ],
        name="add_far",
    )(got)


def line_kernel(line_ref, out_ref):
    total = jnp.sum(line_ref[...], axis=0, keepdims=True)
    out_ref[...] = jnp.broadcast_to(total, out_ref.shape)


def add_line(line):
    return pl.pallas_call(
        line_kernel, out_shape=jax.ShapeDtypeStruct((ZH, 128), F32), name="add_line"
    )(line)


def update(scaled, first, second, master, corr_one, corr_two):
    first_new = BETA_ONE * first + (1.0 - BETA_ONE) * scaled
    second_new = BETA_TWO * second + (1.0 - BETA_TWO) * scaled * scaled
    step = (
        first_new / corr_one / (jnp.sqrt(second_new / corr_two) + EPSILON) + DECAY_RATE * master
    )
    return first_new, second_new, step, master - LEARN_RATE * step


def adam_kernel(
    line_ref,
    total_ref,
    rms_ref,
    corr_ref,
    exp_m,
    exp_f,
    exp_s,
    emb_m,
    emb_f,
    emb_s,
    sma_m,
    sma_f,
    sma_s,
    weights_ref,
    exp_mo,
    exp_fo,
    exp_so,
    emb_mo,
    emb_fo,
    emb_so,
    emb_step,
    sma_mo,
    sma_fo,
    sma_so,
    clip_ref,
):
    fixed = (1.0 - BETA_ONE**STEP, 1.0 - BETA_TWO**STEP)
    squares = jnp.sum(line_ref[...], axis=0, keepdims=True)
    factor = rms_ref[0, 0] * jnp.sqrt(P_TOT / squares)
    clip_ref[...] = factor
    first, second, step, master = update(
        factor * total_ref[:EMB], emb_f[...], emb_s[...], emb_m[...], corr_ref[0], corr_ref[1]
    )
    emb_fo[...], emb_so[...], emb_step[...], emb_mo[...] = first, second, step, master
    chunks = [master.astype(BF16).astype(F32)]
    for m in range(2):
        halves = []
        for h in range(2):
            at = (m, slice(None), slice(128 * h, 128 * h + 128))
            row = EMB + 8 * m + 4 * h
            first, second, _, master = update(
                factor * total_ref[row : row + 4], exp_f[at], exp_s[at], exp_m[at], *fixed
            )
            exp_fo[at], exp_so[at], exp_mo[at] = first, second, master
            halves.append(master)
        chunks.append(jnp.concatenate(halves, axis=0))
    first, second, _, master = update(
        factor[:, :9] * total_ref[SMA : SMA + 4, :9], sma_f[...], sma_s[...], sma_m[...], *fixed
    )
    sma_fo[...], sma_so[...], sma_mo[...] = first, second, master
    wide = jnp.concatenate([master, jnp.zeros((4, 128 - 9), F32)], axis=1)
    chunks.append(jnp.concatenate([wide, jnp.zeros((4, 128), F32)], axis=0))
    chunk = jnp.concatenate(chunks, axis=0).astype(BF16)
    for a in range(ZH):
        weights_ref[a] = chunk


def adam(line, total, rms, corr, states):
    shapes = [(ZH, ROWS, 128)] + [(2, 4, 256)] * 3 + [(32, 128)] * 4 + [(4, 9)] * 3 + [(1, 128)]
    out = [jax.ShapeDtypeStruct(n, F32) for n in shapes]
    out[0] = jax.ShapeDtypeStruct(shapes[0], BF16)
    vmem = pl.BlockSpec(memory_space=pltpu.VMEM)
    return pl.pallas_call(
        adam_kernel,
        in_specs=[vmem, vmem, pl.BlockSpec(memory_space=pltpu.SMEM)] + [vmem] * 10,
        out_shape=out,
        name="adam",
    )(line, total, rms, corr, *states)


def unpack_kernel(own_ref, other_ref, expert_ref, embed_ref, small_ref):
    first_core = lax.axis_index("c") == 0
    tiles = []
    for z in range(ZH):
        for w in range(W):
            own, other = own_ref[w, z], other_ref[w, z]
            pair = (jnp.where(first_core, own, other), jnp.where(first_core, other, own))
            base = (z * W + w) * C * EMB
            for c in range(C):
                embed_ref[pl.ds(base + c * EMB, EMB), :] = pair[c][:EMB]
            row = (z * W + w) * 8
            upper = low_rows((8, 128))
            for m in range(2):
                zero, one = (p[EMB + 8 * m : EMB + 8 * m + 8].astype(F32) for p in pair)
                expert_ref[m, pl.ds(row, 8), :128] = jnp.where(upper, zero, flip(one)).astype(BF16)
                expert_ref[m, pl.ds(row, 8), 128:] = jnp.where(upper, flip(zero), one).astype(BF16)
            zero, one = (p[SMA:].astype(F32) for p in pair)
            tiles.append(jnp.where(upper, zero, flip(one)))
    small_ref[...] = jnp.concatenate(tiles, axis=0).T[:9].astype(BF16)


def unpack(own, other):
    spec = pl.BlockSpec((W, ZH, ROWS, 128), lambda y: (y, 0, 0, 0))
    expert, embed, small = pl.pallas_call(
        unpack_kernel,
        grid=(Y,),
        in_specs=[spec, spec],
        out_specs=[
            pl.BlockSpec((2, 128, 256), lambda y: (0, y, 0)),
            pl.BlockSpec((1024, 128), lambda y: (y, 0)),
            pl.BlockSpec((9, 128), lambda y: (0, y)),
        ],
        out_shape=[
            jax.ShapeDtypeStruct((2, 512, 256), BF16),
            jax.ShapeDtypeStruct((4096, 128), BF16),
            jax.ShapeDtypeStruct((9, 512), BF16),
        ],
        name="unpack",
    )(own, other)
    return expert, embed, small.T


def exchange(x, axes):
    return lax.all_to_all(x, axes, 0, 0, tiled=True)


def body(
    expert_grads,
    embed_grads,
    small_grads,
    expert_master,
    expert_first,
    expert_second,
    embed_master,
    embed_first,
    embed_second,
    small_master,
    small_first,
    small_second,
    class_steps,
    clip_rms,
):
    keep, send = pack(expert_grads, embed_grads, small_grads)
    near = add_pair(keep, lax.ppermute(send, "c", SWAP))
    far = add_near(exchange(near, NEAR))
    total, line = add_far(exchange(far, ("z",)))
    line = exchange(add_line(exchange(line, NEAR + ("c", "t"))), ("z",))
    row_float = class_steps.astype(F32)[:, None]
    corr = jnp.stack([1.0 - BETA_ONE**row_float, 1.0 - BETA_TWO**row_float])
    corr = jnp.broadcast_to(corr, (2, EMB, 128))
    states = (
        expert_master,
        expert_first,
        expert_second,
        embed_master,
        embed_first,
        embed_second,
        small_master,
        small_first,
        small_second,
    )
    weights, *new, clip = adam(line, total, clip_rms.reshape(1, 1), corr, states)
    own = exchange(weights, ("z",))
    own = exchange(jnp.broadcast_to(own[None], (A,) + own.shape), NEAR)
    expert_w, embed_w, small_w = unpack(own, lax.ppermute(own, "c", SWAP))
    return (expert_w, embed_w, small_w, *new, clip[0, 0])


def solution(mesh):
    fine = Mesh(mesh.devices.reshape(Y, ZH, W, C, T), ("y", "z", "w", "c", "t"))
    sh = ("y", "z", "w", "c")
    in_specs = (
        P(None, sh, None, None, "t"),
        P(None, sh, None, "t"),
        P(None, sh, None, "t"),
        P(None, sh, "t"),
        P(None, sh, "t"),
        P(None, sh, "t"),
        P(sh, "t"),
        P(sh, "t"),
        P(sh, "t"),
        P(sh, "t"),
        P(sh, "t"),
        P(sh, "t"),
        P(sh),
        P(),
    )
    out_specs = (
        P(None, None, "t"),
        P(None, "t"),
        P(None, "t"),
        P(None, sh, "t"),
        P(None, sh, "t"),
        P(None, sh, "t"),
        P(sh, "t"),
        P(sh, "t"),
        P(sh, "t"),
        P(sh, "t"),
        P(sh, "t"),
        P(sh, "t"),
        P(sh, "t"),
        P(),
    )
    return jax.shard_map(body, mesh=fine, in_specs=in_specs, out_specs=out_specs, check_vma=False)
```

time: 154 us -> 153 us (level)
  blocking collectives: 99.9 us -> 73.5 us
  Pallas kernels: 0 us -> 20.2 us
  starting transfers between devices: 10.2 us -> 29.1 us
  other arithmetic: 6.73 us -> 0.01 us
  local copies, waits for them, and re-layouts: 9.22 us -> 3.67 us
  between operations: 3.51 us -> 1.37 us
    all_to_all x6 -> x4, blocking collectives: 99.9 us -> 73.5 us  [exchange(): return lax.all_to_all(x, axes, 0, 0, tiled=True)]
    pallas_call x0 -> x7, Pallas kernels: none -> 20.2 us  [the longest x1 4.51 us: pack(): pl.pallas_call(pack_kernel, grid=(Y,), in_specs=[pl.BlockSpec((2, 1, 2, 1...]
    ppermute x0 -> x2, starting transfers between devices: none -> 15.2 us  [the longest x1 8.77 us: body(): near = add_pair(keep, lax.ppermute(send, 'c', SWAP))]
    ppermute x0 -> x2, waiting for transfers between devices: none -> 5.68 us  [the longest x1 3.6 us: body(): near = add_pair(keep, lax.ppermute(send, 'c', SWAP))]
    all_to_all x2, waiting for transfers between devices: 23.9 us -> 18.2 us  [exchange(): return lax.all_to_all(x, axes, 0, 0, tiled=True)]
    all_to_all x2, starting transfers between devices: 10.2 us -> 13.9 us  [exchange(): return lax.all_to_all(x, axes, 0, 0, tiled=True)]
    convert_element_type x5 -> x0, other arithmetic: 2.12 us -> none  [the longest x1 0.71 us: body(): embed_master_new.astype(jnp.bfloat16)]
    add x6 -> x0, other arithmetic: 1.82 us -> none  [the longest x3 1.54 us: local_total(): gradients[0, 0].astype(jnp.float32) + gradients[1, 0].astype(jnp.float32)]
  transfers between devices with their start and end apart: 2 -> 4, of which waited for: 2 -> 4; matrix products, arithmetic and copies ran while one was open for 0% -> 0% of each run, Pallas kernels for 0% -> 0%
where the time goes in v3:
time: 153 us; the launch traced here: 152 us
  blocking collectives  73.5 us (48%)
  starting transfers between devices  29.1 us (19%)
  waiting for transfers between devices  23.9 us (16%)
  Pallas kernels  20.2 us (13%)
  local copies, waits for them, and re-layouts  3.67 us (2%)
    all_to_all x4, blocking collectives, exchange(): return lax.all_to_all(x, axes, 0, 0, tiled=True)  73.5 us
    all_to_all x2, waiting for transfers between devices, exchange(): return lax.all_to_all(x, axes, 0, 0, tiled=True)  18.2 us
    all_to_all x2, starting transfers between devices, exchange(): return lax.all_to_all(x, axes, 0, 0, tiled=True)  13.9 us
    ppermute x1, starting transfers between devices, body(): near = add_pair(keep, lax.ppermute(send, 'c', SWAP))  8.77 us
    ppermute x1, starting transfers between devices, body(): expert_w, embed_w, small_w = unpack(own, lax.ppermute(own, 'c', SWAP))  6.45 us
    pallas_call x1, Pallas kernels, pack(): pl.pallas_call(pack_kernel, grid=(Y,), in_specs=[pl.BlockSpec((2, 1, 2, 1...  4.51 us
    pallas_call x1, Pallas kernels, unpack(): pl.pallas_call(unpack_kernel, grid=(Y,), in_specs=[spec, spec], out_specs...  3.96 us
    pallas_call x1, Pallas kernels, add_pair(): pl.pallas_call(pair_kernel, grid=(Y,), in_specs=[spec, spec], out_specs=s...  3.86 us
  transfers between devices with their start and end apart: 4, of which 4 were waited for; matrix products, arithmetic and copies ran while one was open for 0% of the time, Pallas kernels for 0%

profile of v3, /device:TPU:1, one launch (start us, length us, event | category | flops | bytes accessed | tf_op | source)
XLA Modules:
  0.0 151.8 jit_solution(18359057856172176072)
XLA Ops:
  0.6 4.5 %pack.1 = (f32[4,2,8,56,128]{4,3,2,1,0:T(8,128)}, f32[4,2,8,56,128]{4,3,2,1,0:T(8,128)}) custom-call(bf16[2,1,2,512,256]{4,3,2,1,0:T(8,128)(2,1)} %expert_ref.1, bf16[2,1,4096,128]{3,2,1,0:T(8,128)(2,1)} %embed_ref.1, bf16[9,2,512]{2,1,0:T(2,128)(2,1)} %bitcast.27), custom_call_target="tpu_custom_call" | custom-call | tf_op jit(solution)/shard_map/pack/pallas_call | solution.py:79
  5.2 8.8 %collective-permute-start = (f32[4,2,8,56,128]{4,3,2,1,0:T(8,128)}, f32[4,2,8,56,128]{4,3,2,1,0:T(8,128)S(1)}, u32[]{:S(2)}, u32[]{:S(2)}) collective-permute-start(f32[4,2,8,56,128]{4,3,2,1,0:T(8,128)} %get-tuple-element.34), channel_id=1, source_target_pairs={{0,4},{4,0},{1,5},{5,1},{2,6},{6,2},{3,7},{7,3},{8,12},{12,8},{9,1... | collective-permute-start | bytes 5505032 | tf_op jit(solution)/shard_map/ppermute | solution.py:309
  13.9 3.6 %collective-permute-done = f32[4,2,8,56,128]{4,3,2,1,0:T(8,128)S(1)} collective-permute-done((f32[4,2,8,56,128]{4,3,2,1,0:T(8,128)}, f32[4,2,8,56,128]{4,3,2,1,0:T(8,128)S(1)}, u32[]{:S(2)}, u32[]{:S(2)}) %collective-permute-start) | collective-permute-done | bytes 1835040 | tf_op jit(solution)/shard_map/ppermute | solution.py:309
  17.5 0.0 copy-start.1
  17.5 1.2 copy-done.1
  18.8 3.9 %add_pair.1 = bf16[8,8,56,128]{3,2,1,0:T(8,128)(2,1)} custom-call(f32[8,8,56,128]{3,2,1,0:T(8,128)} %bitcast.23, f32[8,8,56,128]{3,2,1,0:T(8,128)} %bitcast.24), custom_call_target="tpu_custom_call" | custom-call | tf_op jit(solution)/shard_map/add_pair/pallas_call | solution.py:105
  22.6 0.0 copy-start.5
  22.6 18.4 %all_to_all.42.got_ref = bf16[8,8,56,128]{3,2,1,0:T(8,128)(2,1)} all-to-all(bf16[8,8,56,128]{3,2,1,0:T(8,128)(2,1)} %add_pair.1), channel_id=1, replica_groups=mesh['y'=4,'z'=8,'w'=2,'c'=2,'t'=4] {'y','w'}, dimensions={0} | all-to-all | bytes 1835008 | tf_op jit(solution)/shard_map/all_to_all | solution.py:289
  41.1 3.2 %add_near.1 = f32[8,56,128]{2,1,0:T(8,128)} custom-call(bf16[8,8,56,128]{3,2,1,0:T(8,128)(2,1)} %all_to_all.42.got_ref), custom_call_target="tpu_custom_call" | custom-call | tf_op jit(solution)/shard_map/add_near/pallas_call | solution.py:125
  44.3 25.8 %all_to_all.43.got_ref = f32[8,56,128]{2,1,0:T(8,128)} all-to-all(f32[8,56,128]{2,1,0:T(8,128)} %add_near.1), channel_id=1, replica_groups=mesh['y'=4,'z'=8,'w'=2,'c'=2,'t'=4] {'z'}, dimensions={0} | all-to-all | bytes 458752 | tf_op jit(solution)/shard_map/all_to_all | solution.py:289
  70.1 1.7 %add_far.1 = (f32[56,128]{1,0:T(8,128)}, f32[64,128]{1,0:T(8,128)}) custom-call(f32[8,56,128]{2,1,0:T(8,128)} %all_to_all.43.got_ref), custom_call_target="tpu_custom_call" | custom-call | tf_op jit(solution)/shard_map/add_far/pallas_call | solution.py:145
  71.8 10.6 %all-to-all-start.2 = ((f32[64,1,128]{2,1,0:T(1,128)}), f32[64,1,128]{2,1,0:T(1,128)S(1)}, u32[]{:S(2)}, u32[]{:S(2)}) async-start(f32[64,1,128]{2,1,0:T(1,128)} %bitcast.26), calls=%async_computation.2 | async-start | bytes 65536 | tf_op jit(solution)/shard_map/all_to_all | solution.py:289
  82.4 0.0 copy-done.5
  82.4 7.7 %all-to-all-done.2 = f32[64,1,128]{2,1,0:T(1,128)S(1)} async-done(((f32[64,1,128]{2,1,0:T(1,128)}), f32[64,1,128]{2,1,0:T(1,128)S(1)}, u32[]{:S(2)}, u32[]{:S(2)}) %all-to-all-start.2) | async-done | bytes 32800 | tf_op jit(solution)/shard_map/all_to_all | solution.py:289
  90.1 0.0 copy-start.3
  90.1 0.6 copy-done.3
  90.7 1.4 add_line.1
  92.1 3.3 %all-to-all-start.3 = ((f32[8,1,128]{2,1,0:T(1,128)}), f32[8,1,128]{2,1,0:T(1,128)S(1)}, u32[]{:S(2)}, u32[]{:S(2)}) async-start(f32[8,1,128]{2,1,0:T(1,128)} %bitcast.29), calls=%async_computation.3 | async-start | bytes 8192 | tf_op jit(solution)/shard_map/all_to_all | solution.py:289
  96.0 10.5 %all-to-all-done.3 = f32[8,1,128]{2,1,0:T(1,128)S(1)} async-done(((f32[8,1,128]{2,1,0:T(1,128)}), f32[8,1,128]{2,1,0:T(1,128)S(1)}, u32[]{:S(2)}, u32[]{:S(2)}) %all-to-all-start.3) | async-done | bytes 4128 | tf_op jit(solution)/shard_map/all_to_all | solution.py:289
  106.6 0.0 copy-start.4
  106.6 0.7 broadcast_in_dim.7.corr_ref
  107.3 0.0 copy-done.4
  107.3 1.6 %adam.1 = (bf16[8,56,128]{2,1,0:T(8,128)(2,1)}, f32[2,4,256]{2,1,0:T(4,128)}, f32[2,4,256]{2,1,0:T(4,128)}, f32[2,4,256]{2,1,0:T(4,128)}, f32[32,128]{1,0:T(8,12...) custom-call(f32[8,128]{1,0:T(8,128)} %bitcast.28, ...), custom_call_target="tpu_custom_call" | custom-call | tf_op jit(solution)/shard_map/adam/pallas_call | solution.py:238
  108.9 15.9 %all_to_all.44 = bf16[8,56,128]{2,1,0:T(8,128)(2,1)S(1)} all-to-all(bf16[8,56,128]{2,1,0:T(8,128)(2,1)} %get-tuple-element.37), channel_id=1, replica_groups=mesh['y'=4,'z'=8,'w'=2,'c'=2,'t'=4] {'z'}, dimensions={0} | all-to-all | bytes 229376 | tf_op jit(solution)/shard_map/all_to_all | solution.py:289
  124.7 0.1 broadcast_in_dim.16
  124.9 13.4 %all_to_all.45.own_ref = bf16[8,8,56,128]{3,2,1,0:T(8,128)(2,1)S(1)} all-to-all(bf16[8,8,56,128]{3,2,1,0:T(8,128)(2,1)S(1)} %broadcast_in_dim.16), channel_id=1, replica_groups=mesh['y'=4,'z'=8,'w'=2,'c'=2,'t'=4] {'y','w'}, dimensions={0} | all-to-all | bytes 1835008 | tf_op jit(solution)/shard_map/all_to_all | solution.py:289
  138.3 0.0 copy-start
  138.3 6.5 %collective-permute-start.1 = (bf16[8,8,56,128]{3,2,1,0:T(8,128)(2,1)S(1)}, bf16[8,8,56,128]{3,2,1,0:T(8,128)(2,1)S(1)}, u32[]{:S(2)}, u32[]{:S(2)}) collective-permute-start(bf16[8,8,56,128]{3,2,1,0:T(8,128)(2,1)S(1)} %all_to_all.45.own_ref), channel_id=1, source_target_pairs={{0,4},{4,0},{1,5},{5,1},{2,6},{6,2},{3,7},{7,3},{8,12},{12,8},{9,1... | collective-permute-start | bytes 2752520 | tf_op jit(solution)/shard_map/ppermute | solution.py:330
  144.7 2.1 %collective-permute-done.1.other_ref = bf16[8,8,56,128]{3,2,1,0:T(8,128)(2,1)S(1)} collective-permute-done((bf16[8,8,56,128]{3,2,1,0:T(8,128)(2,1)S(1)}, bf16[8,8,56,128]{3,2,1,0:T(8,128)(2,1)S(1)}, u32[]{:S(2)}, u32[]{:S(2)}) %collective-permute-start.1) | collective-permute-done | bytes 917536 | tf_op jit(solution)/shard_map/ppermute | solution.py:330
  146.8 0.0 copy-done
  146.8 1.0 copy-done.2
  147.8 4.0 %unpack.1 = (bf16[2,512,256]{2,1,0:T(8,128)(2,1)}, bf16[4096,128]{1,0:T(8,128)(2,1)}, bf16[9,512]{1,0:T(8,128)(2,1)}) custom-call(bf16[8,8,56,128]{3,2,1,0:T(8,128)(2,1)} %copy-done, bf16[8,8,56,128]{3,2,1,0:T(8,128)(2,1)} %copy-done.2), custom_call_target="tpu_custom_call" | custom-call | tf_op jit(solution)/shard_map/unpack/pallas_call | solution.py:269
  (3 shorter events, 0.0 us)
Async XLA Ops:
  5.2 12.4 %collective-permute-start = (f32[4,2,8,56,128]{4,3,2,1,0:T(8,128)}, f32[4,2,8,56,128]{4,3,2,1,0:T(8,128)S(1)}, u32[]{:S(2)}, u32[]{:S(2)}) collective-permute-start(f32[4,2,8,56,128]{4,3,2,1,0:T(8,128)} %get-tuple-element.34), channel_id=1, source_target_pairs={{0,4},{4,0},{1,5},{5,1},{2,6},{6,2},{3,7},{7,3},{8,12},{12,8},{9,1... | collective-permute-start | bytes 5505032 | tf_op jit(solution)/shard_map/ppermute | solution.py:309
  17.5 1.2 copy-start.1
  22.6 59.7 %copy-start.5 = (s32[32]{0:T(128)S(1)}, s32[32]{0:T(128)}, u32[]{:S(2)}) copy-start(s32[32]{0:T(128)} %param.26) | copy-start | bytes 388
  71.8 18.3 %all-to-all-start.2 = ((f32[64,1,128]{2,1,0:T(1,128)}), f32[64,1,128]{2,1,0:T(1,128)S(1)}, u32[]{:S(2)}, u32[]{:S(2)}) async-start(f32[64,1,128]{2,1,0:T(1,128)} %bitcast.26), calls=%async_computation.2 | async-start | bytes 65536 | tf_op jit(solution)/shard_map/all_to_all | solution.py:289
  90.1 0.6 copy-start.3
  92.1 14.5 %all-to-all-start.3 = ((f32[8,1,128]{2,1,0:T(1,128)}), f32[8,1,128]{2,1,0:T(1,128)S(1)}, u32[]{:S(2)}, u32[]{:S(2)}) async-start(f32[8,1,128]{2,1,0:T(1,128)} %bitcast.29), calls=%async_computation.3 | async-start | bytes 8192 | tf_op jit(solution)/shard_map/all_to_all | solution.py:289
  106.6 0.7 copy-start.4
  138.3 8.5 %copy-start = (bf16[8,8,56,128]{3,2,1,0:T(8,128)(2,1)}, bf16[8,8,56,128]{3,2,1,0:T(8,128)(2,1)S(1)}, u32[]{:S(2)}) copy-start(bf16[8,8,56,128]{3,2,1,0:T(8,128)(2,1)S(1)} %all_to_all.45.own_ref) | copy-start | bytes 2752516
  138.3 8.5 %collective-permute-start.1 = (bf16[8,8,56,128]{3,2,1,0:T(8,128)(2,1)S(1)}, bf16[8,8,56,128]{3,2,1,0:T(8,128)(2,1)S(1)}, u32[]{:S(2)}, u32[]{:S(2)}) collective-permute-start(bf16[8,8,56,128]{3,2,1,0:T(8,128)(2,1)S(1)} %all_to_all.45.own_ref), channel_id=1, source_target_pairs={{0,4},{4,0},{1,5},{5,1},{2,6},{6,2},{3,7},{7,3},{8,12},{12,8},{9,1... | collective-permute-start | bytes 2752520 | tf_op jit(solution)/shard_map/ppermute | solution.py:330
  146.8 1.0 copy-start.2

commit v4 on v3

--- a/solution.py
+++ b/solution.py
@@ -1,5 +1,3 @@
-import functools
-
 import jax
 import jax.numpy as jnp
 from jax import lax
@@ -23,10 +21,11 @@
 SMA = EMB + EXP
 SWAP = ((0, 1), (1, 0))
 F32, BF16 = jnp.float32, jnp.bfloat16
-
-
-def whole(shape):
-    return pl.BlockSpec(shape, lambda *_: (0,) * len(shape))
+VMEM = pl.BlockSpec(memory_space=pltpu.VMEM)
+
+
+def in_hbm(x):
+    return pltpu.with_memory_space_constraint(x, pltpu.HBM)
 
 
 def low_rows(shape):
@@ -38,17 +37,27 @@
 
 
 def pack_kernel(expert_ref, embed_ref, small_ref, keep_ref, send_ref):
-    first_core = lax.axis_index("c") == 0
-
-    def put(index, rows, zero, one):
-        keep_ref[index + rows] = jnp.where(first_core, zero, one)
-        send_ref[index + rows] = jnp.where(first_core, one, zero)
+    @pl.when(lax.axis_index("c") == 0)
+    def _():
+        pack_rows(expert_ref, embed_ref, small_ref, (keep_ref, send_ref))
+
+    @pl.when(lax.axis_index("c") == 1)
+    def _():
+        pack_rows(expert_ref, embed_ref, small_ref, (send_ref, keep_ref))
+
+
+def pack_rows(expert_ref, embed_ref, small_ref, outs):
+    y = pl.program_id(0)
+
+    def put(index, rows, *values):
+        for ref, value in zip(outs, values):
+            ref[index + rows] = value
 
     small = small_ref[:, 0, :].astype(F32) + small_ref[:, 1, :].astype(F32)
     small = jnp.concatenate([small, jnp.zeros((128 - 9, 128), F32)], axis=0).T
     for z in range(ZH):
         for w in range(W):
-            index = (0, w, z)
+            index = (y, w, z)
             base = (z * W + w) * C * EMB
             pair = [
                 embed_ref[0, 0, pl.ds(base + c * EMB, EMB), :].astype(F32)
@@ -74,8 +83,7 @@
 
 
 def pack(expert_grads, embed_grads, small_grads):
-    out = jax.ShapeDtypeStruct((Y, W, ZH, ROWS, 128), F32)
-    spec = pl.BlockSpec((1, W, ZH, ROWS, 128), lambda y: (y, 0, 0, 0, 0))
+    out = pltpu.VMEM((Y, W, ZH, ROWS, 128), F32)
     return pl.pallas_call(
         pack_kernel,
         grid=(Y,),
@@ -84,83 +92,25 @@
             pl.BlockSpec((2, 1, 1024, 128), lambda y: (0, 0, y, 0)),
             pl.BlockSpec((9, 2, 128), lambda y: (0, 0, y)),
         ],
-        out_specs=[spec, spec],
+        out_specs=[VMEM, VMEM],
         out_shape=[out, out],
+        compiler_params=pltpu.CompilerParams(vmem_limit_bytes=16 << 20),
         name="pack",
-    )(expert_grads, embed_grads, small_grads[:, 0].transpose(2, 0, 1))
-
-
-def pair_kernel(keep_ref, got_ref, out_ref):
-    out_ref[:, :, :SMA] = (keep_ref[:, :, :SMA] + got_ref[:, :, :SMA]).astype(BF16)
-    small = keep_ref[:, :, SMA:] + got_ref[:, :, SMA:]
-    high = small.astype(BF16).astype(F32)
-    low = small - high
-    shape = (W * ZH, 8, 128)
-    both = jnp.where(low_rows(shape), high.reshape(shape), flip(low.reshape(shape)))
-    out_ref[:, :, SMA:] = both.astype(BF16).reshape(W, ZH, 8, 128)
+    )(in_hbm(expert_grads), in_hbm(embed_grads), in_hbm(small_grads[:, 0].transpose(2, 0, 1)))
 
 
 def add_pair(keep, got):
-    spec = pl.BlockSpec((W, ZH, ROWS, 128), lambda y: (y, 0, 0, 0))
-    return pl.pallas_call(
-        pair_kernel,
-        grid=(Y,),
-        in_specs=[spec, spec],
-        out_specs=spec,
-        out_shape=jax.ShapeDtypeStruct((A, ZH, ROWS, 128), BF16),
-        name="add_pair",
-    )(keep.reshape(A, ZH, ROWS, 128), got.reshape(A, ZH, ROWS, 128))
-
-
-def near_kernel(got_ref, out_ref):
-    total = got_ref[0].astype(F32)
-    for a in range(1, A):
-        total = total + got_ref[a].astype(F32)
-    out_ref[:, :SMA] = total[:, :SMA]
-    small = total[:, SMA:]
-    out_ref[:, SMA:] = small + flip(small)
+    part = (keep + got).reshape(A, ZH, ROWS, 128)
+    small = part[:, :, SMA : SMA + 4]
+    high = lax.reduce_precision(small, 8, 7)
+    terms = [part[:, :, :SMA], high, small - high]
+    return jnp.concatenate([x.astype(BF16) for x in terms], axis=2)
 
 
 def add_near(got):
-    return pl.pallas_call(
-        near_kernel,
-        grid=(4,),
-        in_specs=[pl.BlockSpec((A, ZH // 4, ROWS, 128), lambda i: (0, i, 0, 0))],
-        out_specs=pl.BlockSpec((ZH // 4, ROWS, 128), lambda i: (i, 0, 0)),
-        out_shape=jax.ShapeDtypeStruct((ZH, ROWS, 128), F32),
-        name="add_near",
-    )(got)
-
-
-def far_kernel(got_ref, total_ref, line_ref):
-    total = got_ref[0]
-    for a in range(1, ZH):
-        total = total + got_ref[a]
-    total_ref[...] = total
-    main = total[: SMA + 4]
-    line_ref[...] = jnp.full(line_ref.shape, jnp.sum(main * main), F32)
-
-
-def add_far(got):
-    return pl.pallas_call(
-        far_kernel,
-        out_shape=[
-            jax.ShapeDtypeStruct((ROWS, 128), F32),
-            jax.ShapeDtypeStruct((A * C * T, 128), F32),
-        ],
-        name="add_far",
-    )(got)
-
-
-def line_kernel(line_ref, out_ref):
-    total = jnp.sum(line_ref[...], axis=0, keepdims=True)
-    out_ref[...] = jnp.broadcast_to(total, out_ref.shape)
-
-
-def add_line(line):
-    return pl.pallas_call(
-        line_kernel, out_shape=jax.ShapeDtypeStruct((ZH, 128), F32), name="add_line"
-    )(line)
+    total = jnp.sum(got.astype(F32), axis=0)
+    small = total[:, SMA : SMA + 4] + total[:, SMA + 4 :]
+    return jnp.concatenate([total[:, :SMA], small, jnp.zeros((ZH, 4, 128), F32)], axis=1)
 
 
 def update(scaled, first, second, master, corr_one, corr_two):
@@ -233,22 +183,24 @@
 def adam(line, total, rms, corr, states):
     shapes = [(ZH, ROWS, 128)] + [(2, 4, 256)] * 3 + [(32, 128)] * 4 + [(4, 9)] * 3 + [(1, 128)]
     out = [jax.ShapeDtypeStruct(n, F32) for n in shapes]
-    out[0] = jax.ShapeDtypeStruct(shapes[0], BF16)
-    vmem = pl.BlockSpec(memory_space=pltpu.VMEM)
+    out[0] = pltpu.VMEM(shapes[0], BF16)
     return pl.pallas_call(
         adam_kernel,
-        in_specs=[vmem, vmem, pl.BlockSpec(memory_space=pltpu.SMEM)] + [vmem] * 10,
+        in_specs=[VMEM, VMEM, pl.BlockSpec(memory_space=pltpu.SMEM)] + [VMEM] * 10,
+        out_specs=[VMEM] * len(out),
         out_shape=out,
+        compiler_params=pltpu.CompilerParams(vmem_limit_bytes=16 << 20),
         name="adam",
     )(line, total, rms, corr, *states)
 
 
 def unpack_kernel(own_ref, other_ref, expert_ref, embed_ref, small_ref):
     first_core = lax.axis_index("c") == 0
+    y = pl.program_id(0)
     tiles = []
     for z in range(ZH):
         for w in range(W):
-            own, other = own_ref[w, z], other_ref[w, z]
+            own, other = own_ref[y * W + w, z], other_ref[y * W + w, z]
             pair = (jnp.where(first_core, own, other), jnp.where(first_core, other, own))
             base = (z * W + w) * C * EMB
             for c in range(C):
@@ -265,11 +217,10 @@
 
 
 def unpack(own, other):
-    spec = pl.BlockSpec((W, ZH, ROWS, 128), lambda y: (y, 0, 0, 0))
     expert, embed, small = pl.pallas_call(
         unpack_kernel,
         grid=(Y,),
-        in_specs=[spec, spec],
+        in_specs=[VMEM, VMEM],
         out_specs=[
             pl.BlockSpec((2, 128, 256), lambda y: (0, y, 0)),
             pl.BlockSpec((1024, 128), lambda y: (y, 0)),
@@ -280,8 +231,9 @@
             jax.ShapeDtypeStruct((4096, 128), BF16),
             jax.ShapeDtypeStruct((9, 512), BF16),
         ],
+        compiler_params=pltpu.CompilerParams(vmem_limit_bytes=16 << 20),
         name="unpack",
-    )(own, other)
+    )(pltpu.with_memory_space_constraint(own, pltpu.VMEM), pltpu.with_memory_space_constraint(other, pltpu.VMEM))
     return expert, embed, small.T
 
 
@@ -305,14 +257,17 @@
     class_steps,
     clip_rms,
 ):
-    keep, send = pack(expert_grads, embed_grads, small_grads)
-    near = add_pair(keep, lax.ppermute(send, "c", SWAP))
-    far = add_near(exchange(near, NEAR))
-    total, line = add_far(exchange(far, ("z",)))
-    line = exchange(add_line(exchange(line, NEAR + ("c", "t"))), ("z",))
     row_float = class_steps.astype(F32)[:, None]
     corr = jnp.stack([1.0 - BETA_ONE**row_float, 1.0 - BETA_TWO**row_float])
     corr = jnp.broadcast_to(corr, (2, EMB, 128))
+    keep, send = pack(expert_grads, embed_grads, small_grads)
+    got, corr = lax.optimization_barrier((lax.ppermute(send, "c", SWAP), corr))
+    far = add_near(exchange(add_pair(keep, got), NEAR))
+    total = jnp.sum(exchange(far, ("z",)), axis=0)
+    squares = jnp.sum(total * total)
+    line = exchange(jnp.broadcast_to(squares, (A * C * T, 128)), NEAR + ("c", "t"))
+    line = jnp.broadcast_to(jnp.sum(line, axis=0), (ZH, 128))
+    line = exchange(line, ("z",))
     states = (
         expert_master,
         expert_first,

time: 153 us -> 136 us (0.89)
  Pallas kernels: 20.2 us -> 5.37 us
  starting transfers between devices: 29.1 us -> 22.1 us
  waiting for transfers between devices: 23.9 us -> 29.8 us
  other arithmetic: 0.01 us -> 2.2 us
  local copies, waits for them, and re-layouts: 3.67 us -> 1.73 us
    pallas_call x6 -> x2, Pallas kernels: 15.7 us -> 2.5 us  [the longest x1 1.81 us: unpack(): pl.pallas_call(unpack_kernel, grid=(Y,), in_specs=[VMEM, VMEM], out_specs...]
    all_to_all x2, starting transfers between devices: 13.9 us -> 6.86 us  [exchange(): return lax.all_to_all(x, axes, 0, 0, tiled=True)]
    all_to_all x2, waiting for transfers between devices: 18.2 us -> 24.4 us  [exchange(): return lax.all_to_all(x, axes, 0, 0, tiled=True)]
    unnamed x12 -> x20, local copies, waits for them, and re-layouts: 2.85 us -> 0.06 us
    pallas_call x1, Pallas kernels: 4.51 us -> 2.87 us  [pack(): pl.pallas_call(pack_kernel, grid=(Y,), in_specs=[pl.BlockSpec((2, 1, 2, 1...]
where the time goes in v4:
time: 136 us; the launch traced here: 135 us
  blocking collectives  72.7 us (53%)
  waiting for transfers between devices  29.8 us (22%)
  starting transfers between devices  22.1 us (16%)
  Pallas kernels  5.37 us (4%)
  other arithmetic  2.2 us (2%)
  local copies, waits for them, and re-layouts  1.73 us (1%)
  between operations  1.57 us (1%)
    all_to_all x4, blocking collectives, exchange(): return lax.all_to_all(x, axes, 0, 0, tiled=True)  72.7 us
    all_to_all x2, waiting for transfers between devices, exchange(): return lax.all_to_all(x, axes, 0, 0, tiled=True)  24.4 us
    ppermute x1, starting transfers between devices, body(): got, corr = lax.optimization_barrier((lax.ppermute(send, 'c', SWAP), corr))  8.8 us
    all_to_all x2, starting transfers between devices, exchange(): return lax.all_to_all(x, axes, 0, 0, tiled=True)  6.86 us
    ppermute x1, starting transfers between devices, body(): expert_w, embed_w, small_w = unpack(own, lax.ppermute(own, 'c', SWAP))  6.45 us
    ppermute x1, waiting for transfers between devices, body(): got, corr = lax.optimization_barrier((lax.ppermute(send, 'c', SWAP), corr))  3.35 us
    pallas_call x1, Pallas kernels, pack(): pl.pallas_call(pack_kernel, grid=(Y,), in_specs=[pl.BlockSpec((2, 1, 2, 1...  2.87 us
  transfers between devices with their start and end apart: 4, of which 4 were waited for; matrix products, arithmetic and copies ran while one was open for 0% of the time, Pallas kernels for 0%

profile of v4, /device:TPU:1, one launch (start us, length us, event | category | flops | bytes accessed | tf_op | source)
XLA Modules:
  0.0 135.4 jit_solution(13412833088157480802)
XLA Ops:
  0.7 2.9 %pack.1 = (f32[4,2,8,56,128]{4,3,2,1,0:T(8,128)S(1)}, f32[4,2,8,56,128]{4,3,2,1,0:T(8,128)S(1)}) custom-call(bf16[2,1,2,512,256]{4,3,2,1,0:T(8,128)(2,1)} %expert_ref.1, bf16[2,1,4096,128]{3,2,1,0:T(8,128)(2,1)} %embed_ref.1, bf16[9,2,512]{2,1,0:T(2,128)(2,1)} %bitcast.20), custom_call_target="tpu_custom_call" | custom-call | tf_op jit(solution)/shard_map/pack/pallas_call | solution.py:87
  3.5 8.8 %collective-permute-start = (f32[4,2,8,56,128]{4,3,2,1,0:T(8,128)S(1)}, f32[4,2,8,56,128]{4,3,2,1,0:T(8,128)S(1)}, u32[]{:S(2)}, u32[]{:S(2)}) collective-permute-start(f32[4,2,8,56,128]{4,3,2,1,0:T(8,128)S(1)} %get-tuple-element.34), channel_id=1, source_target_pairs={{0,4},{4,0},{1,5},{5,1},{2,6},{6,2},{3,7},{7,3},{8,12},{12,8},{9,1... | collective-permute-start | bytes 5505032 | tf_op jit(solution)/shard_map/ppermute | solution.py:264
  12.4 3.4 %collective-permute-done = f32[4,2,8,56,128]{4,3,2,1,0:T(8,128)S(1)} collective-permute-done((f32[4,2,8,56,128]{4,3,2,1,0:T(8,128)S(1)}, f32[4,2,8,56,128]{4,3,2,1,0:T(8,128)S(1)}, u32[]{:S(2)}, u32[]{:S(2)}) %collective-permute-start) | collective-permute-done | bytes 1835040 | tf_op jit(solution)/shard_map/ppermute | solution.py:264
  15.7 0.1 broadcast_in_dim.24.corr_ref
  15.8 0.2 add.6
  16.1 0.1 slice.35
  16.2 1.1 pad_maximum_fusion
  17.3 3.6 %all-to-all-start = ((bf16[8,8,56,128]{3,2,1,0:T(8,128)(2,1)}), bf16[8,8,56,128]{3,2,1,0:T(8,128)(2,1)S(1)}, u32[]{:S(2)}, u32[]{:S(2)}) async-start(bf16[8,8,56,128]{3,2,1,0:T(8,128)(2,1)} %pad_maximum_fusion), calls=%async_computation | async-start | bytes 1835008 | tf_op jit(solution)/shard_map/all_to_all | solution.py:241
  20.8 0.0 copy-start
  20.8 0.0 copy-start.1
  20.9 0.0 copy-start.3
  20.9 0.0 copy-start.4
  20.9 0.0 copy-start.6
  20.9 0.0 copy-start.7
  20.9 0.1 pad.2.clone
  21.0 13.8 %all-to-all-done = bf16[8,8,56,128]{3,2,1,0:T(8,128)(2,1)S(1)} async-done(((bf16[8,8,56,128]{3,2,1,0:T(8,128)(2,1)}), bf16[8,8,56,128]{3,2,1,0:T(8,128)(2,1)S(1)}, u32[]{:S(2)}, u32[]{:S(2)}) %all-to-all-start) | async-done | bytes 917536 | tf_op jit(solution)/shard_map/all_to_all | solution.py:241
  34.9 0.1 convert_reduce_fusion
  35.0 0.1 maximum_maximum_fusion
  35.1 26.8 %all_to_all.34 = f32[8,56,128]{2,1,0:T(8,128)S(1)} all-to-all(f32[8,56,128]{2,1,0:T(8,128)S(1)} %maximum_maximum_fusion), channel_id=1, replica_groups=mesh['y'=4,'z'=8,'w'=2,'c'=2,'t'=4] {'z'}, dimensions={0} | all-to-all | bytes 458752 | tf_op jit(solution)/shard_map/all_to_all | solution.py:241
  61.9 0.6 multiply_reduce_fusion
  62.6 0.7 broadcast_in_dim.26
  63.2 17.5 %all_to_all.35 = f32[64,1,128]{2,1,0:T(1,128)S(1)} all-to-all(f32[64,1,128]{2,1,0:T(1,128)S(1)} %broadcast_in_dim.26), channel_id=1, replica_groups=mesh['y'=4,'z'=8,'w'=2,'c'=2,'t'=4] {'y','w','c','t'}, dimensions={0} | all-to-all | bytes 65536 | tf_op jit(solution)/shard_map/all_to_all | solution.py:241
  80.7 0.6 broadcast_in_dim.27
  81.3 3.3 %all-to-all-start.3 = ((f32[8,1,128]{2,1,0:T(1,128)}), f32[8,1,128]{2,1,0:T(1,128)S(1)}, u32[]{:S(2)}, u32[]{:S(2)}) async-start(f32[8,1,128]{2,1,0:T(1,128)} %broadcast_in_dim.27), calls=%async_computation.3 | async-start | bytes 8192 | tf_op jit(solution)/shard_map/all_to_all | solution.py:241
  85.3 10.5 %all-to-all-done.3 = f32[8,1,128]{2,1,0:T(1,128)S(1)} async-done(((f32[8,1,128]{2,1,0:T(1,128)}), f32[8,1,128]{2,1,0:T(1,128)S(1)}, u32[]{:S(2)}, u32[]{:S(2)}) %all-to-all-start.3) | async-done | bytes 4128 | tf_op jit(solution)/shard_map/all_to_all | solution.py:241
  95.9 0.7 adam.1
  96.6 15.0 %all_to_all.36 = bf16[8,56,128]{2,1,0:T(8,128)(2,1)S(1)} all-to-all(bf16[8,56,128]{2,1,0:T(8,128)(2,1)S(1)} %get-tuple-element.37), channel_id=1, replica_groups=mesh['y'=4,'z'=8,'w'=2,'c'=2,'t'=4] {'z'}, dimensions={0} | all-to-all | bytes 229376 | tf_op jit(solution)/shard_map/all_to_all | solution.py:241
  111.6 0.1 broadcast_in_dim.28
  111.7 13.4 %all_to_all.37.own_ref = bf16[8,8,56,128]{3,2,1,0:T(8,128)(2,1)S(1)} all-to-all(bf16[8,8,56,128]{3,2,1,0:T(8,128)(2,1)S(1)} %broadcast_in_dim.28), channel_id=1, replica_groups=mesh['y'=4,'z'=8,'w'=2,'c'=2,'t'=4] {'y','w'}, dimensions={0} | all-to-all | bytes 1835008 | tf_op jit(solution)/shard_map/all_to_all | solution.py:241
  125.1 6.4 %collective-permute-start.1 = (bf16[8,8,56,128]{3,2,1,0:T(8,128)(2,1)S(1)}, bf16[8,8,56,128]{3,2,1,0:T(8,128)(2,1)S(1)}, u32[]{:S(2)}, u32[]{:S(2)}) collective-permute-start(bf16[8,8,56,128]{3,2,1,0:T(8,128)(2,1)S(1)} %all_to_all.37.own_ref), channel_id=1, source_target_pairs={{0,4},{4,0},{1,5},{5,1},{2,6},{6,2},{3,7},{7,3},{8,12},{12,8},{9,1... | collective-permute-start | bytes 2752520 | tf_op jit(solution)/shard_map/ppermute | solution.py:285
  131.6 2.1 %collective-permute-done.1.other_ref = bf16[8,8,56,128]{3,2,1,0:T(8,128)(2,1)S(1)} collective-permute-done((bf16[8,8,56,128]{3,2,1,0:T(8,128)(2,1)S(1)}, bf16[8,8,56,128]{3,2,1,0:T(8,128)(2,1)S(1)}, u32[]{:S(2)}, u32[]{:S(2)}) %collective-permute-start.1) | collective-permute-done | bytes 917536 | tf_op jit(solution)/shard_map/ppermute | solution.py:285
  133.6 1.8 %unpack.1 = (bf16[2,512,256]{2,1,0:T(8,128)(2,1)}, bf16[4096,128]{1,0:T(8,128)(2,1)}, bf16[9,512]{1,0:T(8,128)(2,1)}) custom-call(bf16[8,8,56,128]{3,2,1,0:T(8,128)(2,1)S(1)} %all_to_all.37.own_ref, bf16[8,8,56,128]{3,2,1,0:T(8,128)(2,1)S(1)} %collective-permute-done.1.other_ref), custom_call_target="tpu_custom_call" | custom-call | tf_op jit(solution)/shard_map/unpack/pallas_call | solution.py:220
  (22 shorter events, 0.2 us)
Async XLA Ops:
  0.6 11.7 %copy-start.9 = (s32[32]{0:T(128)S(1)}, s32[32]{0:T(128)}, u32[]{:S(2)}) copy-start(s32[32]{0:T(128)} %param.26) | copy-start | bytes 388
  3.5 12.2 %collective-permute-start = (f32[4,2,8,56,128]{4,3,2,1,0:T(8,128)S(1)}, f32[4,2,8,56,128]{4,3,2,1,0:T(8,128)S(1)}, u32[]{:S(2)}, u32[]{:S(2)}) collective-permute-start(f32[4,2,8,56,128]{4,3,2,1,0:T(8,128)S(1)} %get-tuple-element.34), channel_id=1, source_target_pairs={{0,4},{4,0},{1,5},{5,1},{2,6},{6,2},{3,7},{7,3},{8,12},{12,8},{9,1... | collective-permute-start | bytes 5505032 | tf_op jit(solution)/shard_map/ppermute | solution.py:264
  17.3 17.6 %all-to-all-start = ((bf16[8,8,56,128]{3,2,1,0:T(8,128)(2,1)}), bf16[8,8,56,128]{3,2,1,0:T(8,128)(2,1)S(1)}, u32[]{:S(2)}, u32[]{:S(2)}) async-start(bf16[8,8,56,128]{3,2,1,0:T(8,128)(2,1)} %pad_maximum_fusion), calls=%async_computation | async-start | bytes 1835008 | tf_op jit(solution)/shard_map/all_to_all | solution.py:241
  20.8 75.0 %copy-start = (f32[32,128]{1,0:T(8,128)S(1)}, f32[32,128]{1,0:T(8,128)}, u32[]{:S(2)}) copy-start(f32[32,128]{1,0:T(8,128)} %emb_m.1) | copy-start | bytes 49156
  20.8 75.0 %copy-start.1 = (f32[32,128]{1,0:T(8,128)S(1)}, f32[32,128]{1,0:T(8,128)}, u32[]{:S(2)}) copy-start(f32[32,128]{1,0:T(8,128)} %emb_f.1) | copy-start | bytes 49156
  20.9 75.0 %copy-start.2 = (f32[32,128]{1,0:T(8,128)S(1)}, f32[32,128]{1,0:T(8,128)}, u32[]{:S(2)}) copy-start(f32[32,128]{1,0:T(8,128)} %emb_s.1) | copy-start | bytes 49156
  20.9 75.0 %copy-start.3 = (f32[2,4,256]{2,1,0:T(4,128)S(1)}, f32[2,4,256]{2,1,0:T(4,128)}, u32[]{:S(2)}) copy-start(f32[2,4,256]{2,1,0:T(4,128)} %exp_m.1) | copy-start | bytes 24580
  20.9 75.0 %copy-start.4 = (f32[2,4,256]{2,1,0:T(4,128)S(1)}, f32[2,4,256]{2,1,0:T(4,128)}, u32[]{:S(2)}) copy-start(f32[2,4,256]{2,1,0:T(4,128)} %exp_f.1) | copy-start | bytes 24580
  20.9 75.0 %copy-start.5 = (f32[2,4,256]{2,1,0:T(4,128)S(1)}, f32[2,4,256]{2,1,0:T(4,128)}, u32[]{:S(2)}) copy-start(f32[2,4,256]{2,1,0:T(4,128)} %exp_s.1) | copy-start | bytes 24580
  20.9 75.0 %copy-start.6 = (f32[4,9]{1,0:T(4,128)S(1)}, f32[4,9]{1,0:T(4,128)}, u32[]{:S(2)}) copy-start(f32[4,9]{1,0:T(4,128)} %sma_m.1) | copy-start | bytes 436
  20.9 74.9 %copy-start.7 = (f32[4,9]{1,0:T(4,128)S(1)}, f32[4,9]{1,0:T(4,128)}, u32[]{:S(2)}) copy-start(f32[4,9]{1,0:T(4,128)} %sma_f.1) | copy-start | bytes 436
  20.9 74.9 %copy-start.8 = (f32[4,9]{1,0:T(4,128)S(1)}, f32[4,9]{1,0:T(4,128)}, u32[]{:S(2)}) copy-start(f32[4,9]{1,0:T(4,128)} %sma_s.1) | copy-start | bytes 436
  81.3 14.5 %all-to-all-start.3 = ((f32[8,1,128]{2,1,0:T(1,128)}), f32[8,1,128]{2,1,0:T(1,128)S(1)}, u32[]{:S(2)}, u32[]{:S(2)}) async-start(f32[8,1,128]{2,1,0:T(1,128)} %broadcast_in_dim.27), calls=%async_computation.3 | async-start | bytes 8192 | tf_op jit(solution)/shard_map/all_to_all | solution.py:241
  125.1 8.5 %collective-permute-start.1 = (bf16[8,8,56,128]{3,2,1,0:T(8,128)(2,1)S(1)}, bf16[8,8,56,128]{3,2,1,0:T(8,128)(2,1)S(1)}, u32[]{:S(2)}, u32[]{:S(2)}) collective-permute-start(bf16[8,8,56,128]{3,2,1,0:T(8,128)(2,1)S(1)} %all_to_all.37.own_ref), channel_id=1, source_target_pairs={{0,4},{4,0},{1,5},{5,1},{2,6},{6,2},{3,7},{7,3},{8,12},{12,8},{9,1... | collective-permute-start | bytes 2752520 | tf_op jit(solution)/shard_map/ppermute | solution.py:285

commit v5 on v4

--- a/solution.py
+++ b/solution.py
@@ -99,18 +99,37 @@
     )(in_hbm(expert_grads), in_hbm(embed_grads), in_hbm(small_grads[:, 0].transpose(2, 0, 1)))
 
 
-def add_pair(keep, got):
-    part = (keep + got).reshape(A, ZH, ROWS, 128)
-    small = part[:, :, SMA : SMA + 4]
+def terms(part):
+    main, small = part[..., :SMA, :], part[..., SMA : SMA + 4, :]
     high = lax.reduce_precision(small, 8, 7)
-    terms = [part[:, :, :SMA], high, small - high]
-    return jnp.concatenate([x.astype(BF16) for x in terms], axis=2)
+    return jnp.concatenate([x.astype(BF16) for x in (main, high, small - high)], axis=-2)
 
 
 def add_near(got):
     total = jnp.sum(got.astype(F32), axis=0)
-    small = total[:, SMA : SMA + 4] + total[:, SMA + 4 :]
-    return jnp.concatenate([total[:, :SMA], small, jnp.zeros((ZH, 4, 128), F32)], axis=1)
+    return terms(jnp.concatenate([total[:, :SMA], total[:, SMA : SMA + 4] + total[:, SMA + 4 :]], axis=1))
+
+
+def far_kernel(got_ref, total_ref, line_ref):
+    total = got_ref[0].astype(F32)
+    for k in range(1, ZH):
+        total = total + got_ref[k].astype(F32)
+    small = total[SMA:] + flip(total[SMA:])
+    total_ref[:SMA] = total[:SMA]
+    total_ref[SMA:] = small
+    squares = jnp.sum(total[:SMA] * total[:SMA]) + 0.5 * jnp.sum(small * small)
+    line_ref[...] = jnp.full(line_ref.shape, squares, F32)
+
+
+def add_far(got):
+    return pl.pallas_call(
+        far_kernel,
+        in_specs=[VMEM],
+        out_specs=[VMEM, VMEM],
+        out_shape=[pltpu.VMEM((ROWS, 128), F32), pltpu.VMEM((A * C * T, 128), F32)],
+        compiler_params=pltpu.CompilerParams(vmem_limit_bytes=16 << 20),
+        name="add_far",
+    )(pltpu.with_memory_space_constraint(got, pltpu.VMEM))
 
 
 def update(scaled, first, second, master, corr_one, corr_two):
@@ -262,12 +281,11 @@
     corr = jnp.broadcast_to(corr, (2, EMB, 128))
     keep, send = pack(expert_grads, embed_grads, small_grads)
     got, corr = lax.optimization_barrier((lax.ppermute(send, "c", SWAP), corr))
-    far = add_near(exchange(add_pair(keep, got), NEAR))
-    total = jnp.sum(exchange(far, ("z",)), axis=0)
-    squares = jnp.sum(total * total)
-    line = exchange(jnp.broadcast_to(squares, (A * C * T, 128)), NEAR + ("c", "t"))
-    line = jnp.broadcast_to(jnp.sum(line, axis=0), (ZH, 128))
-    line = exchange(line, ("z",))
+    near = terms((keep + got).reshape(A, ZH, ROWS, 128))
+    far = add_near(exchange(near, NEAR))
+    total, line = add_far(exchange(far, ("z",)))
+    line = jnp.sum(exchange(line, NEAR + ("c", "t")), axis=0)
+    line = exchange(jnp.broadcast_to(line, (ZH, 128)), ("z",))
     states = (
         expert_master,
         expert_first,

time: 136 us -> 130 us (0.956)
  waiting for transfers between devices: 29.8 us -> 16 us
  blocking collectives: 72.7 us -> 85.8 us
  starting transfers between devices: 22.1 us -> 18.6 us
  other arithmetic: 2.2 us -> 0.65 us
    all_to_all x2 -> x1, waiting for transfers between devices: 24.4 us -> 10.5 us  [exchange(): return lax.all_to_all(x, axes, 0, 0, tiled=True)]
    all_to_all x4 -> x5, blocking collectives: 72.7 us -> 85.8 us  [exchange(): return lax.all_to_all(x, axes, 0, 0, tiled=True)]
    all_to_all x2 -> x1, starting transfers between devices: 6.86 us -> 3.31 us  [exchange(): return lax.all_to_all(x, axes, 0, 0, tiled=True)]
  transfers between devices with their start and end apart: 4 -> 3, of which waited for: 4 -> 3; matrix products, arithmetic and copies ran while one was open for 0% -> 0% of each run, Pallas kernels for 0% -> 0%
where the time goes in v5:
time: 130 us; the launch traced here: 129 us
  blocking collectives  85.8 us (66%)
  starting transfers between devices  18.6 us (14%)
  waiting for transfers between devices  16 us (12%)
  Pallas kernels  5.51 us (4%)
  between operations  1.55 us (1%)
    all_to_all x5, blocking collectives, exchange(): return lax.all_to_all(x, axes, 0, 0, tiled=True)  85.8 us
    all_to_all x1, waiting for transfers between devices, exchange(): return lax.all_to_all(x, axes, 0, 0, tiled=True)  10.5 us
    ppermute x1, starting transfers between devices, body(): got, corr = lax.optimization_barrier((lax.ppermute(send, 'c', SWAP), corr))  8.8 us
    ppermute x1, starting transfers between devices, body(): expert_w, embed_w, small_w = unpack(own, lax.ppermute(own, 'c', SWAP))  6.45 us
    ppermute x1, waiting for transfers between devices, body(): got, corr = lax.optimization_barrier((lax.ppermute(send, 'c', SWAP), corr))  3.35 us
    all_to_all x1, starting transfers between devices, exchange(): return lax.all_to_all(x, axes, 0, 0, tiled=True)  3.31 us
    pallas_call x1, Pallas kernels, pack(): pl.pallas_call(pack_kernel, grid=(Y,), in_specs=[pl.BlockSpec((2, 1, 2, 1...  2.87 us
  transfers between devices with their start and end apart: 3, of which 3 were waited for; matrix products, arithmetic and copies ran while one was open for 0% of the time, Pallas kernels for 0%

profile of v5, /device:TPU:1, one launch (start us, length us, event | category | flops | bytes accessed | tf_op | source)
XLA Modules:
  0.0 129.0 jit_solution(6158707489158348027)
XLA Ops:
  0.7 2.9 %pack.1 = (f32[4,2,8,56,128]{4,3,2,1,0:T(8,128)S(1)}, f32[4,2,8,56,128]{4,3,2,1,0:T(8,128)S(1)}) custom-call(bf16[2,1,2,512,256]{4,3,2,1,0:T(8,128)(2,1)} %expert_ref.1, bf16[2,1,4096,128]{3,2,1,0:T(8,128)(2,1)} %embed_ref.1, bf16[9,2,512]{2,1,0:T(2,128)(2,1)} %bitcast.22), custom_call_target="tpu_custom_call" | custom-call | tf_op jit(solution)/shard_map/pack/pallas_call | solution.py:87
  3.5 8.8 %collective-permute-start = (f32[4,2,8,56,128]{4,3,2,1,0:T(8,128)S(1)}, f32[4,2,8,56,128]{4,3,2,1,0:T(8,128)S(1)}, u32[]{:S(2)}, u32[]{:S(2)}) collective-permute-start(f32[4,2,8,56,128]{4,3,2,1,0:T(8,128)S(1)} %get-tuple-element.36), channel_id=1, source_target_pairs={{0,4},{4,0},{1,5},{5,1},{2,6},{6,2},{3,7},{7,3},{8,12},{12,8},{9,1... | collective-permute-start | bytes 5505032 | tf_op jit(solution)/shard_map/ppermute | solution.py:283
  12.4 3.4 %collective-permute-done = f32[4,2,8,56,128]{4,3,2,1,0:T(8,128)S(1)} collective-permute-done((f32[4,2,8,56,128]{4,3,2,1,0:T(8,128)S(1)}, f32[4,2,8,56,128]{4,3,2,1,0:T(8,128)S(1)}, u32[]{:S(2)}, u32[]{:S(2)}) %collective-permute-start) | collective-permute-done | bytes 1835040 | tf_op jit(solution)/shard_map/ppermute | solution.py:283
  15.7 0.1 broadcast_in_dim.18.corr_ref
  15.8 0.2 add.6
  16.1 0.1 slice.45
  16.2 0.2 pad_maximum_fusion
  16.3 0.0 copy-start
  16.4 0.0 copy-start.1
  16.4 0.0 copy-start.2
  16.4 0.0 copy-start.3
  16.4 0.0 copy-start.4
  16.4 0.0 copy-start.5
  16.4 0.0 copy-start.6
  16.4 0.0 copy-start.7
  16.4 0.0 copy-start.8
  16.5 16.6 %all_to_all.37 = bf16[8,8,56,128]{3,2,1,0:T(8,128)(2,1)S(1)} all-to-all(bf16[8,8,56,128]{3,2,1,0:T(8,128)(2,1)S(1)} %pad_maximum_fusion), channel_id=1, replica_groups=mesh['y'=4,'z'=8,'w'=2,'c'=2,'t'=4] {'y','w'}, dimensions={0} | all-to-all | bytes 1835008 | tf_op jit(solution)/shard_map/all_to_all | solution.py:260
  33.0 0.1 convert_reduce_fusion
  33.2 24.3 %all_to_all.38.got_ref = bf16[8,56,128]{2,1,0:T(8,128)(2,1)S(1)} all-to-all(bf16[8,56,128]{2,1,0:T(8,128)(2,1)S(1)} %pad_maximum_fusion.1), channel_id=1, replica_groups=mesh['y'=4,'z'=8,'w'=2,'c'=2,'t'=4] {'z'}, dimensions={0} | all-to-all | bytes 229376 | tf_op jit(solution)/shard_map/all_to_all | solution.py:260
  57.5 0.1 add_far.1
  57.7 16.5 %all_to_all.39 = f32[64,1,128]{2,1,0:T(1,128)S(1)} all-to-all(f32[64,1,128]{2,1,0:T(1,128)S(1)} %bitcast.18), channel_id=1, replica_groups=mesh['y'=4,'z'=8,'w'=2,'c'=2,'t'=4] {'y','w','c','t'}, dimensions={0} | all-to-all | bytes 65536 | tf_op jit(solution)/shard_map/all_to_all | solution.py:260
  74.2 0.1 reduce_sum.19
  74.3 0.6 broadcast_in_dim.19
  74.9 3.3 %all-to-all-start.3 = ((f32[8,1,128]{2,1,0:T(1,128)}), f32[8,1,128]{2,1,0:T(1,128)S(1)}, u32[]{:S(2)}, u32[]{:S(2)}) async-start(f32[8,1,128]{2,1,0:T(1,128)} %broadcast_in_dim.19), calls=%async_computation.3 | async-start | bytes 8192 | tf_op jit(solution)/shard_map/all_to_all | solution.py:260
  78.9 10.5 %all-to-all-done.3 = f32[8,1,128]{2,1,0:T(1,128)S(1)} async-done(((f32[8,1,128]{2,1,0:T(1,128)}), f32[8,1,128]{2,1,0:T(1,128)S(1)}, u32[]{:S(2)}, u32[]{:S(2)}) %all-to-all-start.3) | async-done | bytes 4128 | tf_op jit(solution)/shard_map/all_to_all | solution.py:260
  89.5 0.7 adam.1
  90.2 15.0 %all_to_all.40 = bf16[8,56,128]{2,1,0:T(8,128)(2,1)S(1)} all-to-all(bf16[8,56,128]{2,1,0:T(8,128)(2,1)S(1)} %get-tuple-element.41), channel_id=1, replica_groups=mesh['y'=4,'z'=8,'w'=2,'c'=2,'t'=4] {'z'}, dimensions={0} | all-to-all | bytes 229376 | tf_op jit(solution)/shard_map/all_to_all | solution.py:260
  105.2 0.1 broadcast_in_dim.20
  105.3 13.4 %all_to_all.41.own_ref = bf16[8,8,56,128]{3,2,1,0:T(8,128)(2,1)S(1)} all-to-all(bf16[8,8,56,128]{3,2,1,0:T(8,128)(2,1)S(1)} %broadcast_in_dim.20), channel_id=1, replica_groups=mesh['y'=4,'z'=8,'w'=2,'c'=2,'t'=4] {'y','w'}, dimensions={0} | all-to-all | bytes 1835008 | tf_op jit(solution)/shard_map/all_to_all | solution.py:260
  118.7 6.4 %collective-permute-start.1 = (bf16[8,8,56,128]{3,2,1,0:T(8,128)(2,1)S(1)}, bf16[8,8,56,128]{3,2,1,0:T(8,128)(2,1)S(1)}, u32[]{:S(2)}, u32[]{:S(2)}) collective-permute-start(bf16[8,8,56,128]{3,2,1,0:T(8,128)(2,1)S(1)} %all_to_all.41.own_ref), channel_id=1, source_target_pairs={{0,4},{4,0},{1,5},{5,1},{2,6},{6,2},{3,7},{7,3},{8,12},{12,8},{9,1... | collective-permute-start | bytes 2752520 | tf_op jit(solution)/shard_map/ppermute | solution.py:303
  125.2 2.1 %collective-permute-done.1.other_ref = bf16[8,8,56,128]{3,2,1,0:T(8,128)(2,1)S(1)} collective-permute-done((bf16[8,8,56,128]{3,2,1,0:T(8,128)(2,1)S(1)}, bf16[8,8,56,128]{3,2,1,0:T(8,128)(2,1)S(1)}, u32[]{:S(2)}, u32[]{:S(2)}) %collective-permute-start.1) | collective-permute-done | bytes 917536 | tf_op jit(solution)/shard_map/ppermute | solution.py:303
  127.2 1.8 %unpack.1 = (bf16[2,512,256]{2,1,0:T(8,128)(2,1)}, bf16[4096,128]{1,0:T(8,128)(2,1)}, bf16[9,512]{1,0:T(8,128)(2,1)}) custom-call(bf16[8,8,56,128]{3,2,1,0:T(8,128)(2,1)S(1)} %all_to_all.41.own_ref, bf16[8,8,56,128]{3,2,1,0:T(8,128)(2,1)S(1)} %collective-permute-done.1.other_ref), custom_call_target="tpu_custom_call" | custom-call | tf_op jit(solution)/shard_map/unpack/pallas_call | solution.py:239
  (17 shorter events, 0.1 us)
Async XLA Ops:
  0.6 11.7 %copy-start.9 = (s32[32]{0:T(128)S(1)}, s32[32]{0:T(128)}, u32[]{:S(2)}) copy-start(s32[32]{0:T(128)} %param.26) | copy-start | bytes 388
  3.5 12.2 %collective-permute-start = (f32[4,2,8,56,128]{4,3,2,1,0:T(8,128)S(1)}, f32[4,2,8,56,128]{4,3,2,1,0:T(8,128)S(1)}, u32[]{:S(2)}, u32[]{:S(2)}) collective-permute-start(f32[4,2,8,56,128]{4,3,2,1,0:T(8,128)S(1)} %get-tuple-element.36), channel_id=1, source_target_pairs={{0,4},{4,0},{1,5},{5,1},{2,6},{6,2},{3,7},{7,3},{8,12},{12,8},{9,1... | collective-permute-start | bytes 5505032 | tf_op jit(solution)/shard_map/ppermute | solution.py:283
  16.3 73.1 %copy-start = (f32[32,128]{1,0:T(8,128)S(1)}, f32[32,128]{1,0:T(8,128)}, u32[]{:S(2)}) copy-start(f32[32,128]{1,0:T(8,128)} %emb_m.1) | copy-start | bytes 49156
  16.4 73.0 %copy-start.1 = (f32[32,128]{1,0:T(8,128)S(1)}, f32[32,128]{1,0:T(8,128)}, u32[]{:S(2)}) copy-start(f32[32,128]{1,0:T(8,128)} %emb_f.1) | copy-start | bytes 49156
  16.4 73.0 %copy-start.2 = (f32[32,128]{1,0:T(8,128)S(1)}, f32[32,128]{1,0:T(8,128)}, u32[]{:S(2)}) copy-start(f32[32,128]{1,0:T(8,128)} %emb_s.1) | copy-start | bytes 49156
  16.4 73.0 %copy-start.3 = (f32[2,4,256]{2,1,0:T(4,128)S(1)}, f32[2,4,256]{2,1,0:T(4,128)}, u32[]{:S(2)}) copy-start(f32[2,4,256]{2,1,0:T(4,128)} %exp_m.1) | copy-start | bytes 24580
  16.4 73.0 %copy-start.4 = (f32[2,4,256]{2,1,0:T(4,128)S(1)}, f32[2,4,256]{2,1,0:T(4,128)}, u32[]{:S(2)}) copy-start(f32[2,4,256]{2,1,0:T(4,128)} %exp_f.1) | copy-start | bytes 24580
  16.4 73.0 %copy-start.5 = (f32[2,4,256]{2,1,0:T(4,128)S(1)}, f32[2,4,256]{2,1,0:T(4,128)}, u32[]{:S(2)}) copy-start(f32[2,4,256]{2,1,0:T(4,128)} %exp_s.1) | copy-start | bytes 24580
  16.4 73.0 %copy-start.6 = (f32[4,9]{1,0:T(4,128)S(1)}, f32[4,9]{1,0:T(4,128)}, u32[]{:S(2)}) copy-start(f32[4,9]{1,0:T(4,128)} %sma_m.1) | copy-start | bytes 436
  16.4 73.0 %copy-start.7 = (f32[4,9]{1,0:T(4,128)S(1)}, f32[4,9]{1,0:T(4,128)}, u32[]{:S(2)}) copy-start(f32[4,9]{1,0:T(4,128)} %sma_f.1) | copy-start | bytes 436
  16.4 73.0 %copy-start.8 = (f32[4,9]{1,0:T(4,128)S(1)}, f32[4,9]{1,0:T(4,128)}, u32[]{:S(2)}) copy-start(f32[4,9]{1,0:T(4,128)} %sma_s.1) | copy-start | bytes 436
  74.9 14.5 %all-to-all-start.3 = ((f32[8,1,128]{2,1,0:T(1,128)}), f32[8,1,128]{2,1,0:T(1,128)S(1)}, u32[]{:S(2)}, u32[]{:S(2)}) async-start(f32[8,1,128]{2,1,0:T(1,128)} %broadcast_in_dim.19), calls=%async_computation.3 | async-start | bytes 8192 | tf_op jit(solution)/shard_map/all_to_all | solution.py:260
  118.7 8.5 %collective-permute-start.1 = (bf16[8,8,56,128]{3,2,1,0:T(8,128)(2,1)S(1)}, bf16[8,8,56,128]{3,2,1,0:T(8,128)(2,1)S(1)}, u32[]{:S(2)}, u32[]{:S(2)}) collective-permute-start(bf16[8,8,56,128]{3,2,1,0:T(8,128)(2,1)S(1)} %all_to_all.41.own_ref), channel_id=1, source_target_pairs={{0,4},{4,0},{1,5},{5,1},{2,6},{6,2},{3,7},{7,3},{8,12},{12,8},{9,1... | collective-permute-start | bytes 2752520 | tf_op jit(solution)/shard_map/ppermute | solution.py:303

commit v6 on v5

--- a/solution.py
+++ b/solution.py
@@ -28,6 +28,10 @@
     return pltpu.with_memory_space_constraint(x, pltpu.HBM)
 
 
+def in_vmem(x):
+    return pltpu.with_memory_space_constraint(x, pltpu.VMEM)
+
+
 def low_rows(shape):
     return lax.broadcasted_iota(jnp.int32, shape, len(shape) - 2) < 4
 
@@ -36,39 +40,58 @@
     return pltpu.roll(x, 4, x.ndim - 2)
 
 
-def pack_kernel(expert_ref, embed_ref, small_ref, keep_ref, send_ref):
-    @pl.when(lax.axis_index("c") == 0)
-    def _():
-        pack_rows(expert_ref, embed_ref, small_ref, (keep_ref, send_ref))
-
-    @pl.when(lax.axis_index("c") == 1)
-    def _():
-        pack_rows(expert_ref, embed_ref, small_ref, (send_ref, keep_ref))
-
-
-def pack_rows(expert_ref, embed_ref, small_ref, outs):
-    y = pl.program_id(0)
-
+def two_terms(x):
+    high = x.astype(BF16).astype(F32)
+    return jnp.where(low_rows(x.shape), high, flip(x - high))
+
+
+def pack_kernel(expert_hbm, embed_hbm, small_hbm, keep_ref, send_ref, expert, embed, small, sems):
+    def copies(y):
+        rows = embed_hbm.at[:, 0, pl.ds(y * 1024, 1024)]
+        tiles = expert_hbm.at[:, 0, :, pl.ds(y * 128, 128)]
+        lanes = small_hbm.at[:, :, pl.ds(y * 128, 128)]
+        return [
+            pltpu.make_async_copy(rows, embed.at[y], sems.at[0, y]),
+            pltpu.make_async_copy(tiles, expert.at[y], sems.at[1, y]),
+            pltpu.make_async_copy(lanes, small.at[y], sems.at[2, y]),
+        ]
+
+    for y in range(Y):
+        for copy in copies(y):
+            copy.start()
+
+    @pl.loop(0, Y)
+    def _(y):
+        for copy in copies(y):
+            copy.wait()
+        for core in range(C):
+
+            @pl.when(lax.axis_index("c") == core)
+            def _():
+                pack_rows(core, y, expert, embed, small, keep_ref, send_ref)
+
+
+def pack_rows(core, y, expert_ref, embed_ref, small_ref, keep_ref, send_ref):
     def put(index, rows, *values):
-        for ref, value in zip(outs, values):
-            ref[index + rows] = value
-
-    small = small_ref[:, 0, :].astype(F32) + small_ref[:, 1, :].astype(F32)
+        keep_ref[index + rows] = values[core]
+        send_ref[index + rows] = values[1 - core].astype(BF16)
+
+    small = small_ref[y, :, 0, :].astype(F32) + small_ref[y, :, 1, :].astype(F32)
     small = jnp.concatenate([small, jnp.zeros((128 - 9, 128), F32)], axis=0).T
     for z in range(ZH):
         for w in range(W):
-            index = (y, w, z)
+            index = (y * W + w, z)
             base = (z * W + w) * C * EMB
             pair = [
-                embed_ref[0, 0, pl.ds(base + c * EMB, EMB), :].astype(F32)
-                + embed_ref[1, 0, pl.ds(base + c * EMB, EMB), :].astype(F32)
+                embed_ref[y, 0, pl.ds(base + c * EMB, EMB), :].astype(F32)
+                + embed_ref[y, 1, pl.ds(base + c * EMB, EMB), :].astype(F32)
                 for c in range(C)
             ]
             put(index, (slice(0, EMB),), *pair)
             row = (z * W + w) * 8
             for m in range(2):
-                tile = expert_ref[0, 0, m, pl.ds(row, 8), :].astype(F32) + expert_ref[
-                    1, 0, m, pl.ds(row, 8), :
+                tile = expert_ref[y, 0, m, pl.ds(row, 8), :].astype(F32) + expert_ref[
+                    y, 1, m, pl.ds(row, 8), :
                 ].astype(F32)
                 left, right = tile[:, :128], tile[:, 128:]
                 upper = low_rows((8, 128))
@@ -78,36 +101,61 @@
                     jnp.where(upper, left, flip(right)),
                     jnp.where(upper, flip(left), right),
                 )
-            tile = small[row : row + 8]
-            put(index, (slice(SMA, ROWS),), tile, flip(tile))
+            pair = [small[row : row + 8], flip(small[row : row + 8])]
+            pair[1 - core] = two_terms(pair[1 - core])
+            put(index, (slice(SMA, ROWS),), *pair)
 
 
 def pack(expert_grads, embed_grads, small_grads):
-    out = pltpu.VMEM((Y, W, ZH, ROWS, 128), F32)
+    shape = (A, ZH, ROWS, 128)
     return pl.pallas_call(
         pack_kernel,
-        grid=(Y,),
-        in_specs=[
-            pl.BlockSpec((2, 1, 2, 128, 256), lambda y: (0, 0, 0, y, 0)),
-            pl.BlockSpec((2, 1, 1024, 128), lambda y: (0, 0, y, 0)),
-            pl.BlockSpec((9, 2, 128), lambda y: (0, 0, y)),
+        in_specs=[pl.BlockSpec(memory_space=pltpu.HBM)] * 3,
+        out_specs=[VMEM, VMEM],
+        out_shape=[pltpu.VMEM(shape, F32), pltpu.VMEM(shape, BF16)],
+        scratch_shapes=[
+            pltpu.VMEM((Y, 2, 2, 128, 256), BF16),
+            pltpu.VMEM((Y, 2, 1024, 128), BF16),
+            pltpu.VMEM((Y, 9, 2, 128), BF16),
+            pltpu.SemaphoreType.DMA((3, Y)),
         ],
-        out_specs=[VMEM, VMEM],
-        out_shape=[out, out],
         compiler_params=pltpu.CompilerParams(vmem_limit_bytes=16 << 20),
         name="pack",
     )(in_hbm(expert_grads), in_hbm(embed_grads), in_hbm(small_grads[:, 0].transpose(2, 0, 1)))
 
 
-def terms(part):
-    main, small = part[..., :SMA, :], part[..., SMA : SMA + 4, :]
+def terms(main, small):
     high = lax.reduce_precision(small, 8, 7)
     return jnp.concatenate([x.astype(BF16) for x in (main, high, small - high)], axis=-2)
 
 
+def parts(x):
+    x = x.astype(F32)
+    return x[..., :SMA, :], x[..., SMA : SMA + 4, :] + x[..., SMA + 4 :, :]
+
+
+def pair_kernel(keep_ref, got_ref, out_ref):
+    @pl.loop(0, A)
+    def _(a):
+        out_ref[a, :, :SMA] = (keep_ref[a, :, :SMA] + got_ref[a, :, :SMA].astype(F32)).astype(BF16)
+        small = got_ref[a, :, SMA:].astype(F32)
+        small = keep_ref[a, :, SMA:] + (small + flip(small))
+        out_ref[a, :, SMA:] = two_terms(small).astype(BF16)
+
+
+def add_pair(keep, got):
+    return pl.pallas_call(
+        pair_kernel,
+        in_specs=[VMEM, VMEM],
+        out_specs=VMEM,
+        out_shape=pltpu.VMEM((A, ZH, ROWS, 128), BF16),
+        compiler_params=pltpu.CompilerParams(vmem_limit_bytes=16 << 20),
+        name="add_pair",
+    )(in_vmem(keep), in_vmem(got))
+
+
 def add_near(got):
-    total = jnp.sum(got.astype(F32), axis=0)
-    return terms(jnp.concatenate([total[:, :SMA], total[:, SMA : SMA + 4] + total[:, SMA + 4 :]], axis=1))
+    return terms(*parts(jnp.sum(got.astype(F32), axis=0)))
 
 
 def far_kernel(got_ref, total_ref, line_ref):
@@ -129,7 +177,7 @@
         out_shape=[pltpu.VMEM((ROWS, 128), F32), pltpu.VMEM((A * C * T, 128), F32)],
         compiler_params=pltpu.CompilerParams(vmem_limit_bytes=16 << 20),
         name="add_far",
-    )(pltpu.with_memory_space_constraint(got, pltpu.VMEM))
+    )(in_vmem(got))
 
 
 def update(scaled, first, second, master, corr_one, corr_two):
@@ -170,7 +218,7 @@
 ):
     fixed = (1.0 - BETA_ONE**STEP, 1.0 - BETA_TWO**STEP)
     squares = jnp.sum(line_ref[...], axis=0, keepdims=True)
-    factor = rms_ref[0, 0] * jnp.sqrt(P_TOT / squares)
+    factor = rms_ref[...] * jnp.sqrt(P_TOT / squares)
     clip_ref[...] = factor
     first, second, step, master = update(
         factor * total_ref[:EMB], emb_f[...], emb_s[...], emb_m[...], corr_ref[0], corr_ref[1]
@@ -205,7 +253,7 @@
     out[0] = pltpu.VMEM(shapes[0], BF16)
     return pl.pallas_call(
         adam_kernel,
-        in_specs=[VMEM, VMEM, pl.BlockSpec(memory_space=pltpu.SMEM)] + [VMEM] * 10,
+        in_specs=[VMEM] * 13,
         out_specs=[VMEM] * len(out),
         out_shape=out,
         compiler_params=pltpu.CompilerParams(vmem_limit_bytes=16 << 20),
@@ -214,13 +262,20 @@
 
 
 def unpack_kernel(own_ref, other_ref, expert_ref, embed_ref, small_ref):
-    first_core = lax.axis_index("c") == 0
+    for core in range(C):
+
+        @pl.when(lax.axis_index("c") == core)
+        def _():
+            pair = (own_ref, other_ref) if core == 0 else (other_ref, own_ref)
+            unpack_rows(pair, expert_ref, embed_ref, small_ref)
+
+
+def unpack_rows(refs, expert_ref, embed_ref, small_ref):
     y = pl.program_id(0)
     tiles = []
     for z in range(ZH):
         for w in range(W):
-            own, other = own_ref[y * W + w, z], other_ref[y * W + w, z]
-            pair = (jnp.where(first_core, own, other), jnp.where(first_core, other, own))
+            pair = [ref[y * W + w, z] for ref in refs]
             base = (z * W + w) * C * EMB
             for c in range(C):
                 embed_ref[pl.ds(base + c * EMB, EMB), :] = pair[c][:EMB]
@@ -252,7 +307,7 @@
         ],
         compiler_params=pltpu.CompilerParams(vmem_limit_bytes=16 << 20),
         name="unpack",
-    )(pltpu.with_memory_space_constraint(own, pltpu.VMEM), pltpu.with_memory_space_constraint(other, pltpu.VMEM))
+    )(in_vmem(own), in_vmem(other))
     return expert, embed, small.T
 
 
@@ -280,9 +335,9 @@
     corr = jnp.stack([1.0 - BETA_ONE**row_float, 1.0 - BETA_TWO**row_float])
     corr = jnp.broadcast_to(corr, (2, EMB, 128))
     keep, send = pack(expert_grads, embed_grads, small_grads)
-    got, corr = lax.optimization_barrier((lax.ppermute(send, "c", SWAP), corr))
-    near = terms((keep + got).reshape(A, ZH, ROWS, 128))
-    far = add_near(exchange(near, NEAR))
+    rms = jnp.broadcast_to(clip_rms, (1, 128))
+    got, corr, rms = lax.optimization_barrier((lax.ppermute(send, "c", SWAP), corr, rms))
+    far = add_near(exchange(add_pair(keep, got), NEAR))
     total, line = add_far(exchange(far, ("z",)))
     line = jnp.sum(exchange(line, NEAR + ("c", "t")), axis=0)
     line = exchange(jnp.broadcast_to(line, (ZH, 128)), ("z",))
@@ -297,7 +352,7 @@
         small_first,
         small_second,
     )
-    weights, *new, clip = adam(line, total, clip_rms.reshape(1, 1), corr, states)
+    weights, *new, clip = adam(line, total, rms, corr, states)
     own = exchange(weights, ("z",))
     own = exchange(jnp.broadcast_to(own[None], (A,) + own.shape), NEAR)
     expert_w, embed_w, small_w = unpack(own, lax.ppermute(own, "c", SWAP))

time: 130 us -> 127 us (0.977)
  blocking collectives: 85.8 us -> 99.6 us
  waiting for transfers between devices: 16 us -> 3.68 us
  starting transfers between devices: 18.6 us -> 15.2 us
    all_to_all x5 -> x6, blocking collectives: 85.8 us -> 99.6 us  [exchange(): return lax.all_to_all(x, axes, 0, 0, tiled=True)]
    all_to_all x1 -> x0, waiting for transfers between devices: 10.5 us -> none  [exchange(): return lax.all_to_all(x, axes, 0, 0, tiled=True)]
    all_to_all x1 -> x0, starting transfers between devices: 3.31 us -> none  [exchange(): return lax.all_to_all(x, axes, 0, 0, tiled=True)]
    ppermute x1, waiting for transfers between devices: 3.35 us -> 1.6 us  [body(): lax.ppermute(send, 'c', SWAP)]
    pallas_call x2 -> x3, Pallas kernels: 3.56 us -> 4 us  [the longest x1 3.05 us: pack(): pl.pallas_call(pack_kernel, in_specs=[pl.BlockSpec(memory_space=pltpu.HBM...]
  transfers between devices with their start and end apart: 3 -> 2, of which waited for: 3 -> 2; matrix products, arithmetic and copies ran while one was open for 0% -> 0% of each run, Pallas kernels for 0% -> 0%
where the time goes in v6:
time: 127 us; the launch traced here: 126 us
  blocking collectives  99.6 us (78%)
  starting transfers between devices  15.2 us (12%)
  Pallas kernels  5.97 us (5%)
  waiting for transfers between devices  3.68 us (3%)
  between operations  1.52 us (1%)
    all_to_all x6, blocking collectives, exchange(): return lax.all_to_all(x, axes, 0, 0, tiled=True)  99.6 us
    ppermute x1, starting transfers between devices, body(): lax.ppermute(send, 'c', SWAP)  8.79 us
    ppermute x1, starting transfers between devices, body(): expert_w, embed_w, small_w = unpack(own, lax.ppermute(own, 'c', SWAP))  6.37 us
    pallas_call x1, Pallas kernels, pack(): pl.pallas_call(pack_kernel, in_specs=[pl.BlockSpec(memory_space=pltpu.HBM...  3.05 us
  transfers between devices with their start and end apart: 2, of which 2 were waited for; matrix products, arithmetic and copies ran while one was open for 0% of the time, Pallas kernels for 0%

profile of v6, /device:TPU:1, one launch (start us, length us, event | category | flops | bytes accessed | tf_op | source)
XLA Modules:
  0.0 126.4 jit_solution(1065716566719180393)
XLA Ops:
  0.6 0.0 copy-start.9
  0.7 3.0 %pack.1 = (f32[8,8,56,128]{3,2,1,0:T(8,128)S(1)}, bf16[8,8,56,128]{3,2,1,0:T(8,128)(2,1)}) custom-call(bf16[2,1,2,512,256]{4,3,2,1,0:T(8,128)(2,1)} %expert_hbm.1, bf16[2,1,4096,128]{3,2,1,0:T(8,128)(2,1)} %embed_hbm.1, bf16[9,2,512]{2,1,0:T(2,128)(2,1)} %bitcast.17), custom_call_target="tpu_custom_call" | custom-call | tf_op jit(solution)/shard_map/pack/pallas_call | solution.py:111
  3.7 8.8 %collective-permute-start = (bf16[8,8,56,128]{3,2,1,0:T(8,128)(2,1)}, bf16[8,8,56,128]{3,2,1,0:T(8,128)(2,1)S(1)}, u32[]{:S(2)}, u32[]{:S(2)}) collective-permute-start(bf16[8,8,56,128]{3,2,1,0:T(8,128)(2,1)} %get-tuple-element.37), channel_id=1, source_target_pairs={{0,4},{4,0},{1,5},{5,1},{2,6},{6,2},{3,7},{7,3},{8,12},{12,8},{9,1... | collective-permute-start | bytes 2752520 | tf_op jit(solution)/shard_map/ppermute | solution.py:339
  13.2 0.0 copy-done.9
  13.2 1.6 %collective-permute-done.got_ref = bf16[8,8,56,128]{3,2,1,0:T(8,128)(2,1)S(1)} collective-permute-done((bf16[8,8,56,128]{3,2,1,0:T(8,128)(2,1)}, bf16[8,8,56,128]{3,2,1,0:T(8,128)(2,1)S(1)}, u32[]{:S(2)}, u32[]{:S(2)}) %collective-permute-start) | collective-permute-done | bytes 917536 | tf_op jit(solution)/shard_map/ppermute | solution.py:339
  14.8 0.1 broadcast_in_dim.21.corr_ref
  14.9 0.3 add_pair.1
  15.1 0.0 copy-start
  15.2 0.0 copy-start.1
  15.2 0.0 copy-start.2
  15.2 0.0 copy-start.3
  15.2 0.0 copy-start.4
  15.2 0.0 copy-start.5
  15.2 0.0 copy-start.6
  15.2 0.0 copy-start.7
  15.2 0.0 copy-start.8
  15.2 16.6 %all_to_all.37 = bf16[8,8,56,128]{3,2,1,0:T(8,128)(2,1)S(1)} all-to-all(bf16[8,8,56,128]{3,2,1,0:T(8,128)(2,1)S(1)} %add_pair.1), channel_id=1, replica_groups=mesh['y'=4,'z'=8,'w'=2,'c'=2,'t'=4] {'y','w'}, dimensions={0} | all-to-all | bytes 1835008 | tf_op jit(solution)/shard_map/all_to_all | solution.py:315
  31.8 0.1 convert_reduce_fusion
  32.0 24.3 %all_to_all.38.got_ref = bf16[8,56,128]{2,1,0:T(8,128)(2,1)S(1)} all-to-all(bf16[8,56,128]{2,1,0:T(8,128)(2,1)S(1)} %pad_maximum_fusion), channel_id=1, replica_groups=mesh['y'=4,'z'=8,'w'=2,'c'=2,'t'=4] {'z'}, dimensions={0} | all-to-all | bytes 229376 | tf_op jit(solution)/shard_map/all_to_all | solution.py:315
  56.3 0.1 add_far.1
  56.5 16.5 %all_to_all.39 = f32[64,1,128]{2,1,0:T(1,128)S(1)} all-to-all(f32[64,1,128]{2,1,0:T(1,128)S(1)} %bitcast.15), channel_id=1, replica_groups=mesh['y'=4,'z'=8,'w'=2,'c'=2,'t'=4] {'y','w','c','t'}, dimensions={0} | all-to-all | bytes 65536 | tf_op jit(solution)/shard_map/all_to_all | solution.py:315
  73.0 0.1 reduce_sum.19
  73.1 13.7 %all_to_all.40 = f32[8,1,128]{2,1,0:T(1,128)S(1)} all-to-all(f32[8,1,128]{2,1,0:T(1,128)S(1)} %broadcast_in_dim.23), channel_id=1, replica_groups=mesh['y'=4,'z'=8,'w'=2,'c'=2,'t'=4] {'z'}, dimensions={0} | all-to-all | bytes 8192 | tf_op jit(solution)/shard_map/all_to_all | solution.py:315
  86.8 0.0 copy-done
  86.8 0.0 copy-done.1
  86.9 0.7 adam.1
  87.6 15.2 %all_to_all.41 = bf16[8,56,128]{2,1,0:T(8,128)(2,1)S(1)} all-to-all(bf16[8,56,128]{2,1,0:T(8,128)(2,1)S(1)} %get-tuple-element.43), channel_id=1, replica_groups=mesh['y'=4,'z'=8,'w'=2,'c'=2,'t'=4] {'z'}, dimensions={0} | all-to-all | bytes 229376 | tf_op jit(solution)/shard_map/all_to_all | solution.py:315
  102.7 0.1 broadcast_in_dim.24
  102.9 13.3 %all_to_all.42.own_ref = bf16[8,8,56,128]{3,2,1,0:T(8,128)(2,1)S(1)} all-to-all(bf16[8,8,56,128]{3,2,1,0:T(8,128)(2,1)S(1)} %broadcast_in_dim.24), channel_id=1, replica_groups=mesh['y'=4,'z'=8,'w'=2,'c'=2,'t'=4] {'y','w'}, dimensions={0} | all-to-all | bytes 1835008 | tf_op jit(solution)/shard_map/all_to_all | solution.py:315
  116.2 6.4 %collective-permute-start.1 = (bf16[8,8,56,128]{3,2,1,0:T(8,128)(2,1)S(1)}, bf16[8,8,56,128]{3,2,1,0:T(8,128)(2,1)S(1)}, u32[]{:S(2)}, u32[]{:S(2)}) collective-permute-start(bf16[8,8,56,128]{3,2,1,0:T(8,128)(2,1)S(1)} %all_to_all.42.own_ref), channel_id=1, source_target_pairs={{0,4},{4,0},{1,5},{5,1},{2,6},{6,2},{3,7},{7,3},{8,12},{12,8},{9,1... | collective-permute-start | bytes 2752520 | tf_op jit(solution)/shard_map/ppermute | solution.py:358
  122.5 2.1 %collective-permute-done.1.other_ref = bf16[8,8,56,128]{3,2,1,0:T(8,128)(2,1)S(1)} collective-permute-done((bf16[8,8,56,128]{3,2,1,0:T(8,128)(2,1)S(1)}, bf16[8,8,56,128]{3,2,1,0:T(8,128)(2,1)S(1)}, u32[]{:S(2)}, u32[]{:S(2)}) %collective-permute-start.1) | collective-permute-done | bytes 917536 | tf_op jit(solution)/shard_map/ppermute | solution.py:358
  124.6 1.8 %unpack.1 = (bf16[2,512,256]{2,1,0:T(8,128)(2,1)}, bf16[4096,128]{1,0:T(8,128)(2,1)}, bf16[9,512]{1,0:T(8,128)(2,1)}) custom-call(bf16[8,8,56,128]{3,2,1,0:T(8,128)(2,1)S(1)} %all_to_all.42.own_ref, bf16[8,8,56,128]{3,2,1,0:T(8,128)(2,1)S(1)} %collective-permute-done.1.other_ref), custom_call_target="tpu_custom_call" | custom-call | tf_op jit(solution)/shard_map/unpack/pallas_call | solution.py:294
  (14 shorter events, 0.1 us)
Async XLA Ops:
  0.6 12.5 %copy-start.9 = (s32[32]{0:T(128)S(1)}, s32[32]{0:T(128)}, u32[]{:S(2)}) copy-start(s32[32]{0:T(128)} %param.26) | copy-start | bytes 388
  3.7 11.1 %collective-permute-start = (bf16[8,8,56,128]{3,2,1,0:T(8,128)(2,1)}, bf16[8,8,56,128]{3,2,1,0:T(8,128)(2,1)S(1)}, u32[]{:S(2)}, u32[]{:S(2)}) collective-permute-start(bf16[8,8,56,128]{3,2,1,0:T(8,128)(2,1)} %get-tuple-element.37), channel_id=1, source_target_pairs={{0,4},{4,0},{1,5},{5,1},{2,6},{6,2},{3,7},{7,3},{8,12},{12,8},{9,1... | collective-permute-start | bytes 2752520 | tf_op jit(solution)/shard_map/ppermute | solution.py:339
  15.1 71.7 %copy-start = (f32[32,128]{1,0:T(8,128)S(1)}, f32[32,128]{1,0:T(8,128)}, u32[]{:S(2)}) copy-start(f32[32,128]{1,0:T(8,128)} %emb_m.1) | copy-start | bytes 49156
  15.2 71.7 %copy-start.1 = (f32[32,128]{1,0:T(8,128)S(1)}, f32[32,128]{1,0:T(8,128)}, u32[]{:S(2)}) copy-start(f32[32,128]{1,0:T(8,128)} %emb_f.1) | copy-start | bytes 49156
  15.2 71.7 %copy-start.2 = (f32[32,128]{1,0:T(8,128)S(1)}, f32[32,128]{1,0:T(8,128)}, u32[]{:S(2)}) copy-start(f32[32,128]{1,0:T(8,128)} %emb_s.1) | copy-start | bytes 49156
  15.2 71.6 %copy-start.3 = (f32[2,4,256]{2,1,0:T(4,128)S(1)}, f32[2,4,256]{2,1,0:T(4,128)}, u32[]{:S(2)}) copy-start(f32[2,4,256]{2,1,0:T(4,128)} %exp_m.1) | copy-start | bytes 24580
  15.2 71.6 %copy-start.4 = (f32[2,4,256]{2,1,0:T(4,128)S(1)}, f32[2,4,256]{2,1,0:T(4,128)}, u32[]{:S(2)}) copy-start(f32[2,4,256]{2,1,0:T(4,128)} %exp_f.1) | copy-start | bytes 24580
  15.2 71.6 %copy-start.5 = (f32[2,4,256]{2,1,0:T(4,128)S(1)}, f32[2,4,256]{2,1,0:T(4,128)}, u32[]{:S(2)}) copy-start(f32[2,4,256]{2,1,0:T(4,128)} %exp_s.1) | copy-start | bytes 24580
  15.2 71.6 %copy-start.6 = (f32[4,9]{1,0:T(4,128)S(1)}, f32[4,9]{1,0:T(4,128)}, u32[]{:S(2)}) copy-start(f32[4,9]{1,0:T(4,128)} %sma_m.1) | copy-start | bytes 436
  15.2 71.6 %copy-start.7 = (f32[4,9]{1,0:T(4,128)S(1)}, f32[4,9]{1,0:T(4,128)}, u32[]{:S(2)}) copy-start(f32[4,9]{1,0:T(4,128)} %sma_f.1) | copy-start | bytes 436
  15.2 71.6 %copy-start.8 = (f32[4,9]{1,0:T(4,128)S(1)}, f32[4,9]{1,0:T(4,128)}, u32[]{:S(2)}) copy-start(f32[4,9]{1,0:T(4,128)} %sma_s.1) | copy-start | bytes 436
  116.2 8.5 %collective-permute-start.1 = (bf16[8,8,56,128]{3,2,1,0:T(8,128)(2,1)S(1)}, bf16[8,8,56,128]{3,2,1,0:T(8,128)(2,1)S(1)}, u32[]{:S(2)}, u32[]{:S(2)}) collective-permute-start(bf16[8,8,56,128]{3,2,1,0:T(8,128)(2,1)S(1)} %all_to_all.42.own_ref), channel_id=1, source_target_pairs={{0,4},{4,0},{1,5},{5,1},{2,6},{6,2},{3,7},{7,3},{8,12},{12,8},{9,1... | collective-permute-start | bytes 2752520 | tf_op jit(solution)/shard_map/ppermute | solution.py:358

commit v7 on v6

--- a/solution.py
+++ b/solution.py
@@ -19,6 +19,7 @@
 NEAR = ("y", "w")
 EMB, EXP, ROWS = 32, 16, 56
 SMA = EMB + EXP
+MAIN, MSG = ZH * SMA, ZH * SMA + 8
 SWAP = ((0, 1), (1, 0))
 F32, BF16 = jnp.float32, jnp.bfloat16
 VMEM = pl.BlockSpec(memory_space=pltpu.VMEM)
@@ -38,6 +39,14 @@
 
 def flip(x):
     return pltpu.roll(x, 4, x.ndim - 2)
+
+
+def shift(x, z, back=False):
+    return pltpu.roll(x, (128 - 9 * z) % 128 if back else 9 * z, x.ndim - 1)
+
+
+def nine(x):
+    return jnp.where(lax.broadcasted_iota(jnp.int32, x.shape, x.ndim - 1) < 9, x, 0.0)
 
 
 def two_terms(x):
@@ -72,22 +81,23 @@
 
 
 def pack_rows(core, y, expert_ref, embed_ref, small_ref, keep_ref, send_ref):
-    def put(index, rows, *values):
-        keep_ref[index + rows] = values[core]
-        send_ref[index + rows] = values[1 - core].astype(BF16)
+    def put(w, row, rows, *values):
+        at = (y * W + w, pl.ds(row, rows))
+        keep_ref[at] = values[core]
+        send_ref[at] = values[1 - core].astype(BF16)
 
     small = small_ref[y, :, 0, :].astype(F32) + small_ref[y, :, 1, :].astype(F32)
     small = jnp.concatenate([small, jnp.zeros((128 - 9, 128), F32)], axis=0).T
-    for z in range(ZH):
-        for w in range(W):
-            index = (y * W + w, z)
+    for w in range(W):
+        shared = jnp.zeros((8, 128), F32)
+        for z in range(ZH):
             base = (z * W + w) * C * EMB
             pair = [
                 embed_ref[y, 0, pl.ds(base + c * EMB, EMB), :].astype(F32)
                 + embed_ref[y, 1, pl.ds(base + c * EMB, EMB), :].astype(F32)
                 for c in range(C)
             ]
-            put(index, (slice(0, EMB),), *pair)
+            put(w, z * SMA, EMB, *pair)
             row = (z * W + w) * 8
             for m in range(2):
                 tile = expert_ref[y, 0, m, pl.ds(row, 8), :].astype(F32) + expert_ref[
@@ -96,18 +106,20 @@
                 left, right = tile[:, :128], tile[:, 128:]
                 upper = low_rows((8, 128))
                 put(
-                    index,
-                    (slice(EMB + 8 * m, EMB + 8 * m + 8),),
+                    w,
+                    z * SMA + EMB + 8 * m,
+                    8,
                     jnp.where(upper, left, flip(right)),
                     jnp.where(upper, flip(left), right),
                 )
-            pair = [small[row : row + 8], flip(small[row : row + 8])]
-            pair[1 - core] = two_terms(pair[1 - core])
-            put(index, (slice(SMA, ROWS),), *pair)
+            shared = shared + shift(small[row : row + 8], z)
+        pair = [shared, flip(shared)]
+        pair[1 - core] = two_terms(pair[1 - core])
+        put(w, MAIN, 8, *pair)
 
 
 def pack(expert_grads, embed_grads, small_grads):
-    shape = (A, ZH, ROWS, 128)
+    shape = (A, MSG, 128)
     return pl.pallas_call(
         pack_kernel,
         in_specs=[pl.BlockSpec(memory_space=pltpu.HBM)] * 3,
@@ -124,38 +136,61 @@
     )(in_hbm(expert_grads), in_hbm(embed_grads), in_hbm(small_grads[:, 0].transpose(2, 0, 1)))
 
 
-def terms(main, small):
-    high = lax.reduce_precision(small, 8, 7)
-    return jnp.concatenate([x.astype(BF16) for x in (main, high, small - high)], axis=-2)
-
-
-def parts(x):
-    x = x.astype(F32)
-    return x[..., :SMA, :], x[..., SMA : SMA + 4, :] + x[..., SMA + 4 :, :]
+def kernel_in_vmem(kernel, name, shapes, *args):
+    return pl.pallas_call(
+        kernel,
+        in_specs=[VMEM] * len(args),
+        out_specs=[VMEM] * len(shapes),
+        out_shape=[pltpu.VMEM(*shape) for shape in shapes],
+        compiler_params=pltpu.CompilerParams(vmem_limit_bytes=16 << 20),
+        name=name,
+    )(*(in_vmem(x) for x in args))
 
 
 def pair_kernel(keep_ref, got_ref, out_ref):
     @pl.loop(0, A)
     def _(a):
-        out_ref[a, :, :SMA] = (keep_ref[a, :, :SMA] + got_ref[a, :, :SMA].astype(F32)).astype(BF16)
-        small = got_ref[a, :, SMA:].astype(F32)
-        small = keep_ref[a, :, SMA:] + (small + flip(small))
-        out_ref[a, :, SMA:] = two_terms(small).astype(BF16)
+        out_ref[a, :MAIN] = (keep_ref[a, :MAIN] + got_ref[a, :MAIN].astype(F32)).astype(BF16)
+        small = got_ref[a, MAIN:].astype(F32)
+        small = keep_ref[a, MAIN:] + (small + flip(small))
+        out_ref[a, MAIN:] = two_terms(small).astype(BF16)
 
 
 def add_pair(keep, got):
-    return pl.pallas_call(
-        pair_kernel,
-        in_specs=[VMEM, VMEM],
-        out_specs=VMEM,
-        out_shape=pltpu.VMEM((A, ZH, ROWS, 128), BF16),
-        compiler_params=pltpu.CompilerParams(vmem_limit_bytes=16 << 20),
-        name="add_pair",
-    )(in_vmem(keep), in_vmem(got))
+    return kernel_in_vmem(pair_kernel, "add_pair", [((A, MSG, 128), BF16)], keep, got)[0]
+
+
+def near_kernel(got_ref, out_ref):
+    def total(rows):
+        out = got_ref[0, rows].astype(F32)
+        for a in range(1, A):
+            out = out + got_ref[a, rows].astype(F32)
+        return out
+
+    shared = total(slice(MAIN, MSG))
+    shared = shared + flip(shared)
+    for z in range(ZH):
+        out_ref[z, :SMA] = total(slice(z * SMA, z * SMA + SMA)).astype(BF16)
+        out_ref[z, SMA:] = two_terms(nine(shift(shared, z, True))).astype(BF16)
 
 
 def add_near(got):
-    return terms(*parts(jnp.sum(got.astype(F32), axis=0)))
+    return kernel_in_vmem(near_kernel, "add_near", [((ZH, ROWS, 128), BF16)], got)[0]
+
+
+def spread_kernel(own_ref, out_ref):
+    shared = jnp.zeros((8, 128), F32)
+    for z in range(ZH):
+        main = own_ref[z, :SMA]
+        for a in range(A):
+            out_ref[a, z * SMA : z * SMA + SMA] = main
+        shared = shared + shift(nine(own_ref[z, SMA:].astype(F32)), z)
+    for a in range(A):
+        out_ref[a, MAIN:] = shared.astype(BF16)
+
+
+def spread(own):
+    return kernel_in_vmem(spread_kernel, "spread", [((A, MSG, 128), BF16)], own)[0]
 
 
 def far_kernel(got_ref, total_ref, line_ref):
@@ -170,14 +205,9 @@
 
 
 def add_far(got):
-    return pl.pallas_call(
-        far_kernel,
-        in_specs=[VMEM],
-        out_specs=[VMEM, VMEM],
-        out_shape=[pltpu.VMEM((ROWS, 128), F32), pltpu.VMEM((A * C * T, 128), F32)],
-        compiler_params=pltpu.CompilerParams(vmem_limit_bytes=16 << 20),
-        name="add_far",
-    )(in_vmem(got))
+    return kernel_in_vmem(
+        far_kernel, "add_far", [((ROWS, 128), F32), ((A * C * T, 128), F32)], got
+    )
 
 
 def update(scaled, first, second, master, corr_one, corr_two):
@@ -272,21 +302,22 @@
 
 def unpack_rows(refs, expert_ref, embed_ref, small_ref):
     y = pl.program_id(0)
-    tiles = []
-    for z in range(ZH):
-        for w in range(W):
-            pair = [ref[y * W + w, z] for ref in refs]
+    upper = low_rows((8, 128))
+    tiles = [None] * (ZH * W)
+    for w in range(W):
+        shared = [ref[y * W + w, MAIN:].astype(F32) for ref in refs]
+        shared = jnp.where(upper, shared[0], flip(shared[1]))
+        for z in range(ZH):
+            pair = [ref[y * W + w, z * SMA : z * SMA + SMA] for ref in refs]
             base = (z * W + w) * C * EMB
             for c in range(C):
                 embed_ref[pl.ds(base + c * EMB, EMB), :] = pair[c][:EMB]
             row = (z * W + w) * 8
-            upper = low_rows((8, 128))
             for m in range(2):
                 zero, one = (p[EMB + 8 * m : EMB + 8 * m + 8].astype(F32) for p in pair)
                 expert_ref[m, pl.ds(row, 8), :128] = jnp.where(upper, zero, flip(one)).astype(BF16)
                 expert_ref[m, pl.ds(row, 8), 128:] = jnp.where(upper, flip(zero), one).astype(BF16)
-            zero, one = (p[SMA:].astype(F32) for p in pair)
-            tiles.append(jnp.where(upper, zero, flip(one)))
+            tiles[z * W + w] = shift(shared, z, True)
     small_ref[...] = jnp.concatenate(tiles, axis=0).T[:9].astype(BF16)
 
 
@@ -354,7 +385,7 @@
     )
     weights, *new, clip = adam(line, total, rms, corr, states)
     own = exchange(weights, ("z",))
-    own = exchange(jnp.broadcast_to(own[None], (A,) + own.shape), NEAR)
+    own = exchange(spread(own), NEAR)
     expert_w, embed_w, small_w = unpack(own, lax.ppermute(own, "c", SWAP))
     return (expert_w, embed_w, small_w, *new, clip[0, 0])
 

time: 127 us -> 123 us (0.969)
  blocking collectives: 99.6 us -> 97.3 us
    all_to_all x6, blocking collectives: 99.6 us -> 97.3 us  [exchange(): return lax.all_to_all(x, axes, 0, 0, tiled=True)]
where the time goes in v7:
time: 123 us
  blocking collectives  97.3 us (79%)
  starting transfers between devices  15 us (12%)
  Pallas kernels  5.53 us (4%)
  waiting for transfers between devices  3.14 us (3%)
  between operations  1.5 us (1%)
    all_to_all x6, blocking collectives, exchange(): return lax.all_to_all(x, axes, 0, 0, tiled=True)  97.3 us
    ppermute x1, starting transfers between devices, body(): lax.ppermute(send, 'c', SWAP)  8.79 us
    ppermute x1, starting transfers between devices, body(): expert_w, embed_w, small_w = unpack(own, lax.ppermute(own, 'c', SWAP))  6.22 us
  transfers between devices with their start and end apart: 2, of which 2 were waited for; matrix products, arithmetic and copies ran while one was open for 0% of the time, Pallas kernels for 0%

profile of v7, /device:TPU:1, one launch (start us, length us, event | category | flops | bytes accessed | tf_op | source)
XLA Modules:
  0.0 122.7 jit_solution(15045699884318307546)
XLA Ops:
  0.6 0.0 copy-start.9
  0.7 2.2 %pack.1 = (f32[8,392,128]{2,1,0:T(8,128)S(1)}, bf16[8,392,128]{2,1,0:T(8,128)(2,1)S(1)}) custom-call(bf16[2,1,2,512,256]{4,3,2,1,0:T(8,128)(2,1)} %expert_hbm.1, bf16[2,1,4096,128]{3,2,1,0:T(8,128)(2,1)} %embed_hbm.1, bf16[9,2,512]{2,1,0:T(2,128)(2,1)} %bitcast.17), custom_call_target="tpu_custom_call" | custom-call | tf_op jit(solution)/shard_map/pack/pallas_call | solution.py:123
  2.9 8.8 %collective-permute-start = (bf16[8,392,128]{2,1,0:T(8,128)(2,1)S(1)}, bf16[8,392,128]{2,1,0:T(8,128)(2,1)S(1)}, u32[]{:S(2)}, u32[]{:S(2)}) collective-permute-start(bf16[8,392,128]{2,1,0:T(8,128)(2,1)S(1)} %get-tuple-element.37), channel_id=1, source_target_pairs={{0,4},{4,0},{1,5},{5,1},{2,6},{6,2},{3,7},{7,3},{8,12},{12,8},{9,1... | collective-permute-start | bytes 2408456 | tf_op jit(solution)/shard_map/ppermute | solution.py:370
  12.3 0.0 copy-done.9
  12.3 1.2 collective-permute-done.got_ref
  13.6 0.1 broadcast_in_dim.15.corr_ref
  13.6 0.3 add_pair.1
  13.9 0.0 copy-start
  13.9 0.0 copy-start.1
  13.9 0.0 copy-start.2
  14.0 0.0 copy-start.3
  14.0 0.0 copy-start.4
  14.0 0.0 copy-start.5
  14.0 0.0 copy-start.6
  14.0 0.0 copy-start.7
  14.0 0.0 copy-start.8
  14.0 15.6 %all_to_all.37.got_ref = bf16[8,392,128]{2,1,0:T(8,128)(2,1)S(1)} all-to-all(bf16[8,392,128]{2,1,0:T(8,128)(2,1)S(1)} %add_pair.1), channel_id=1, replica_groups=mesh['y'=4,'z'=8,'w'=2,'c'=2,'t'=4] {'y','w'}, dimensions={0} | all-to-all | bytes 1605632 | tf_op jit(solution)/shard_map/all_to_all | solution.py:346
  29.6 0.1 add_near.1
  29.7 23.5 %all_to_all.38.got_ref = bf16[8,56,128]{2,1,0:T(8,128)(2,1)S(1)} all-to-all(bf16[8,56,128]{2,1,0:T(8,128)(2,1)S(1)} %add_near.1), channel_id=1, replica_groups=mesh['y'=4,'z'=8,'w'=2,'c'=2,'t'=4] {'z'}, dimensions={0} | all-to-all | bytes 229376 | tf_op jit(solution)/shard_map/all_to_all | solution.py:346
  53.2 0.1 add_far.1
  53.3 17.0 %all_to_all.39 = f32[64,1,128]{2,1,0:T(1,128)S(1)} all-to-all(f32[64,1,128]{2,1,0:T(1,128)S(1)} %bitcast.15), channel_id=1, replica_groups=mesh['y'=4,'z'=8,'w'=2,'c'=2,'t'=4] {'y','w','c','t'}, dimensions={0} | all-to-all | bytes 65536 | tf_op jit(solution)/shard_map/all_to_all | solution.py:346
  70.4 0.1 reduce_sum.9
  70.5 13.7 %all_to_all.40 = f32[8,1,128]{2,1,0:T(1,128)S(1)} all-to-all(f32[8,1,128]{2,1,0:T(1,128)S(1)} %broadcast_in_dim.17), channel_id=1, replica_groups=mesh['y'=4,'z'=8,'w'=2,'c'=2,'t'=4] {'z'}, dimensions={0} | all-to-all | bytes 8192 | tf_op jit(solution)/shard_map/all_to_all | solution.py:346
  84.2 0.0 copy-done
  84.2 0.0 copy-done.1
  84.2 0.7 adam.1
  84.9 15.2 %all_to_all.41.own_ref = bf16[8,56,128]{2,1,0:T(8,128)(2,1)S(1)} all-to-all(bf16[8,56,128]{2,1,0:T(8,128)(2,1)S(1)} %get-tuple-element.43), channel_id=1, replica_groups=mesh['y'=4,'z'=8,'w'=2,'c'=2,'t'=4] {'z'}, dimensions={0} | all-to-all | bytes 229376 | tf_op jit(solution)/shard_map/all_to_all | solution.py:346
  100.1 0.1 spread.1
  100.2 12.4 %all_to_all.42.own_ref = bf16[8,392,128]{2,1,0:T(8,128)(2,1)S(1)} all-to-all(bf16[8,392,128]{2,1,0:T(8,128)(2,1)S(1)} %spread.1), channel_id=1, replica_groups=mesh['y'=4,'z'=8,'w'=2,'c'=2,'t'=4] {'y','w'}, dimensions={0} | all-to-all | bytes 1605632 | tf_op jit(solution)/shard_map/all_to_all | solution.py:346
  112.6 6.2 %collective-permute-start.1 = (bf16[8,392,128]{2,1,0:T(8,128)(2,1)S(1)}, bf16[8,392,128]{2,1,0:T(8,128)(2,1)S(1)}, u32[]{:S(2)}, u32[]{:S(2)}) collective-permute-start(bf16[8,392,128]{2,1,0:T(8,128)(2,1)S(1)} %all_to_all.42.own_ref), channel_id=1, source_target_pairs={{0,4},{4,0},{1,5},{5,1},{2,6},{6,2},{3,7},{7,3},{8,12},{12,8},{9,1... | collective-permute-start | bytes 2408456 | tf_op jit(solution)/shard_map/ppermute | solution.py:389
  118.8 1.9 %collective-permute-done.1.other_ref = bf16[8,392,128]{2,1,0:T(8,128)(2,1)S(1)} collective-permute-done((bf16[8,392,128]{2,1,0:T(8,128)(2,1)S(1)}, bf16[8,392,128]{2,1,0:T(8,128)(2,1)S(1)}, u32[]{:S(2)}, u32[]{:S(2)}) %collective-permute-start.1) | collective-permute-done | bytes 802848 | tf_op jit(solution)/shard_map/ppermute | solution.py:389
  120.7 2.0 %unpack.1 = (bf16[2,512,256]{2,1,0:T(8,128)(2,1)}, bf16[4096,128]{1,0:T(8,128)(2,1)}, bf16[9,512]{1,0:T(8,128)(2,1)}) custom-call(bf16[8,392,128]{2,1,0:T(8,128)(2,1)S(1)} %all_to_all.42.own_ref, bf16[8,392,128]{2,1,0:T(8,128)(2,1)S(1)} %collective-permute-done.1.other_ref), custom_call_target="tpu_custom_call" | custom-call | tf_op jit(solution)/shard_map/unpack/pallas_call | solution.py:325
  (11 shorter events, 0.0 us)
Async XLA Ops:
  0.6 11.7 %copy-start.9 = (s32[32]{0:T(128)S(1)}, s32[32]{0:T(128)}, u32[]{:S(2)}) copy-start(s32[32]{0:T(128)} %param.26) | copy-start | bytes 388
  2.9 10.7 %collective-permute-start = (bf16[8,392,128]{2,1,0:T(8,128)(2,1)S(1)}, bf16[8,392,128]{2,1,0:T(8,128)(2,1)S(1)}, u32[]{:S(2)}, u32[]{:S(2)}) collective-permute-start(bf16[8,392,128]{2,1,0:T(8,128)(2,1)S(1)} %get-tuple-element.37), channel_id=1, source_target_pairs={{0,4},{4,0},{1,5},{5,1},{2,6},{6,2},{3,7},{7,3},{8,12},{12,8},{9,1... | collective-permute-start | bytes 2408456 | tf_op jit(solution)/shard_map/ppermute | solution.py:370
  13.9 70.3 %copy-start = (f32[32,128]{1,0:T(8,128)S(1)}, f32[32,128]{1,0:T(8,128)}, u32[]{:S(2)}) copy-start(f32[32,128]{1,0:T(8,128)} %emb_m.1) | copy-start | bytes 49156
  13.9 70.3 %copy-start.1 = (f32[32,128]{1,0:T(8,128)S(1)}, f32[32,128]{1,0:T(8,128)}, u32[]{:S(2)}) copy-start(f32[32,128]{1,0:T(8,128)} %emb_f.1) | copy-start | bytes 49156
  13.9 70.2 %copy-start.2 = (f32[32,128]{1,0:T(8,128)S(1)}, f32[32,128]{1,0:T(8,128)}, u32[]{:S(2)}) copy-start(f32[32,128]{1,0:T(8,128)} %emb_s.1) | copy-start | bytes 49156
  14.0 70.2 %copy-start.3 = (f32[2,4,256]{2,1,0:T(4,128)S(1)}, f32[2,4,256]{2,1,0:T(4,128)}, u32[]{:S(2)}) copy-start(f32[2,4,256]{2,1,0:T(4,128)} %exp_m.1) | copy-start | bytes 24580
  14.0 70.2 %copy-start.4 = (f32[2,4,256]{2,1,0:T(4,128)S(1)}, f32[2,4,256]{2,1,0:T(4,128)}, u32[]{:S(2)}) copy-start(f32[2,4,256]{2,1,0:T(4,128)} %exp_f.1) | copy-start | bytes 24580
  14.0 70.2 %copy-start.5 = (f32[2,4,256]{2,1,0:T(4,128)S(1)}, f32[2,4,256]{2,1,0:T(4,128)}, u32[]{:S(2)}) copy-start(f32[2,4,256]{2,1,0:T(4,128)} %exp_s.1) | copy-start | bytes 24580
  14.0 70.2 %copy-start.6 = (f32[4,9]{1,0:T(4,128)S(1)}, f32[4,9]{1,0:T(4,128)}, u32[]{:S(2)}) copy-start(f32[4,9]{1,0:T(4,128)} %sma_m.1) | copy-start | bytes 436
  14.0 70.2 %copy-start.7 = (f32[4,9]{1,0:T(4,128)S(1)}, f32[4,9]{1,0:T(4,128)}, u32[]{:S(2)}) copy-start(f32[4,9]{1,0:T(4,128)} %sma_f.1) | copy-start | bytes 436
  14.0 70.2 %copy-start.8 = (f32[4,9]{1,0:T(4,128)S(1)}, f32[4,9]{1,0:T(4,128)}, u32[]{:S(2)}) copy-start(f32[4,9]{1,0:T(4,128)} %sma_s.1) | copy-start | bytes 436
  112.6 8.1 %collective-permute-start.1 = (bf16[8,392,128]{2,1,0:T(8,128)(2,1)S(1)}, bf16[8,392,128]{2,1,0:T(8,128)(2,1)S(1)}, u32[]{:S(2)}, u32[]{:S(2)}) collective-permute-start(bf16[8,392,128]{2,1,0:T(8,128)(2,1)S(1)} %all_to_all.42.own_ref), channel_id=1, source_target_pairs={{0,4},{4,0},{1,5},{5,1},{2,6},{6,2},{3,7},{7,3},{8,12},{12,8},{9,1... | collective-permute-start | bytes 2408456 | tf_op jit(solution)/shard_map/ppermute | solution.py:389

commit v8 on v7

--- a/solution.py
+++ b/solution.py
@@ -170,8 +170,8 @@
     shared = total(slice(MAIN, MSG))
     shared = shared + flip(shared)
     for z in range(ZH):
-        out_ref[z, :SMA] = total(slice(z * SMA, z * SMA + SMA)).astype(BF16)
-        out_ref[z, SMA:] = two_terms(nine(shift(shared, z, True))).astype(BF16)
+        out_ref[PLACE[z], :SMA] = total(slice(z * SMA, z * SMA + SMA)).astype(BF16)
+        out_ref[PLACE[z], SMA:] = two_terms(nine(shift(shared, z, True))).astype(BF16)
 
 
 def add_near(got):
@@ -181,10 +181,10 @@
 def spread_kernel(own_ref, out_ref):
     shared = jnp.zeros((8, 128), F32)
     for z in range(ZH):
-        main = own_ref[z, :SMA]
+        main = own_ref[PLACE[z], :SMA]
         for a in range(A):
             out_ref[a, z * SMA : z * SMA + SMA] = main
-        shared = shared + shift(nine(own_ref[z, SMA:].astype(F32)), z)
+        shared = shared + shift(nine(own_ref[PLACE[z], SMA:].astype(F32)), z)
     for a in range(A):
         out_ref[a, MAIN:] = shared.astype(BF16)
 
@@ -346,6 +346,14 @@
     return lax.all_to_all(x, axes, 0, 0, tiled=True)
 
 
+ORDER = (4, 5, 6, 7, 0, 1, 2, 3)
+PLACE = tuple(ORDER.index(z) for z in range(ZH))
+
+
+def exchange_far(x):
+    return lax.all_to_all(x, "z", 0, 0, tiled=True, axis_index_groups=[ORDER])
+
+
 def body(
     expert_grads,
     embed_grads,
@@ -369,9 +377,9 @@
     rms = jnp.broadcast_to(clip_rms, (1, 128))
     got, corr, rms = lax.optimization_barrier((lax.ppermute(send, "c", SWAP), corr, rms))
     far = add_near(exchange(add_pair(keep, got), NEAR))
-    total, line = add_far(exchange(far, ("z",)))
+    total, line = add_far(exchange_far(far))
     line = jnp.sum(exchange(line, NEAR + ("c", "t")), axis=0)
-    line = exchange(jnp.broadcast_to(line, (ZH, 128)), ("z",))
+    line = exchange_far(jnp.broadcast_to(line, (ZH, 128)))
     states = (
         expert_master,
         expert_first,
@@ -384,7 +392,7 @@
         small_second,
     )
     weights, *new, clip = adam(line, total, rms, corr, states)
-    own = exchange(weights, ("z",))
+    own = exchange_far(weights)
     own = exchange(spread(own), NEAR)
     expert_w, embed_w, small_w = unpack(own, lax.ppermute(own, "c", SWAP))
     return (expert_w, embed_w, small_w, *new, clip[0, 0])

time: 123 us -> 117 us (0.951)
  blocking collectives: 97.3 us -> 90.5 us
    all_to_all x6 -> x3, blocking collectives: 97.3 us -> 44.2 us  [exchange(): return lax.all_to_all(x, axes, 0, 0, tiled=True)]
    all_to_all x0 -> x3, blocking collectives: none -> 46.3 us  [exchange_far(): return lax.all_to_all(x, 'z', 0, 0, tiled=True, axis_index_groups=[ORDER])]
where the time goes in v8:
time: 117 us
  blocking collectives  90.5 us (77%)
  starting transfers between devices  15.6 us (13%)
  Pallas kernels  5.53 us (5%)
  waiting for transfers between devices  3.14 us (3%)
  between operations  1.5 us (1%)
    all_to_all x3, blocking collectives, exchange_far(): return lax.all_to_all(x, 'z', 0, 0, tiled=True, axis_index_groups=[ORDER])  46.3 us
    all_to_all x3, blocking collectives, exchange(): return lax.all_to_all(x, axes, 0, 0, tiled=True)  44.2 us
    ppermute x1, starting transfers between devices, body(): lax.ppermute(send, 'c', SWAP)  8.79 us
    ppermute x1, starting transfers between devices, body(): expert_w, embed_w, small_w = unpack(own, lax.ppermute(own, 'c', SWAP))  6.81 us
  transfers between devices with their start and end apart: 2, of which 2 were waited for; matrix products, arithmetic and copies ran while one was open for 0% of the time, Pallas kernels for 0%

profile of v8, /device:TPU:1, one launch (start us, length us, event | category | flops | bytes accessed | tf_op | source)
XLA Modules:
  0.0 116.5 jit_solution(6566495648812427951)
XLA Ops:
  0.6 0.0 copy-start.9
  0.7 2.2 %pack.1 = (f32[8,392,128]{2,1,0:T(8,128)S(1)}, bf16[8,392,128]{2,1,0:T(8,128)(2,1)S(1)}) custom-call(bf16[2,1,2,512,256]{4,3,2,1,0:T(8,128)(2,1)} %expert_hbm.1, bf16[2,1,4096,128]{3,2,1,0:T(8,128)(2,1)} %embed_hbm.1, bf16[9,2,512]{2,1,0:T(2,128)(2,1)} %bitcast.17), custom_call_target="tpu_custom_call" | custom-call | tf_op jit(solution)/shard_map/pack/pallas_call | solution.py:123
  2.9 8.8 %collective-permute-start = (bf16[8,392,128]{2,1,0:T(8,128)(2,1)S(1)}, bf16[8,392,128]{2,1,0:T(8,128)(2,1)S(1)}, u32[]{:S(2)}, u32[]{:S(2)}) collective-permute-start(bf16[8,392,128]{2,1,0:T(8,128)(2,1)S(1)} %get-tuple-element.37), channel_id=1, source_target_pairs={{0,4},{4,0},{1,5},{5,1},{2,6},{6,2},{3,7},{7,3},{8,12},{12,8},{9,1... | collective-permute-start | bytes 2408456 | tf_op jit(solution)/shard_map/ppermute | solution.py:378
  12.3 0.0 copy-done.9
  12.3 1.2 %collective-permute-done.got_ref = bf16[8,392,128]{2,1,0:T(8,128)(2,1)S(1)} collective-permute-done((bf16[8,392,128]{2,1,0:T(8,128)(2,1)S(1)}, bf16[8,392,128]{2,1,0:T(8,128)(2,1)S(1)}, u32[]{:S(2)}, u32[]{:S(2)}) %collective-permute-start) | collective-permute-done | bytes 802848 | tf_op jit(solution)/shard_map/ppermute | solution.py:378
  13.6 0.1 broadcast_in_dim.15.corr_ref
  13.6 0.3 add_pair.1
  13.9 0.0 copy-start
  13.9 0.0 copy-start.1
  13.9 0.0 copy-start.2
  14.0 0.0 copy-start.3
  14.0 0.0 copy-start.4
  14.0 0.0 copy-start.5
  14.0 0.0 copy-start.6
  14.0 0.0 copy-start.7
  14.0 0.0 copy-start.8
  14.0 15.6 %all_to_all.37.got_ref = bf16[8,392,128]{2,1,0:T(8,128)(2,1)S(1)} all-to-all(bf16[8,392,128]{2,1,0:T(8,128)(2,1)S(1)} %add_pair.1), channel_id=1, replica_groups=mesh['y'=4,'z'=8,'w'=2,'c'=2,'t'=4] {'y','w'}, dimensions={0} | all-to-all | bytes 1605632 | tf_op jit(solution)/shard_map/all_to_all | solution.py:346
  29.6 0.1 add_near.1
  29.7 17.5 %all_to_all.38.got_ref = bf16[8,56,128]{2,1,0:T(8,128)(2,1)S(1)} all-to-all(bf16[8,56,128]{2,1,0:T(8,128)(2,1)S(1)} %add_near.1), channel_id=1, replica_groups={{64,80,96,112,0,16,32,48},{65,81,97,113,1,17,33,49},{66,82,98,114,2,18,..., dimensions={0} | all-to-all | bytes 229376 | tf_op jit(solution)/shard_map/all_to_all | solution.py:354
  47.3 0.1 add_far.1
  47.4 16.9 %all_to_all.39 = f32[64,1,128]{2,1,0:T(1,128)S(1)} all-to-all(f32[64,1,128]{2,1,0:T(1,128)S(1)} %bitcast.15), channel_id=1, replica_groups=mesh['y'=4,'z'=8,'w'=2,'c'=2,'t'=4] {'y','w','c','t'}, dimensions={0} | all-to-all | bytes 65536 | tf_op jit(solution)/shard_map/all_to_all | solution.py:346
  64.3 0.1 reduce_sum.9
  64.4 12.9 %all_to_all.40 = f32[8,1,128]{2,1,0:T(1,128)S(1)} all-to-all(f32[8,1,128]{2,1,0:T(1,128)S(1)} %broadcast_in_dim.17), channel_id=1, replica_groups={{64,80,96,112,0,16,32,48},{65,81,97,113,1,17,33,49},{66,82,98,114,2,18,..., dimensions={0} | all-to-all | bytes 8192 | tf_op jit(solution)/shard_map/all_to_all | solution.py:354
  77.3 0.0 copy-done
  77.3 0.0 copy-done.1
  77.3 0.7 adam.1
  78.0 15.9 %all_to_all.41.own_ref = bf16[8,56,128]{2,1,0:T(8,128)(2,1)S(1)} all-to-all(bf16[8,56,128]{2,1,0:T(8,128)(2,1)S(1)} %get-tuple-element.43), channel_id=1, replica_groups={{64,80,96,112,0,16,32,48},{65,81,97,113,1,17,33,49},{66,82,98,114,2,18,..., dimensions={0} | all-to-all | bytes 229376 | tf_op jit(solution)/shard_map/all_to_all | solution.py:354
  93.9 0.1 spread.1
  94.0 11.8 %all_to_all.42.own_ref = bf16[8,392,128]{2,1,0:T(8,128)(2,1)S(1)} all-to-all(bf16[8,392,128]{2,1,0:T(8,128)(2,1)S(1)} %spread.1), channel_id=1, replica_groups=mesh['y'=4,'z'=8,'w'=2,'c'=2,'t'=4] {'y','w'}, dimensions={0} | all-to-all | bytes 1605632 | tf_op jit(solution)/shard_map/all_to_all | solution.py:346
  105.8 6.8 %collective-permute-start.1 = (bf16[8,392,128]{2,1,0:T(8,128)(2,1)S(1)}, bf16[8,392,128]{2,1,0:T(8,128)(2,1)S(1)}, u32[]{:S(2)}, u32[]{:S(2)}) collective-permute-start(bf16[8,392,128]{2,1,0:T(8,128)(2,1)S(1)} %all_to_all.42.own_ref), channel_id=1, source_target_pairs={{0,4},{4,0},{1,5},{5,1},{2,6},{6,2},{3,7},{7,3},{8,12},{12,8},{9,1... | collective-permute-start | bytes 2408456 | tf_op jit(solution)/shard_map/ppermute | solution.py:397
  112.6 1.9 %collective-permute-done.1.other_ref = bf16[8,392,128]{2,1,0:T(8,128)(2,1)S(1)} collective-permute-done((bf16[8,392,128]{2,1,0:T(8,128)(2,1)S(1)}, bf16[8,392,128]{2,1,0:T(8,128)(2,1)S(1)}, u32[]{:S(2)}, u32[]{:S(2)}) %collective-permute-start.1) | collective-permute-done | bytes 802848 | tf_op jit(solution)/shard_map/ppermute | solution.py:397
  114.5 2.0 %unpack.1 = (bf16[2,512,256]{2,1,0:T(8,128)(2,1)}, bf16[4096,128]{1,0:T(8,128)(2,1)}, bf16[9,512]{1,0:T(8,128)(2,1)}) custom-call(bf16[8,392,128]{2,1,0:T(8,128)(2,1)S(1)} %all_to_all.42.own_ref, bf16[8,392,128]{2,1,0:T(8,128)(2,1)S(1)} %collective-permute-done.1.other_ref), custom_call_target="tpu_custom_call" | custom-call | tf_op jit(solution)/shard_map/unpack/pallas_call | solution.py:325
  (11 shorter events, 0.0 us)
Async XLA Ops:
  0.6 11.7 %copy-start.9 = (s32[32]{0:T(128)S(1)}, s32[32]{0:T(128)}, u32[]{:S(2)}) copy-start(s32[32]{0:T(128)} %param.26) | copy-start | bytes 388
  2.9 10.7 %collective-permute-start = (bf16[8,392,128]{2,1,0:T(8,128)(2,1)S(1)}, bf16[8,392,128]{2,1,0:T(8,128)(2,1)S(1)}, u32[]{:S(2)}, u32[]{:S(2)}) collective-permute-start(bf16[8,392,128]{2,1,0:T(8,128)(2,1)S(1)} %get-tuple-element.37), channel_id=1, source_target_pairs={{0,4},{4,0},{1,5},{5,1},{2,6},{6,2},{3,7},{7,3},{8,12},{12,8},{9,1... | collective-permute-start | bytes 2408456 | tf_op jit(solution)/shard_map/ppermute | solution.py:378
  13.9 63.4 %copy-start = (f32[32,128]{1,0:T(8,128)S(1)}, f32[32,128]{1,0:T(8,128)}, u32[]{:S(2)}) copy-start(f32[32,128]{1,0:T(8,128)} %emb_m.1) | copy-start | bytes 49156
  13.9 63.4 %copy-start.1 = (f32[32,128]{1,0:T(8,128)S(1)}, f32[32,128]{1,0:T(8,128)}, u32[]{:S(2)}) copy-start(f32[32,128]{1,0:T(8,128)} %emb_f.1) | copy-start | bytes 49156
  13.9 63.3 %copy-start.2 = (f32[32,128]{1,0:T(8,128)S(1)}, f32[32,128]{1,0:T(8,128)}, u32[]{:S(2)}) copy-start(f32[32,128]{1,0:T(8,128)} %emb_s.1) | copy-start | bytes 49156
  14.0 63.3 %copy-start.3 = (f32[2,4,256]{2,1,0:T(4,128)S(1)}, f32[2,4,256]{2,1,0:T(4,128)}, u32[]{:S(2)}) copy-start(f32[2,4,256]{2,1,0:T(4,128)} %exp_m.1) | copy-start | bytes 24580
  14.0 63.3 %copy-start.4 = (f32[2,4,256]{2,1,0:T(4,128)S(1)}, f32[2,4,256]{2,1,0:T(4,128)}, u32[]{:S(2)}) copy-start(f32[2,4,256]{2,1,0:T(4,128)} %exp_f.1) | copy-start | bytes 24580
  14.0 63.3 %copy-start.5 = (f32[2,4,256]{2,1,0:T(4,128)S(1)}, f32[2,4,256]{2,1,0:T(4,128)}, u32[]{:S(2)}) copy-start(f32[2,4,256]{2,1,0:T(4,128)} %exp_s.1) | copy-start | bytes 24580
  14.0 63.3 %copy-start.6 = (f32[4,9]{1,0:T(4,128)S(1)}, f32[4,9]{1,0:T(4,128)}, u32[]{:S(2)}) copy-start(f32[4,9]{1,0:T(4,128)} %sma_m.1) | copy-start | bytes 436
  14.0 63.3 %copy-start.7 = (f32[4,9]{1,0:T(4,128)S(1)}, f32[4,9]{1,0:T(4,128)}, u32[]{:S(2)}) copy-start(f32[4,9]{1,0:T(4,128)} %sma_f.1) | copy-start | bytes 436
  14.0 63.3 %copy-start.8 = (f32[4,9]{1,0:T(4,128)S(1)}, f32[4,9]{1,0:T(4,128)}, u32[]{:S(2)}) copy-start(f32[4,9]{1,0:T(4,128)} %sma_s.1) | copy-start | bytes 436
  105.8 8.7 %collective-permute-start.1 = (bf16[8,392,128]{2,1,0:T(8,128)(2,1)S(1)}, bf16[8,392,128]{2,1,0:T(8,128)(2,1)S(1)}, u32[]{:S(2)}, u32[]{:S(2)}) collective-permute-start(bf16[8,392,128]{2,1,0:T(8,128)(2,1)S(1)} %all_to_all.42.own_ref), channel_id=1, source_target_pairs={{0,4},{4,0},{1,5},{5,1},{2,6},{6,2},{3,7},{7,3},{8,12},{12,8},{9,1... | collective-permute-start | bytes 2408456 | tf_op jit(solution)/shard_map/ppermute | solution.py:397

commit v9 on v8

--- a/solution.py
+++ b/solution.py
@@ -150,10 +150,11 @@
 def pair_kernel(keep_ref, got_ref, out_ref):
     @pl.loop(0, A)
     def _(a):
-        out_ref[a, :MAIN] = (keep_ref[a, :MAIN] + got_ref[a, :MAIN].astype(F32)).astype(BF16)
+        place = lax.rem(a + A // 2, A)
+        out_ref[place, :MAIN] = (keep_ref[a, :MAIN] + got_ref[a, :MAIN].astype(F32)).astype(BF16)
         small = got_ref[a, MAIN:].astype(F32)
         small = keep_ref[a, MAIN:] + (small + flip(small))
-        out_ref[a, MAIN:] = two_terms(small).astype(BF16)
+        out_ref[place, MAIN:] = two_terms(small).astype(BF16)
 
 
 def add_pair(keep, got):
@@ -301,7 +302,7 @@
 
 
 def unpack_rows(refs, expert_ref, embed_ref, small_ref):
-    y = pl.program_id(0)
+    y = lax.rem(pl.program_id(0) + Y // 2, Y)
     upper = low_rows((8, 128))
     tiles = [None] * (ZH * W)
     for w in range(W):
@@ -343,7 +344,9 @@
 
 
 def exchange(x, axes):
-    return lax.all_to_all(x, axes, 0, 0, tiled=True)
+    half = x.shape[0] // 2
+    order = [*range(half, 2 * half), *range(half)]
+    return lax.all_to_all(x, axes, 0, 0, tiled=True, axis_index_groups=[order])
 
 
 ORDER = (4, 5, 6, 7, 0, 1, 2, 3)

time: 117 us -> 116 us (level)
  no operation moved by 1% of the time
where the time goes in v9:
time: 116 us; the launch traced here: 115 us
  blocking collectives  90.1 us (78%)
  starting transfers between devices  14.9 us (13%)
  Pallas kernels  5.53 us (5%)
  waiting for transfers between devices  3.14 us (3%)
  between operations  1.5 us (1%)
    all_to_all x3, blocking collectives, exchange_far(): return lax.all_to_all(x, 'z', 0, 0, tiled=True, axis_index_groups=[ORDER])  46.2 us
    all_to_all x3, blocking collectives, exchange(): return lax.all_to_all(x, axes, 0, 0, tiled=True, axis_index_groups=[order])  43.9 us
    ppermute x1, starting transfers between devices, body(): lax.ppermute(send, 'c', SWAP)  8.79 us
    ppermute x1, starting transfers between devices, body(): expert_w, embed_w, small_w = unpack(own, lax.ppermute(own, 'c', SWAP))  6.07 us
  transfers between devices with their start and end apart: 2, of which 2 were waited for; matrix products, arithmetic and copies ran while one was open for 0% of the time, Pallas kernels for 0%

profile of v9, /device:TPU:1, one launch (start us, length us, event | category | flops | bytes accessed | tf_op | source)
XLA Modules:
  0.0 115.3 jit_solution(3433433913253882278)
XLA Ops:
  0.6 0.0 copy-start.9
  0.7 2.2 %pack.1 = (f32[8,392,128]{2,1,0:T(8,128)S(1)}, bf16[8,392,128]{2,1,0:T(8,128)(2,1)S(1)}) custom-call(bf16[2,1,2,512,256]{4,3,2,1,0:T(8,128)(2,1)} %expert_hbm.1, bf16[2,1,4096,128]{3,2,1,0:T(8,128)(2,1)} %embed_hbm.1, bf16[9,2,512]{2,1,0:T(2,128)(2,1)} %bitcast.17), custom_call_target="tpu_custom_call" | custom-call | tf_op jit(solution)/shard_map/pack/pallas_call | solution.py:123
  2.9 8.8 %collective-permute-start = (bf16[8,392,128]{2,1,0:T(8,128)(2,1)S(1)}, bf16[8,392,128]{2,1,0:T(8,128)(2,1)S(1)}, u32[]{:S(2)}, u32[]{:S(2)}) collective-permute-start(bf16[8,392,128]{2,1,0:T(8,128)(2,1)S(1)} %get-tuple-element.37), channel_id=1, source_target_pairs={{0,4},{4,0},{1,5},{5,1},{2,6},{6,2},{3,7},{7,3},{8,12},{12,8},{9,1... | collective-permute-start | bytes 2408456 | tf_op jit(solution)/shard_map/ppermute | solution.py:381
  12.3 0.0 copy-done.9
  12.3 1.2 %collective-permute-done.got_ref = bf16[8,392,128]{2,1,0:T(8,128)(2,1)S(1)} collective-permute-done((bf16[8,392,128]{2,1,0:T(8,128)(2,1)S(1)}, bf16[8,392,128]{2,1,0:T(8,128)(2,1)S(1)}, u32[]{:S(2)}, u32[]{:S(2)}) %collective-permute-start) | collective-permute-done | bytes 802848 | tf_op jit(solution)/shard_map/ppermute | solution.py:381
  13.6 0.1 broadcast_in_dim.15.corr_ref
  13.6 0.3 add_pair.1
  13.9 0.0 copy-start
  13.9 0.0 copy-start.1
  13.9 0.0 copy-start.2
  13.9 0.0 copy-start.3
  14.0 0.0 copy-start.4
  14.0 0.0 copy-start.5
  14.0 0.0 copy-start.6
  14.0 0.0 copy-start.7
  14.0 0.0 copy-start.8
  14.0 14.3 %all_to_all.37.got_ref = bf16[8,392,128]{2,1,0:T(8,128)(2,1)S(1)} all-to-all(bf16[8,392,128]{2,1,0:T(8,128)(2,1)S(1)} %add_pair.1), channel_id=1, replica_groups={{256,264,384,392,0,8,128,136},{257,265,385,393,1,9,129,137},{258,266,38..., dimensions={0} | all-to-all | bytes 1605632 | tf_op jit(solution)/shard_map/all_to_all | solution.py:349
  28.3 0.1 add_near.1
  28.4 17.4 %all_to_all.38.got_ref = bf16[8,56,128]{2,1,0:T(8,128)(2,1)S(1)} all-to-all(bf16[8,56,128]{2,1,0:T(8,128)(2,1)S(1)} %add_near.1), channel_id=1, replica_groups={{64,80,96,112,0,16,32,48},{65,81,97,113,1,17,33,49},{66,82,98,114,2,18,..., dimensions={0} | all-to-all | bytes 229376 | tf_op jit(solution)/shard_map/all_to_all | solution.py:357
  45.8 0.1 add_far.1
  45.9 17.0 %all_to_all.39 = f32[64,1,128]{2,1,0:T(1,128)S(1)} all-to-all(f32[64,1,128]{2,1,0:T(1,128)S(1)} %bitcast.15), channel_id=1, replica_groups={{256,257,258,259,260,261,262,263,264,265,266,267,268,269,270,271,384,38..., dimensions={0} | all-to-all | bytes 65536 | tf_op jit(solution)/shard_map/all_to_all | solution.py:349
  62.9 0.1 reduce_sum.9
  63.0 12.7 %all_to_all.40 = f32[8,1,128]{2,1,0:T(1,128)S(1)} all-to-all(f32[8,1,128]{2,1,0:T(1,128)S(1)} %broadcast_in_dim.17), channel_id=1, replica_groups={{64,80,96,112,0,16,32,48},{65,81,97,113,1,17,33,49},{66,82,98,114,2,18,..., dimensions={0} | all-to-all | bytes 8192 | tf_op jit(solution)/shard_map/all_to_all | solution.py:357
  75.7 0.0 copy-done
  75.7 0.0 copy-done.1
  75.8 0.7 adam.1
  76.5 16.1 %all_to_all.41.own_ref = bf16[8,56,128]{2,1,0:T(8,128)(2,1)S(1)} all-to-all(bf16[8,56,128]{2,1,0:T(8,128)(2,1)S(1)} %get-tuple-element.43), channel_id=1, replica_groups={{64,80,96,112,0,16,32,48},{65,81,97,113,1,17,33,49},{66,82,98,114,2,18,..., dimensions={0} | all-to-all | bytes 229376 | tf_op jit(solution)/shard_map/all_to_all | solution.py:357
  92.6 0.1 spread.1
  92.7 12.6 %all_to_all.42.own_ref = bf16[8,392,128]{2,1,0:T(8,128)(2,1)S(1)} all-to-all(bf16[8,392,128]{2,1,0:T(8,128)(2,1)S(1)} %spread.1), channel_id=1, replica_groups={{256,264,384,392,0,8,128,136},{257,265,385,393,1,9,129,137},{258,266,38..., dimensions={0} | all-to-all | bytes 1605632 | tf_op jit(solution)/shard_map/all_to_all | solution.py:349
  105.3 6.1 %collective-permute-start.1 = (bf16[8,392,128]{2,1,0:T(8,128)(2,1)S(1)}, bf16[8,392,128]{2,1,0:T(8,128)(2,1)S(1)}, u32[]{:S(2)}, u32[]{:S(2)}) collective-permute-start(bf16[8,392,128]{2,1,0:T(8,128)(2,1)S(1)} %all_to_all.42.own_ref), channel_id=1, source_target_pairs={{0,4},{4,0},{1,5},{5,1},{2,6},{6,2},{3,7},{7,3},{8,12},{12,8},{9,1... | collective-permute-start | bytes 2408456 | tf_op jit(solution)/shard_map/ppermute | solution.py:400
  111.4 1.9 %collective-permute-done.1.other_ref = bf16[8,392,128]{2,1,0:T(8,128)(2,1)S(1)} collective-permute-done((bf16[8,392,128]{2,1,0:T(8,128)(2,1)S(1)}, bf16[8,392,128]{2,1,0:T(8,128)(2,1)S(1)}, u32[]{:S(2)}, u32[]{:S(2)}) %collective-permute-start.1) | collective-permute-done | bytes 802848 | tf_op jit(solution)/shard_map/ppermute | solution.py:400
  113.3 2.0 %unpack.1 = (bf16[2,512,256]{2,1,0:T(8,128)(2,1)}, bf16[4096,128]{1,0:T(8,128)(2,1)}, bf16[9,512]{1,0:T(8,128)(2,1)}) custom-call(bf16[8,392,128]{2,1,0:T(8,128)(2,1)S(1)} %all_to_all.42.own_ref, bf16[8,392,128]{2,1,0:T(8,128)(2,1)S(1)} %collective-permute-done.1.other_ref), custom_call_target="tpu_custom_call" | custom-call | tf_op jit(solution)/shard_map/unpack/pallas_call | solution.py:326
  (11 shorter events, 0.0 us)
Async XLA Ops:
  0.6 11.7 %copy-start.9 = (s32[32]{0:T(128)S(1)}, s32[32]{0:T(128)}, u32[]{:S(2)}) copy-start(s32[32]{0:T(128)} %param.26) | copy-start | bytes 388
  2.9 10.7 %collective-permute-start = (bf16[8,392,128]{2,1,0:T(8,128)(2,1)S(1)}, bf16[8,392,128]{2,1,0:T(8,128)(2,1)S(1)}, u32[]{:S(2)}, u32[]{:S(2)}) collective-permute-start(bf16[8,392,128]{2,1,0:T(8,128)(2,1)S(1)} %get-tuple-element.37), channel_id=1, source_target_pairs={{0,4},{4,0},{1,5},{5,1},{2,6},{6,2},{3,7},{7,3},{8,12},{12,8},{9,1... | collective-permute-start | bytes 2408456 | tf_op jit(solution)/shard_map/ppermute | solution.py:381
  13.9 61.8 %copy-start = (f32[32,128]{1,0:T(8,128)S(1)}, f32[32,128]{1,0:T(8,128)}, u32[]{:S(2)}) copy-start(f32[32,128]{1,0:T(8,128)} %emb_m.1) | copy-start | bytes 49156
  13.9 61.8 %copy-start.1 = (f32[32,128]{1,0:T(8,128)S(1)}, f32[32,128]{1,0:T(8,128)}, u32[]{:S(2)}) copy-start(f32[32,128]{1,0:T(8,128)} %emb_f.1) | copy-start | bytes 49156
  13.9 61.8 %copy-start.2 = (f32[32,128]{1,0:T(8,128)S(1)}, f32[32,128]{1,0:T(8,128)}, u32[]{:S(2)}) copy-start(f32[32,128]{1,0:T(8,128)} %emb_s.1) | copy-start | bytes 49156
  13.9 61.8 %copy-start.3 = (f32[2,4,256]{2,1,0:T(4,128)S(1)}, f32[2,4,256]{2,1,0:T(4,128)}, u32[]{:S(2)}) copy-start(f32[2,4,256]{2,1,0:T(4,128)} %exp_m.1) | copy-start | bytes 24580
  14.0 61.8 %copy-start.4 = (f32[2,4,256]{2,1,0:T(4,128)S(1)}, f32[2,4,256]{2,1,0:T(4,128)}, u32[]{:S(2)}) copy-start(f32[2,4,256]{2,1,0:T(4,128)} %exp_f.1) | copy-start | bytes 24580
  14.0 61.8 %copy-start.5 = (f32[2,4,256]{2,1,0:T(4,128)S(1)}, f32[2,4,256]{2,1,0:T(4,128)}, u32[]{:S(2)}) copy-start(f32[2,4,256]{2,1,0:T(4,128)} %exp_s.1) | copy-start | bytes 24580
  14.0 61.7 %copy-start.6 = (f32[4,9]{1,0:T(4,128)S(1)}, f32[4,9]{1,0:T(4,128)}, u32[]{:S(2)}) copy-start(f32[4,9]{1,0:T(4,128)} %sma_m.1) | copy-start | bytes 436
  14.0 61.7 %copy-start.7 = (f32[4,9]{1,0:T(4,128)S(1)}, f32[4,9]{1,0:T(4,128)}, u32[]{:S(2)}) copy-start(f32[4,9]{1,0:T(4,128)} %sma_f.1) | copy-start | bytes 436
  14.0 61.7 %copy-start.8 = (f32[4,9]{1,0:T(4,128)S(1)}, f32[4,9]{1,0:T(4,128)}, u32[]{:S(2)}) copy-start(f32[4,9]{1,0:T(4,128)} %sma_s.1) | copy-start | bytes 436
  105.3 8.0 %collective-permute-start.1 = (bf16[8,392,128]{2,1,0:T(8,128)(2,1)S(1)}, bf16[8,392,128]{2,1,0:T(8,128)(2,1)S(1)}, u32[]{:S(2)}, u32[]{:S(2)}) collective-permute-start(bf16[8,392,128]{2,1,0:T(8,128)(2,1)S(1)} %all_to_all.42.own_ref), channel_id=1, source_target_pairs={{0,4},{4,0},{1,5},{5,1},{2,6},{6,2},{3,7},{7,3},{8,12},{12,8},{9,1... | collective-permute-start | bytes 2408456 | tf_op jit(solution)/shard_map/ppermute | solution.py:400
